TPU v7x, 32 devices: a whole 2x2x4 slice. The times are simulated.
32 devices in a mesh: fourier: 4 (over y, core), meridian: 8 (over z, x).
Axes of the slice: x: 2, y: 2, z: 4, core: 2. Of those that a mesh axis runs over, the one named last changes fastest.
Arguments:
- forward_now: float32 [3, 1056, 2048], P(None, 'meridian', 'fourier'), may hold values from -3 to 3
- forward_last: float32 [3, 1056, 2048], P(None, 'meridian', 'fourier'), may hold values from -3 to 3
- adjoint_now: float32 [3, 1056, 2048], P(None, 'meridian', 'fourier'), may hold values from -3 to 3
- adjoint_last: float32 [3, 1056, 2048], P(None, 'meridian', 'fourier'), may hold values from -3 to 3
- moduli: float32 [21, 17, 8, 400], P(None, None, 'meridian', 'fourier'), may hold values from -1.8 to 1.8
- inv_radius: float32 [3200], P('meridian'), may hold values from 0.0009765625 to 0.0078125
- inv_mass: float32 [2112], P('meridian'), may hold values from 0.005 to 0.05
Outputs:
- forward_next: float32 [3, 1056, 2048], P(None, 'meridian', 'fourier')
- adjoint_next: float32 [3, 1056, 2048], P(None, 'meridian', 'fourier')
- kernel: float32 [21, 17, 8, 400], P(None, None, 'meridian', 'fourier')
All inputs are finite; a program needn't handle non-finite values.
Results may differ from a plain program's by a relative error of at most 0.0001.
Values sent between devices are 32-bit elements; how exact they have to be, the bound alone decides.
A program may use at most 128 MiB of HBM per device.

v0:
```python
import functools
import math

import jax
import jax.numpy as jnp
import numpy as np
from jax import lax
from jax.experimental import pallas as pl
from jax.experimental.pallas import tpu as pltpu
from jax.sharding import PartitionSpec as P

ORD = 8
EB = 8
LANES = 128
kernel_weight = 0.0001
high = lax.Precision.HIGH
bf16 = jnp.bfloat16
f32 = jnp.float32
PAIRS = [(a, b) for a in range(6) for b in range(a, 6)]
PART_A, PART_B, PART_P = (0, 5, 4), (5, 1, 3), (4, 3, 2)


def gll_tables():
    x = np.array([-1.0, -math.sqrt(3.0 / 7.0), 0.0, math.sqrt(3.0 / 7.0), 1.0])
    weights = np.array([0.1, 49.0 / 90.0, 32.0 / 45.0, 49.0 / 90.0, 0.1])
    factor = np.array([np.prod([x[i] - x[k] for k in range(5) if k != i]) for i in range(5)])
    derive = np.zeros((5, 5))
    for i in range(5):
        for k in range(5):
            if i != k:
                derive[i, k] = factor[i] / (factor[k] * (x[i] - x[k]))
            else:
                derive[i, k] = sum(1.0 / (x[i] - x[o]) for o in range(5) if o != i)
    return derive, np.outer(weights, weights).reshape(25)


def split_host(values):
    wide = np.asarray(values, np.float32)
    hi = wide.astype(bf16)
    return hi, (wide - hi.astype(np.float32)).astype(bf16)


def split_device(values):
    hi = lax.reduce_precision(values, 8, 7)
    return hi.astype(bf16), (values - hi).astype(bf16)


def split_kernel(values):
    hi = values.astype(bf16)
    return hi, (values - hi.astype(f32)).astype(bf16)


def cosine_turn(phase, count):
    folded = (phase + count // 2) % count - count // 2
    x = (count // 4 - jnp.abs(folded)).astype(f32) * (2.0 * math.pi / count)
    y = x * x
    tail = 1.0 / 362880 - y * (1.0 / 39916800)
    return x * (1.0 + y * (-1.0 / 6 + y * (1.0 / 120 + y * (-1.0 / 5040 + y * tail))))


def sample_tables(count):
    n = lax.broadcasted_iota(jnp.int32, (count, count), 0)
    k = lax.broadcasted_iota(jnp.int32, (count, count), 1)
    pair = k // 2
    order = jnp.where(k == 1, count // 2, pair)
    odd = k % 2
    base = cosine_turn(n * order - jnp.where(k == 1, 0, odd * (count // 4)), count)
    turned = pair.astype(f32) * cosine_turn(n * pair + (1 - odd) * (count // 4), count)
    return base, turned


def basis_rows(count):
    n = lax.broadcasted_iota(jnp.int32, (count, 2 * ORD + 1), 0)
    j = lax.broadcasted_iota(jnp.int32, (count, 2 * ORD + 1), 1)
    sine = jnp.where((j % 2 == 0) & (j > 0), count // 4, 0)
    return cosine_turn(n * ((j + 1) // 2) - sine, count)


def nt(a, b):
    return lax.dot_general(a, b, (((1,), (1,)), ((), ())), preferred_element_type=f32)


def nn(a, b):
    return lax.dot_general(a, b, (((1,), (0,)), ((), ())), preferred_element_type=f32)


def dot3(left, right, op):
    return op(left[0], right[0]) + op(left[0], right[1]) + op(left[1], right[0])


def core(nf, pts, nodes, u_ref, bh_ref, bl_ref, zh_ref, zl_ref, am_ref, m_ref, gh_ref, gl_ref,
         rh_ref, rl_ref, gth_ref, gtl_ref, rth_ref, rtl_ref, out_ref, acc_ref,
         uh, ul, us, zs, cs, es, ss, ps, xs, ys):
    step = pl.program_id(0)
    local = u_ref.shape[2]

    @pl.when(step == 0)
    def _():
        for f in range(nf):
            hi, lo = split_kernel(u_ref[f])
            uh[:, f * local:(f + 1) * local] = hi
            ul[:, f * local:(f + 1) * local] = lo
        out_ref[...] = jnp.zeros_like(out_ref)
        acc_ref[...] = jnp.zeros_like(acc_ref)

    us[...] = nt(uh[...], bh_ref[...])
    us[...] += nt(uh[...], bl_ref[...])
    us[...] += nt(ul[...], bh_ref[...])
    zs[...] = nt(uh[...], zh_ref[...])
    zs[...] += nt(uh[...], zl_ref[...])
    zs[...] += nt(ul[...], zh_ref[...])
    cs[...] = nt(m_ref[...], am_ref[...])
    grads = (gh_ref[...], gl_ref[...])
    spins = (rh_ref[...], rl_ref[...])
    for l in range(2):
        ga, gb, gp = [], [], []
        for c in range(3):
            at = pl.ds((3 * l + c) * pts, pts)
            both = dot3(grads, split_kernel(us[at, :]), nn)
            ga.append(both[:nodes])
            gb.append(both[nodes:])
            gp.append(dot3(spins, split_kernel(zs[at, :]), nn))
        es[6 * l + 0] = ga[0]
        es[6 * l + 1] = gb[1]
        es[6 * l + 2] = gp[2]
        es[6 * l + 3] = gb[2] + gp[1]
        es[6 * l + 4] = ga[2] + gp[0]
        es[6 * l + 5] = ga[1] + gb[0]

    def tile(t, carry):
        row = pl.multiple_of(t * 8, 8)
        at = pl.ds(row, 8)
        fw = [es[v, at, :] for v in range(6)]
        ad = [es[6 + v, at, :] for v in range(6)]
        sf, sa = [None] * 6, [None] * 6

        def add(sums, v, term):
            sums[v] = term if sums[v] is None else sums[v] + term

        for r, (v, w) in enumerate(PAIRS):
            c = cs[pl.ds(pl.multiple_of(r * nodes + row, 8), 8), :]
            add(sf, v, c * fw[w])
            add(sa, v, c * ad[w])
            if v != w:
                add(sf, w, c * fw[v])
                add(sa, w, c * ad[v])
                prod = fw[v] * ad[w] + fw[w] * ad[v]
            else:
                prod = fw[v] * ad[v]
            ps[pl.ds(pl.multiple_of(r * nodes + row, 8), 8), :] = prod
        for v in range(6):
            ss[v, at, :] = sf[v]
            ss[6 + v, at, :] = sa[v]
        return carry

    lax.fori_loop(0, nodes // 8, tile, 0)
    ph, plo = split_kernel(ps[...])
    acc_ref[...] += nn(ph, am_ref[...]) + nn(plo, am_ref[...])
    gt = (gth_ref[...], gtl_ref[...])
    rt = (rth_ref[...], rtl_ref[...])
    for l in range(2):
        for c in range(3):
            at = pl.ds((3 * l + c) * pts, pts)
            ta, tb, tp = (6 * l + part[c] for part in (PART_A, PART_B, PART_P))
            pair = jnp.concatenate([ss[ta], ss[tb]], axis=0)
            xs[at, :] = dot3(gt, split_kernel(pair), nn)
            ys[at, :] = dot3(rt, split_kernel(ss[tp]), nn)
    xh, xl = split_kernel(xs[...])
    yh, yl = split_kernel(ys[...])
    for f in range(nf):
        cols = slice(f * local, (f + 1) * local)
        bh, zh = bh_ref[:, cols], zh_ref[:, cols]
        out_ref[f] += (nn(xh, bh) + nn(xl, bh) + nn(xh, bl_ref[:, cols])
                       + nn(yh, zh) + nn(yl, zh) + nn(yh, zl_ref[:, cols]))


def body(forward_now, forward_last, adjoint_now, adjoint_last, moduli, inv_radius, inv_mass):
    derive, weights = gll_tables()
    wide = 4 * EB + 1
    nf = lax.axis_size("fourier")
    nm = lax.axis_size("meridian")
    comps, rows, lanes = forward_now.shape
    local = lanes // 2
    total = local * nf
    row_count = 2 * rows // wide
    count_a = row_count // 4
    nodes_mine = moduli.shape[3]
    elements = nodes_mine // 25
    tile_b = min(elements, EB)
    tile_a = elements // tile_b
    points = (4 * tile_a + 1) * (4 * tile_b + 1)
    pts = -(-points // 16) * 16 if points % 16 > 8 or points % 16 == 0 else points // 16 * 16 + 8
    nodes = -(-nodes_mine // 8) * 8
    edge = (wide + 1) // 2

    pick = np.zeros((2, nf * pts, rows + edge), np.float32)
    for d in range(nf):
        ea, eb = d * elements // EB, d * elements % EB
        for i in range(4 * tile_a + 1):
            for j in range(4 * tile_b + 1):
                p = (4 * ea + i) * wide + 4 * eb + j
                pick[p % 2, d * pts + i * (4 * tile_b + 1) + j, p // 2] = 1.0
    pick = [jnp.asarray(part.astype(bf16)).astype(f32) for part in pick]
    grads = np.zeros((2, nodes, pts))
    node_at = np.zeros((nodes, pts))
    for ea in range(tile_a):
        for eb in range(tile_b):
            for i in range(5):
                for j in range(5):
                    q = ((ea * tile_b + eb) * 5 + i) * 5 + j
                    at = lambda a, b: (4 * ea + a) * (4 * tile_b + 1) + 4 * eb + b
                    node_at[q, at(i, j)] = 1.0
                    for k in range(5):
                        grads[0, q, at(k, j)] += derive[i, k]
                        grads[1, q, at(i, k)] += derive[j, k]
    grads = grads.reshape(2 * nodes, pts)
    gh, gl = (jnp.asarray(part) for part in split_host(grads))
    gth, gtl = (jnp.asarray(part) for part in split_host(grads.T))
    start = lax.axis_index("fourier") * nodes_mine
    radius = lax.dynamic_slice_in_dim(inv_radius, start, nodes_mine)
    radius = jnp.pad(radius, (0, nodes - nodes_mine))
    spin = jnp.asarray(node_at, f32) * radius[:, None]
    spin_t = jnp.asarray(node_at.T, f32) * radius[None, :]
    rh, rl = split_device(spin)
    rth, rtl = split_device(spin_t)

    lane = lax.broadcasted_iota(jnp.int32, (lanes, lanes), 0)
    spot = lax.broadcasted_iota(jnp.int32, (lanes, lanes), 1)
    order = ((lane % 2) * local + lane // 2 == spot).astype(f32)

    packed = jnp.concatenate([forward_now, adjoint_now], axis=0)
    below = [(i + 1, i) for i in range(nm - 1)]
    above = [(i, i + 1) for i in range(nm - 1)]
    upper = lax.ppermute(packed[:, :edge], "meridian", below)
    packed = jnp.concatenate([packed, upper], axis=1)
    apart = jnp.einsum("crx,xy->cry", packed, order, precision=high)
    tiles = (jnp.einsum("sr,crk->sck", pick[0], apart[:, :, :local], precision=high)
             + jnp.einsum("sr,crk->sck", pick[1], apart[:, :, local:], precision=high))
    tiles = jnp.transpose(tiles.reshape(nf, pts, 2 * comps, local), (0, 2, 1, 3))
    tiles = tiles.reshape(nf, 2 * comps * pts, local)
    mine = lax.all_to_all(tiles, "fourier", split_axis=0, concat_axis=0, tiled=True)

    base, turned = sample_tables(total)
    bh, bl = split_device(base)
    zh, zl = split_device(turned)
    ah, al = split_device(basis_rows(total))
    basis = 2 * ORD + 1
    am = jnp.pad(jnp.concatenate([ah, al, ah], axis=1), ((0, 0), (0, LANES - 3 * basis)))
    wq = jnp.asarray(np.tile(weights, elements), f32)
    scaled = jnp.transpose(moduli[:, :, 0, :] * (wq / total), (0, 2, 1))
    mh, ml = split_device(jnp.pad(scaled, ((0, 0), (0, nodes - nodes_mine), (0, 0))))
    m3 = jnp.concatenate([mh, mh, ml], axis=2)
    m3 = jnp.pad(m3, ((0, 0), (0, 0), (0, LANES - 3 * basis))).reshape(21 * nodes, LANES)

    chunk = min(256, total)
    width = 2 * comps * pts
    whole = lambda shape: pl.BlockSpec(shape, lambda i: (0,) * len(shape))
    table = pl.BlockSpec((chunk, total), lambda i: (i, 0))
    pushed, acc = pl.pallas_call(
        functools.partial(core, nf, pts, nodes),
        grid=(total // chunk,),
        out_shape=(jax.ShapeDtypeStruct((nf, width, local), f32),
                   jax.ShapeDtypeStruct((21 * nodes, LANES), f32)),
        in_specs=[whole((nf, width, local)), table, table, table, table,
                  pl.BlockSpec((chunk, LANES), lambda i: (i, 0)), whole((21 * nodes, LANES)),
                  whole(gh.shape), whole(gh.shape), whole(rh.shape), whole(rh.shape),
                  whole(gth.shape), whole(gth.shape), whole(rth.shape), whole(rth.shape)],
        out_specs=(whole((nf, width, local)), whole((21 * nodes, LANES))),
        scratch_shapes=[pltpu.VMEM((width, total), bf16), pltpu.VMEM((width, total), bf16),
                        pltpu.VMEM((width, chunk), f32), pltpu.VMEM((width, chunk), f32),
                        pltpu.VMEM((21 * nodes, chunk), f32),
                        pltpu.VMEM((12, nodes, chunk), f32), pltpu.VMEM((12, nodes, chunk), f32),
                        pltpu.VMEM((21 * nodes, chunk), f32),
                        pltpu.VMEM((width, chunk), f32), pltpu.VMEM((width, chunk), f32)],
        compiler_params=pltpu.CompilerParams(dimension_semantics=("arbitrary",),
                                             vmem_limit_bytes=56 * 1024 * 1024),
        cost_estimate=pl.CostEstimate(flops=24 * width * total * total, transcendentals=0,
                                      bytes_accessed=8 * total * total + 8 * width * total),
    )(mine, bh, bl, zh, zl, am, m3, gh, gl, rh, rl, gth, gtl, rth, rtl)

    back = lax.all_to_all(pushed, "fourier", split_axis=0, concat_axis=0, tiled=True)
    back = back.reshape(nf, 2 * comps, pts, local)
    sums = [jnp.einsum("dpr,dcpk->crk", part.reshape(nf, pts, rows + edge), back, precision=high)
            for part in pick]
    force = (jnp.einsum("crk,xk->crx", sums[0], order[:, :local], precision=high)
             + jnp.einsum("crk,xk->crx", sums[1], order[:, local:], precision=high))
    carried = lax.ppermute(force[:, rows:], "meridian", above)
    force = force[:, :rows] + jnp.pad(carried, ((0, 0), (0, rows - edge), (0, 0)))
    mass = inv_mass.reshape(rows, 2)
    is_even = lax.broadcasted_iota(jnp.int32, (rows, lanes), 1) % 2 == 0
    mass = jnp.where(is_even, mass[:, :1], mass[:, 1:])
    forward_next = 2.0 * forward_now - forward_last - mass * force[:comps]
    adjoint_next = 2.0 * adjoint_now - adjoint_last - mass * force[comps:]
    acc = acc.reshape(21, nodes, LANES)[:, :nodes_mine]
    terms = (acc[:, :, :basis] + acc[:, :, basis:2 * basis]) * (wq * kernel_weight)[:, None]
    return (forward_next, adjoint_next, jnp.transpose(terms, (0, 2, 1))[:, :, None, :])


def solution(mesh):
    field = P(None, "meridian", "fourier")
    grid = P(None, None, "meridian", "fourier")
    in_specs = (field, field, field, field, grid, P("meridian"), P("meridian"))
    return jax.shard_map(body, mesh=mesh, in_specs=in_specs, out_specs=(field, field, grid),
                         check_vma=False)
```

profile of v0, /device:TPU:0, one launch (start us, length us, event | category | flops | bytes accessed | tf_op | source)
XLA Modules:
  0.0 128.7 jit_solution(3293986218356755489)
XLA Ops:
  0.7 1.3 %constant_dynamic-update-slice_fusion.1 = f32[6,132,512]{2,1,0:T(8,128)S(1)} fusion(f32[3,132,512]{2,1,0:T(8,128)} %param.16), kind=kLoop, calls=%fused_computation.115 | loop fusion | bytes 1646592
  2.1 1.3 %collective-permute-start = (f32[6,17,512]{2,1,0:T(8,128)S(1)}, f32[6,17,512]{2,1,0:T(8,128)}, u32[]{:S(2)}, u32[]{:S(2)}) collective-permute-start(f32[6,17,512]{2,1,0:T(8,128)S(1)} %slice.57), channel_id=1, source_target_pairs={{1,0},{2,1},{3,2},{4,3},{5,4},{6,5},{7,6},{9,8},{10,9},{11,10},{12... | collective-permute-start | bytes 626696 | tf_op jit(solution)/shard_map/ppermute | solution.py:234
  4.6 0.8 pad.20.am_ref
  5.4 0.9 pad.22.clone
  6.3 0.8 dynamic_slice.3
  7.1 0.7 fusion.53
  7.8 0.6 fusion.54
  8.4 5.7 %collective-permute-done = f32[6,17,512]{2,1,0:T(8,128)} collective-permute-done((f32[6,17,512]{2,1,0:T(8,128)S(1)}, f32[6,17,512]{2,1,0:T(8,128)}, u32[]{:S(2)}, u32[]{:S(2)}) %collective-permute-start) | collective-permute-done | bytes 208928 | tf_op jit(solution)/shard_map/ppermute | solution.py:234
  14.1 2.4 %fusion.28 = f32[6,149,512]{2,1,0:T(8,128)S(1)} fusion(f32[6,17,512]{2,1,0:T(8,128)} %collective-permute-done, f32[6,132,512]{2,1,0:T(8,128)S(1)} %constant_dynamic-update-slice_fusion, s32[512]{0:T(512)S(1)} %get-tuple-element.31, s32[512]{0:T(512)S(1)} %get-tuple-element.34, s32[512]{0:T(512)S(1)} %get-tuple-element.32, s32[512]{0:T(512)S(1)} %get-tuple-element.33, ...), kind=kOutput, calls=%fused_computation.50 | convolution fusion | flops 1407908864 | bytes 3671040 | tf_op jit(solution)/shard_map/crx,xy->cry/dot_general | solution.py:236
  16.6 0.8 fusion.34
  17.5 0.8 convolution_add_fusion
  18.3 1.6 %copy.29 = f32[4,88,6,256]{3,1,2,0:T(8,128)} copy(f32[4,88,6,256]{3,1,0,2:T(8,128)S(1)} %bitcast.54) | data formatting | bytes 4325376 | tf_op jit(solution)/shard_map/reshape | solution.py:239
  19.9 3.8 %all-to-all-start = ((f32[4,528,256]{2,1,0:T(8,128)}), f32[4,528,256]{2,1,0:T(8,128)S(1)}, u32[]{:S(2)}, u32[]{:S(2)}) async-start(f32[4,528,256]{2,1,0:T(8,128)} %bitcast.6), calls=%async_computation | async-start | bytes 4325376 | tf_op jit(solution)/shard_map/all_to_all | solution.py:241
  23.7 11.8 %fusion.6 = (bf16[1024,1024]{1,0:T(8,128)(2,1)}, bf16[1024,1024]{1,0:T(8,128)(2,1)}, bf16[1024,1024]{1,0:T(8,128)(2,1)}, bf16[1024,1024]{1,0:T(8,128)(2,1)}) fusion(s32[1024]{0:T(1024)S(1)} %get-tuple-element.38, s32[1024]{0:T(1024)S(1)} %get-tuple-element.41, pred[1024]{0:T(1024)(128)(4,1)S(1)} %get-tuple-element.40, s32[1024]{0:T(1024)S(1)} %get-tuple-element.37, ...), kind=kLoop, calls=%fused_computation.21 | loop fusion | flops 82837504 | bytes 8408064 | tf_op jit(solution)/shard_map/convert_element_type | solution.py:45
  35.5 14.4 %all-to-all-done.u_ref = f32[4,528,256]{2,1,0:T(8,128)S(1)} async-done(((f32[4,528,256]{2,1,0:T(8,128)}), f32[4,528,256]{2,1,0:T(8,128)S(1)}, u32[]{:S(2)}, u32[]{:S(2)}) %all-to-all-start) | async-done | bytes 2162720 | tf_op jit(solution)/shard_map/all_to_all | solution.py:241
  49.8 1.4 %copy-done.4 = f32[4,528,256]{2,1,0:T(8,128)} copy-done((f32[4,528,256]{2,1,0:T(8,128)}, f32[4,528,256]{2,1,0:T(8,128)S(1)}, u32[]{:S(2)}) %copy-start.4) | copy-done | bytes 2162712
  51.2 31.8 %shard_map.175 = (f32[4,528,256]{2,1,0:T(8,128)}, f32[2184,128]{1,0:T(8,128)}) custom-call(f32[4,528,256]{2,1,0:T(8,128)} %copy-done.4, bf16[1024,1024]{1,0:T(8,128)(2,1)} %get-tuple-element.26.bh_ref, bf16[1024,1024]{1,0:T(8,128)(2,1)} %get-tuple-element.25.bl_ref, bf16[1024,1024]{1,0:T(8,128)(2,1)} %get-tuple-element.28.zh_ref, ...), custom_call_target="tpu_custom_call" | custom-call | flops 13287555072 | bytes 12713984 | tf_op jit(solution)/shard_map/pallas_call | solution.py:259
  83.0 4.0 %all-to-all-start.1 = ((f32[4,528,256]{2,1,0:T(8,128)}), f32[4,528,256]{2,1,0:T(8,128)S(1)}, u32[]{:S(2)}, u32[]{:S(2)}) async-start(f32[4,528,256]{2,1,0:T(8,128)} %get-tuple-element.5), calls=%async_computation.1 | async-start | bytes 4325376 | tf_op jit(solution)/shard_map/all_to_all | solution.py:281
  87.4 1.5 %iota_compare_fusion = pred[512,512]{1,0:T(32,128)(4,1)S(1)} fusion(s32[512]{0:T(512)S(1)} %get-tuple-element.31, s32[512]{0:T(512)} %copy-done.15, s32[512]{0:T(512)S(1)} %get-tuple-element.32, s32[512]{0:T(512)S(1)} %get-tuple-element.33, pred[512]{0:T(512)(128)(4,1)} %copy-done.18, pred[512]{0:T(512)(128)(4,1)} %copy-done.16), kind=kLoop, calls=%fused_computation.59 | loop fusion | flops 1310720 | bytes 271360 | tf_op jit(solution)/shard_map/eq | solution.py:229
  88.9 1.4 %fusion.39 = f32[132,512]{1,0:T(8,128)} fusion(f32[132]{0:T(256)S(1)} %get-tuple-element.14, f32[132]{0:T(256)S(1)} %get-tuple-element.13, s32[512]{0:T(512)S(1)} %get-tuple-element.32, s32[512]{0:T(512)S(1)} %get-tuple-element.33, pred[512]{0:T(512)(128)(4,1)} %copy-done.16), kind=kLoop, calls=%fused_computation.75 | loop fusion | flops 202752 | bytes 276000 | tf_op jit(solution)/shard_map/jit(_where)/select_n | solution.py:291
  90.3 1.7 %fusion.69 = (f32[21,100,17]{2,1,0:T(8,128)}, f32[21,100,17]{2,1,0:T(8,128)}) fusion(f32[21,104,128]{2,1,0:T(8,128)S(1)} %bitcast.55), kind=kLoop, calls=%fused_computation.145 | loop fusion | bytes 571200 | tf_op jit(solution)/shard_map/slice | solution.py:295
  92.1 1.7 %copy.38 = f32[21,100,17]{1,0,2:T(8,128)S(1)} copy(f32[21,100,17]{2,1,0:T(8,128)} %get-tuple-element.18) | data formatting | bytes 285600
  93.8 1.7 %copy.39 = f32[21,100,17]{1,0,2:T(8,128)S(1)} copy(f32[21,100,17]{2,1,0:T(8,128)} %get-tuple-element.17) | data formatting | bytes 285600
  95.5 17.6 %all-to-all-done.1 = f32[4,528,256]{2,1,0:T(8,128)S(1)} async-done(((f32[4,528,256]{2,1,0:T(8,128)}), f32[4,528,256]{2,1,0:T(8,128)S(1)}, u32[]{:S(2)}, u32[]{:S(2)}) %all-to-all-start.1) | async-done | bytes 2162720 | tf_op jit(solution)/shard_map/all_to_all | solution.py:281
  113.1 0.7 convolution_bitcast_fusion.1
  113.9 0.7 convolution_bitcast_fusion
  114.7 0.7 fusion.38
  115.4 0.7 convolution_add_fusion.1
  116.2 4.6 %collective-permute-start.1 = (f32[6,17,512]{2,1,0:T(8,128)S(1)}, f32[6,17,512]{2,1,0:T(8,128)S(1)}, u32[]{:S(2)}, u32[]{:S(2)}) collective-permute-start(f32[6,17,512]{2,1,0:T(8,128)S(1)} %slice.63), channel_id=1, source_target_pairs={{0,1},{1,2},{2,3},{3,4},{4,5},{5,6},{6,7},{8,9},{9,10},{10,11},{11... | collective-permute-start | bytes 626696 | tf_op jit(solution)/shard_map/ppermute | solution.py:287
  120.9 0.9 copy.35
  121.7 5.0 %collective-permute-done.1 = f32[6,17,512]{2,1,0:T(8,128)S(1)} collective-permute-done((f32[6,17,512]{2,1,0:T(8,128)S(1)}, f32[6,17,512]{2,1,0:T(8,128)S(1)}, u32[]{:S(2)}, u32[]{:S(2)}) %collective-permute-start.1) | collective-permute-done | bytes 208928 | tf_op jit(solution)/shard_map/ppermute | solution.py:287
  126.9 1.8 %fusion.36 = (f32[3,132,512]{2,1,0:T(8,128)}, f32[3,132,512]{2,1,0:T(8,128)}) fusion(f32[6,132,512]{2,1,0:T(8,128)S(1)} %slice_add_fusion, f32[3,132,512]{2,1,0:T(8,128)S(1)} %copy-done.6, f32[3,132,512]{2,1,0:T(8,128)S(1)} %copy-done.3, f32[132,512]{1,0:T(8,128)S(1)} %copy-done.5, f32[3,132,512]{2,1,0:T(8,128)S(1)} %copy-done.7, f32[3,132,512]{2,1,0:T(8,128)S(1)} %copy-done.1), kind=kLoop, calls=%fused_computation.65 | loop fusion | flops 1622016 | bytes 6758400 | tf_op jit(solution)/shard_map/sub | solution.py:293
  (67 shorter events, 1.9 us)
Async XLA Ops:
  0.6 3.5 %copy-start.19 = (f32[100]{0:T(128)S(1)}, f32[100]{0:T(128)}, u32[]{:S(2)}) copy-start(f32[100]{0:T(128)} %constant.199) | copy-start | bytes 1204
  0.6 1.4 %copy-start.2 = (f32[3,132,512]{2,1,0:T(8,128)S(1)}, f32[3,132,512]{2,1,0:T(8,128)}, u32[]{:S(2)}) copy-start(f32[3,132,512]{2,1,0:T(8,128)} %param.18) | copy-start | bytes 2433028
  0.7 3.5 %copy-start.8 = (f32[21,17,1,100]{3,2,1,0:T(1,128)S(1)}, f32[21,17,1,100]{3,2,1,0:T(1,128)}, u32[]{:S(2)}) copy-start(f32[21,17,1,100]{3,2,1,0:T(1,128)} %param.20) | copy-start | bytes 428404
  2.1 12.0 %collective-permute-start = (f32[6,17,512]{2,1,0:T(8,128)S(1)}, f32[6,17,512]{2,1,0:T(8,128)}, u32[]{:S(2)}, u32[]{:S(2)}) collective-permute-start(f32[6,17,512]{2,1,0:T(8,128)S(1)} %slice.57), channel_id=1, source_target_pairs={{1,0},{2,1},{3,2},{4,3},{5,4},{6,5},{7,6},{9,8},{10,9},{11,10},{12... | collective-permute-start | bytes 626696 | tf_op jit(solution)/shard_map/ppermute | solution.py:234
  3.5 10.7 %copy-start.15 = (s32[512]{0:T(512)}, s32[512]{0:T(512)S(1)}, u32[]{:S(2)}) copy-start(s32[512]{0:T(512)S(1)} %get-tuple-element.34) | copy-start | bytes 6148
  3.5 10.6 %copy-start.16 = (pred[512]{0:T(512)(128)(4,1)}, pred[512]{0:T(512)(128)(4,1)S(1)}, u32[]{:S(2)}) copy-start(pred[512]{0:T(512)(128)(4,1)S(1)} %get-tuple-element.35) | copy-start | bytes 1540
  3.5 10.6 %copy-start.18 = (pred[512]{0:T(512)(128)(4,1)}, pred[512]{0:T(512)(128)(4,1)S(1)}, u32[]{:S(2)}) copy-start(pred[512]{0:T(512)(128)(4,1)S(1)} %get-tuple-element.36) | copy-start | bytes 1540
  3.9 3.2 %copy-start.13 = (f32[104,88]{1,0:T(8,128)S(1)}, f32[104,88]{1,0:T(8,128)}, u32[]{:S(2)}) copy-start(f32[104,88]{1,0:T(8,128)} %constant.181.clone) | copy-start | bytes 109828
  3.9 3.9 %copy-start.14 = (f32[88,104]{1,0:T(8,128)S(1)}, f32[88,104]{1,0:T(8,128)}, u32[]{:S(2)}) copy-start(f32[88,104]{1,0:T(8,128)} %constant.182.clone) | copy-start | bytes 109828
  14.1 2.4 %copy-start.12 = (bf16[352,149,1]{0,1,2:T(8,128)(2,1)S(1)}, bf16[352,149,1]{0,1,2:T(8,128)(2,1)}, u32[]{:S(2)}) copy-start(bf16[352,149,1]{0,1,2:T(8,128)(2,1)} %constant.203) | copy-start | bytes 314692
  16.6 0.9 copy-start.11
  19.9 30.0 %all-to-all-start = ((f32[4,528,256]{2,1,0:T(8,128)}), f32[4,528,256]{2,1,0:T(8,128)S(1)}, u32[]{:S(2)}, u32[]{:S(2)}) async-start(f32[4,528,256]{2,1,0:T(8,128)} %bitcast.6), calls=%async_computation | async-start | bytes 4325376 | tf_op jit(solution)/shard_map/all_to_all | solution.py:241
  49.8 1.4 %copy-start.4 = (f32[4,528,256]{2,1,0:T(8,128)}, f32[4,528,256]{2,1,0:T(8,128)S(1)}, u32[]{:S(2)}) copy-start(f32[4,528,256]{2,1,0:T(8,128)S(1)} %all-to-all-done.u_ref) | copy-start | bytes 6488068
  83.0 4.0 %copy-start.17 = (f32[264]{0:T(512)S(1)}, f32[264]{0:T(512)}, u32[]{:S(2)}) copy-start(f32[264]{0:T(512)} %param.22) | copy-start | bytes 3172
  83.0 7.3 %copy-start = (f32[2184,128]{1,0:T(8,128)S(1)}, f32[2184,128]{1,0:T(8,128)}, u32[]{:S(2)}) copy-start(f32[2184,128]{1,0:T(8,128)} %get-tuple-element.6) | copy-start | bytes 3354628
  83.0 30.1 %all-to-all-start.1 = ((f32[4,528,256]{2,1,0:T(8,128)}), f32[4,528,256]{2,1,0:T(8,128)S(1)}, u32[]{:S(2)}, u32[]{:S(2)}) async-start(f32[4,528,256]{2,1,0:T(8,128)} %get-tuple-element.5), calls=%async_computation.1 | async-start | bytes 4325376 | tf_op jit(solution)/shard_map/all_to_all | solution.py:281
  92.0 21.1 %copy-start.10 = (bf16[4,88,149,1]{1,2,3,0:T(8,128)(2,1)S(1)}, bf16[4,88,149,1]{1,2,3,0:T(8,128)(2,1)}, u32[]{:S(2)}) copy-start(bf16[4,88,149,1]{1,2,3,0:T(8,128)(2,1)} %constant.205) | copy-start | bytes 314692
  93.8 20.1 %copy-start.9 = (bf16[4,88,149,1]{1,2,3,0:T(8,128)(2,1)S(1)}, bf16[4,88,149,1]{1,2,3,0:T(8,128)(2,1)}, u32[]{:S(2)}) copy-start(bf16[4,88,149,1]{1,2,3,0:T(8,128)(2,1)} %constant.206) | copy-start | bytes 314692
  115.4 5.4 %copy-start.20 = (f32[100]{0:T(128)S(1)}, f32[100]{0:T(128)}, u32[]{:S(2)}) copy-start(f32[100]{0:T(128)} %constant.202) | copy-start | bytes 1204
  116.2 10.5 %collective-permute-start.1 = (f32[6,17,512]{2,1,0:T(8,128)S(1)}, f32[6,17,512]{2,1,0:T(8,128)S(1)}, u32[]{:S(2)}, u32[]{:S(2)}) collective-permute-start(f32[6,17,512]{2,1,0:T(8,128)S(1)} %slice.63), channel_id=1, source_target_pairs={{0,1},{1,2},{2,3},{3,4},{4,5},{5,6},{6,7},{8,9},{9,10},{10,11},{11... | collective-permute-start | bytes 626696 | tf_op jit(solution)/shard_map/ppermute | solution.py:287
  120.8 6.1 %copy-start.1 = (f32[3,132,512]{2,1,0:T(8,128)S(1)}, f32[3,132,512]{2,1,0:T(8,128)}, u32[]{:S(2)}) copy-start(f32[3,132,512]{2,1,0:T(8,128)} %param.16) | copy-start | bytes 2433028
  120.8 6.1 %copy-start.3 = (f32[3,132,512]{2,1,0:T(8,128)S(1)}, f32[3,132,512]{2,1,0:T(8,128)}, u32[]{:S(2)}) copy-start(f32[3,132,512]{2,1,0:T(8,128)} %param.18) | copy-start | bytes 2433028
  120.8 6.1 %copy-start.5 = (f32[132,512]{1,0:T(8,128)S(1)}, f32[132,512]{1,0:T(8,128)}, u32[]{:S(2)}) copy-start(f32[132,512]{1,0:T(8,128)} %fusion.39) | copy-start | bytes 811012
  120.8 6.1 %copy-start.6 = (f32[3,132,512]{2,1,0:T(8,128)S(1)}, f32[3,132,512]{2,1,0:T(8,128)}, u32[]{:S(2)}) copy-start(f32[3,132,512]{2,1,0:T(8,128)} %param.19) | copy-start | bytes 2433028
  120.8 6.0 %copy-start.7 = (f32[3,132,512]{2,1,0:T(8,128)S(1)}, f32[3,132,512]{2,1,0:T(8,128)}, u32[]{:S(2)}) copy-start(f32[3,132,512]{2,1,0:T(8,128)} %param.17) | copy-start | bytes 2433028
where the time goes:
time: 129 us
  waiting for transfers between devices  42.7 us (33%)
  Pallas kernels  31.8 us (25%)
  other arithmetic  18.5 us (14%)
  local copies, waits for them, and re-layouts  13.9 us (11%)
  starting transfers between devices  13.6 us (11%)
  matrix products  7.01 us (5%)
    pallas_call x1, Pallas kernels, body(): pl.pallas_call(functools.partial(core, nf, pts, nodes), grid=(total // ch...  31.8 us
    all_to_all x1, waiting for transfers between devices, body(): lax.all_to_all(pushed, 'fourier', split_axis=0, concat_axis=0, tiled=True)  17.6 us
    all_to_all x1, waiting for transfers between devices, body(): lax.all_to_all(tiles, 'fourier', split_axis=0, concat_axis=0, tiled=True)  14.4 us
    convert_element_type x5, other arithmetic, split_device(): return (hi.astype(bf16), (values - hi).astype(bf16))  13.4 us
    unnamed x47, local copies, waits for them, and re-layouts  7.61 us
    ppermute x1, waiting for transfers between devices, body(): upper = lax.ppermute(packed[:, :edge], 'meridian', below)  5.7 us
    ppermute x1, waiting for transfers between devices, body(): carried = lax.ppermute(force[:, rows:], 'meridian', above)  4.96 us
    ppermute x1, starting transfers between devices, body(): carried = lax.ppermute(force[:, rows:], 'meridian', above)  4.56 us
  transfers between devices with their start and end apart: 4, of which 4 were waited for; matrix products, arithmetic and copies ran while one was open for 20% of the time, Pallas kernels for 0%

commit v1 on v0

v1 whole, which is shorter than its diff:
```python
import functools
import math

import jax
import jax.numpy as jnp
import numpy as np
from jax import lax
from jax.experimental import pallas as pl
from jax.experimental.pallas import tpu as pltpu
from jax.sharding import PartitionSpec as P

ORD = 8
EB = 8
BASIS = 2 * ORD + 1
kernel_weight = 0.0001
bf16 = jnp.bfloat16
f32 = jnp.float32
PAIRS = [(a, b) for a in range(6) for b in range(a, 6)]
PART_A, PART_B, PART_P = (0, 5, 4), (5, 1, 3), (4, 3, 2)


def gll_tables():
    x = np.array([-1.0, -math.sqrt(3.0 / 7.0), 0.0, math.sqrt(3.0 / 7.0), 1.0])
    weights = np.array([0.1, 49.0 / 90.0, 32.0 / 45.0, 49.0 / 90.0, 0.1])
    factor = np.array([np.prod([x[i] - x[k] for k in range(5) if k != i]) for i in range(5)])
    derive = np.zeros((5, 5))
    for i in range(5):
        for k in range(5):
            if i != k:
                derive[i, k] = factor[i] / (factor[k] * (x[i] - x[k]))
            else:
                derive[i, k] = sum(1.0 / (x[i] - x[o]) for o in range(5) if o != i)
    return derive, np.outer(weights, weights).reshape(25)


def sample_count(orders):
    n = orders + 2 * ORD + 1
    return n, 0 if n <= 64 else -(-(n - 64) // 128)


def place(re, im, nb):
    cut, n = 128 * nb, re.shape[1]
    rest = np.zeros((re.shape[0], 128))
    head = np.zeros((2, re.shape[0], cut))
    wide = min(n, cut)
    head[0, :, :wide], head[1, :, :wide] = re[:, :wide], im[:, :wide]
    if n > cut:
        rest[:, :n - cut], rest[:, 64:64 + n - cut] = re[:, cut:], im[:, cut:]
    return np.concatenate([head[0], head[1], rest], axis=1)


def waves(orders):
    n, nb = sample_count(orders)
    at = np.arange(-ORD, orders + ORD + 1)
    turn = 2 * np.pi * ((at[:, None] * np.arange(n)[None, :]) % n) / n
    return place(np.cos(turn), np.sin(turn), nb), place(np.sin(turn), -np.cos(turn), nb)


def with_turned(table):
    turned = np.zeros_like(table)
    turned[0::2], turned[1::2] = -table[1::2], table[0::2]
    return np.concatenate([table, turned], axis=1).astype(np.float32)


def block_tables(orders, own):
    ec, es = waves(orders)
    inner = np.zeros((own + 4 * ORD, ec.shape[1]))
    for row, p in [(2 * p, p) for p in range(orders)] + [(own + 2 * i, i - ORD) for i in range(ORD)] \
            + [(own + 2 * ORD + 2 * i, orders + i) for i in range(ORD)]:
        inner[row], inner[row + 1] = 0.5 * ec[p + ORD], 0.5 * es[p + ORD]
    first, last = np.zeros_like(inner), np.zeros_like(inner)
    first[0], first[1] = 0.5 * ec[ORD], -inner[1]
    for p in range(1, ORD + 1):
        first[2 * p] += 0.5 * ec[ORD - p]
        first[2 * p + 1] -= 0.5 * es[ORD - p]
    first[own:own + 2 * ORD] = -inner[own:own + 2 * ORD]
    last[own + 2 * ORD:] = -inner[own + 2 * ORD:]
    last[own + 2 * ORD + 1] += ec[orders + ORD]
    for j in range(1, ORD + 1):
        last[2 * (orders - j)] += 0.5 * ec[orders + j + ORD]
        last[2 * (orders - j) + 1] -= 0.5 * es[orders + j + ORD]
    halo_last = np.zeros_like(inner)
    halo_last[own + 2 * ORD + 1] = 0.5 * ec[orders + ORD]
    return [with_turned(t) for t in (inner, first, last, halo_last)]


def basis_rows(orders):
    n, nb = sample_count(orders)
    j = np.arange(BASIS)[:, None]
    turn = ((j + 1) // 2) * (2 * np.pi * np.arange(n)[None, :] / n)
    rows = np.where((j % 2 == 0) & (j > 0), np.sin(turn), np.cos(turn))
    both = place(rows, rows, nb)
    return both[:, 128 * nb:]


def split_host(values):
    wide = np.asarray(values, np.float32)
    hi = wide.astype(bf16)
    return hi, (wide - hi.astype(np.float32)).astype(bf16)


def split_device(values):
    hi = lax.reduce_precision(values, 8, 7)
    return hi.astype(bf16), (values - hi).astype(bf16)


def split(values):
    hi = values.astype(bf16)
    return hi, (values - hi.astype(f32)).astype(bf16)


def nt(a, b):
    return lax.dot_general(a, b, (((1,), (1,)), ((), ())), preferred_element_type=f32)


def nn(a, b):
    return lax.dot_general(a, b, (((1,), (0,)), ((), ())), preferred_element_type=f32)


def line(matrix, u):
    s0, d0, s1, d1 = u[0] + u[4], u[0] - u[4], u[1] + u[3], u[1] - u[3]
    out = [None] * 5
    for i in range(2):
        m = [float(v) for v in matrix[i]]
        odd = (0.5 * (m[0] - m[4])) * d0 + (0.5 * (m[1] - m[3])) * d1
        even = (0.5 * (m[0] + m[4])) * s0 + (0.5 * (m[1] + m[3])) * s1 + m[2] * u[2]
        out[i], out[4 - i] = even + odd, odd - even
    m = [float(v) for v in matrix[2]]
    out[2] = m[0] * d0 + m[1] * d1
    return out


def core(cfg, x_ref, hx_ref, mod_ref, rad_ref, fh_ref, fl_ref, ah_ref, al_ref, perm_ref, a3_ref, aa_ref, wrow_ref,
         f_ref, hb_ref, k_ref, uz, es, cs, ps, accb, s_ref, s1_ref, s2_ref, t3_ref):
    nf, own, R, wide, count_a, nodes, nb, hrow, derive = cfg
    lanes = x_ref.shape[2]
    W = 256 * nb + 128
    blocks = 2 * nb + 1
    halo = 4 * ORD
    tables = ((fh_ref, fl_ref), (ah_ref, al_ref))

    def onehot(shape, hit):
        a = lax.broadcasted_iota(jnp.int32, shape, 0)
        b = lax.broadcasted_iota(jnp.int32, shape, 1)
        return jnp.where(hit(a, b), 1.0, 0.0).astype(bf16)

    s_ref[...] = onehot((lanes, 2 * own), lambda a, b: (a % 2) * own + a // 2 == b)
    spot = lambda a: (a % 2) * 128 + (a // halo) * (2 * ORD) + (a % halo) // 2
    s1_ref[...] = onehot((128, 256), lambda a, b: (a < 2 * halo) & ((spot(a) == b) | (spot(a) + halo == b)))
    s2_ref[...] = onehot((128, 256), lambda a, b: (a < 2 * halo) & (spot(a) + 2 * halo == b))
    for l, (h, lo) in enumerate(tables):
        t3_ref[l, 0:halo] = h[own:]
        t3_ref[l, halo:2 * halo] = lo[own:]
        t3_ref[l, 2 * halo:3 * halo] = h[own:]
        t3_ref[l, 3 * halo:] = jnp.zeros((128 - 3 * halo, 2 * W), bf16)

    def moduli_step(r, carry):
        m = jnp.concatenate([mod_ref[d, r] for d in range(nf)], axis=1) * wrow_ref[0:1, :]
        h, lo = split(m)
        rows = jnp.concatenate([h, h, lo, jnp.zeros_like(h)], axis=0)
        mt = nt(perm_ref[...], rows).astype(bf16)
        cs[pl.ds(pl.multiple_of(r * nodes, 8), nodes), :] = nn(mt, a3_ref[...])
        return carry

    lax.fori_loop(0, 21, moduli_step, 0)

    for l, (h_ref, l_ref) in enumerate(tables):
        def ahead(c, carry, l=l, h_ref=h_ref, l_ref=l_ref):
            lc = 3 * l + c
            xh, xl = split(x_ref[lc])
            dh, dl = nn(xh, s_ref[...]).astype(bf16), nn(xl, s_ref[...]).astype(bf16)
            hh, hl = split(hx_ref[lc])
            he = (nn(hh, s1_ref[...]) + nn(hl, s2_ref[...])).astype(bf16)
            for par in range(2):
                ph, plo = dh[:, par * own:(par + 1) * own], dl[:, par * own:(par + 1) * own]
                at = pl.ds(pl.multiple_of((2 * lc + par) * R, 8), R)
                out = (nn(ph, h_ref[:own]) + nn(ph, l_ref[:own]) + nn(plo, h_ref[:own])
                       + nn(he[:, par * 128:(par + 1) * 128], t3_ref[l]))
                for b in range(2 * blocks):
                    uz[b, at, :] = out[:, 128 * b:128 * (b + 1)]
            return carry
        lax.fori_loop(0, 3, ahead, 0)

    def point(a, j):
        p = wide * a + j
        return p % 2, p // 2 + (hrow if a == 4 * count_a else 0)

    def strain_step(t, carry):
        l, blk = t // blocks, t % blocks
        lane = pl.multiple_of(blk * 128, 128)
        blk_z = blocks + blk

        def grid(c, ea, at_blk):
            out = []
            for i in range(5):
                row = []
                for j in range(5):
                    par, r = point(4 * ea + i, j)
                    base = (2 * (3 * l + c) + par) * R + r
                    row.append(uz[at_blk, pl.ds(base, 8, stride=2), :])
                out.append(row)
            return out

        def put(v, ea, i, j, value):
            row = pl.multiple_of((6 * l + v) * nodes + ((ea * 5 + i) * 5 + j) * 8, 8)
            es[pl.ds(row, 8), pl.ds(lane, 128)] = value

        for ea in range(count_a):
            rad = lambda i, j: rad_ref[((ea * 5 + i) * 5 + j) * 8:((ea * 5 + i) * 5 + j) * 8 + 8, :]
            cols = lambda u: [[row[j] for row in u] for j in range(5)]
            u = grid(0, ea, blk)
            for j, col in enumerate(cols(u)):
                for i, v in enumerate(line(derive, col)):
                    put(0, ea, i, j, v)
            shear = [line(derive, row) for row in u]
            u = grid(1, ea, blk)
            for j, col in enumerate(cols(u)):
                for i, v in enumerate(line(derive, col)):
                    put(5, ea, i, j, v + shear[i][j])
            for i, row in enumerate(u):
                for j, v in enumerate(line(derive, row)):
                    put(1, ea, i, j, v)
            u = grid(2, ea, blk)
            z = grid(0, ea, blk_z)
            for j, col in enumerate(cols(u)):
                for i, v in enumerate(line(derive, col)):
                    put(4, ea, i, j, v + rad(i, j) * z[i][j])
            z = grid(1, ea, blk_z)
            for i, row in enumerate(u):
                for j, v in enumerate(line(derive, row)):
                    put(3, ea, i, j, v + rad(i, j) * z[i][j])
            z = grid(2, ea, blk_z)
            for i in range(5):
                for j in range(5):
                    put(2, ea, i, j, rad(i, j) * z[i][j])
        return carry

    lax.fori_loop(0, 2 * blocks, strain_step, 0)

    def node_step(t, carry):
        row = pl.multiple_of(t * 8, 8)
        at = lambda v: pl.ds(pl.multiple_of(v * nodes + row, 8), 8)

        def one(c_lane, e_lane, prods):
            ce, el = slice(c_lane, c_lane + 128), slice(e_lane, e_lane + 128)
            fw = [es[at(v), el] for v in range(6)]
            ad = [es[at(6 + v), el] for v in range(6)]
            sf, sa = [None] * 6, [None] * 6

            def add(sums, v, term):
                sums[v] = term if sums[v] is None else sums[v] + term

            out = []
            for r, (v, w) in enumerate(PAIRS):
                c = cs[at(r), ce]
                add(sf, v, c * fw[w])
                add(sa, v, c * ad[w])
                if v != w:
                    add(sf, w, c * fw[v])
                    add(sa, w, c * ad[v])
                    prod = fw[v] * ad[w] + fw[w] * ad[v]
                else:
                    prod = fw[v] * ad[v]
                if prods is not None:
                    ps[at(r), ce] = ps[at(r), ce] + prod
                else:
                    ps[at(r), ce] = prod
            for v in range(6):
                es[at(v), el] = sf[v]
                es[at(6 + v), el] = sa[v]
            return out

        for b in range(nb):
            one(128 * b, 128 * b, None)
            one(128 * b, 128 * (nb + b), True)
        one(128 * nb, 256 * nb, None)
        return carry

    lax.fori_loop(0, nodes // 8, node_step, 0)

    def project_step(r, carry):
        ph, plo = split(ps[pl.ds(pl.multiple_of(r * nodes, 8), nodes), :])
        first = nt(aa_ref[...], ph)
        accb[r] = first[:32] + first[32:] + nt(aa_ref[:32], plo)
        return carry

    lax.fori_loop(0, 21, project_step, 0)

    def force_step(t, carry):
        l, blk = t // blocks, t % blocks
        lane = pl.multiple_of(blk * 128, 128)
        blk_z = blocks + blk
        top = lax.broadcasted_iota(jnp.int32, (8, 128), 0) == 0

        def get(v, ea, i, j):
            row = pl.multiple_of((6 * l + v) * nodes + ((ea * 5 + i) * 5 + j) * 8, 8)
            return es[pl.ds(row, 8), pl.ds(lane, 128)]

        def store(c, a, row, at_blk):
            def where(j):
                par, r = point(a, j)
                return (2 * (3 * l + c) + par) * R + r
            for j in range(1, 4):
                uz[at_blk, pl.ds(where(j), 8, stride=2), :] = row[j]
            back = pltpu.roll(row[4], 1, 0)
            uz[at_blk, pl.ds(where(0), 8, stride=2), :] = row[0] + jnp.where(top, 0.0, back)
            uz[at_blk, pl.ds(where(4) + 14, 1), :] = row[4][7:8]

        last = wide * (4 * count_a + 1)
        for c in range(3):
            held, held_z = None, None
            spare = (2 * (3 * l + c) + last % 2) * R + last // 2 + hrow
            for b in (blk, blk_z):
                uz[b, pl.ds(spare, 1), :] = jnp.zeros((1, 128), f32)
            for ea in range(count_a):
                rad = lambda i, j: rad_ref[((ea * 5 + i) * 5 + j) * 8:((ea * 5 + i) * 5 + j) * 8 + 8, :]
                cols = [line(derive.T, [get(PART_A[c], ea, i, j) for i in range(5)]) for j in range(5)]
                for i in range(5):
                    row = line(derive.T, [get(PART_B[c], ea, i, j) for j in range(5)])
                    row = [row[j] + cols[j][i] for j in range(5)]
                    row_z = [rad(i, j) * get(PART_P[c], ea, i, j) for j in range(5)]
                    if i == 0 and held is not None:
                        row = [p + q for p, q in zip(row, held)]
                        row_z = [p + q for p, q in zip(row_z, held_z)]
                    if i == 4 and ea + 1 < count_a:
                        held, held_z = row, row_z
                    else:
                        store(c, 4 * ea + i, row, blk)
                        store(c, 4 * ea + i, row_z, blk_z)
        return carry

    lax.fori_loop(0, 2 * blocks, force_step, 0)

    for l in range(2):
        h_ref, l_ref = tables[1 - l]

        def back(c, carry, l=l, h_ref=h_ref, l_ref=l_ref):
            lc = 3 * l + c
            both, edge_h, edge_l = [], [], []
            for par in range(2):
                at = pl.ds(pl.multiple_of((2 * lc + par) * R, 8), R)
                h, lo = split(jnp.concatenate([uz[b, at, :] for b in range(2 * blocks)], axis=1))
                both.append(nt(h, h_ref[:own]) + nt(h, l_ref[:own]) + nt(lo, h_ref[:own]))
                edge_h.append(nt(h, t3_ref[1 - l]))
                edge_l.append(nt(lo, t3_ref[1 - l]))
            h, lo = split(jnp.concatenate(both, axis=1))
            f_ref[lc] = nt(h, s_ref[...]) + nt(lo, s_ref[...])
            h, lo = split(jnp.concatenate(edge_h, axis=1))
            edge = nt(h, s1_ref[...]) + nt(lo, s1_ref[...])
            h, lo = split(jnp.concatenate(edge_l, axis=1))
            hb_ref[lc] = edge + nt(h, s2_ref[...]) + nt(lo, s2_ref[...])
            return carry
        lax.fori_loop(0, 3, back, 0)

    acc = accb[...].reshape(21 * 32, nodes)
    h, lo = split(acc)
    k_ref[...] = (nn(h, perm_ref[...]) + nn(lo, perm_ref[...])).reshape(k_ref.shape)


def body(forward_now, forward_last, adjoint_now, adjoint_last, moduli, inv_radius, inv_mass):
    derive, weights = gll_tables()
    wide = 4 * EB + 1
    nf = lax.axis_size("fourier")
    nm = lax.axis_size("meridian")
    me = lax.axis_index("fourier")
    comps, rows, lanes = forward_now.shape
    local = lanes // 2
    total = local * nf
    orders = local // 2
    own = -(-local // 128) * 128
    row_count = 2 * rows // wide
    count_a = row_count // 4
    nodes_mine = moduli.shape[3]
    nodes = nodes_mine * nf
    edge = (wide + 1) // 2
    start = -(-rows // 8) * 8
    R = -(-(start + edge) // 16) * 16
    n, nb = sample_count(orders)
    W = 256 * nb + 128
    halo = 4 * ORD

    packed = jnp.concatenate([forward_now, adjoint_now], axis=0)
    below = [(i + 1, i) for i in range(nm - 1)]
    above = [(i, i + 1) for i in range(nm - 1)]
    upper = lax.ppermute(packed[:, :edge], "meridian", below)
    packed = jnp.concatenate([jnp.pad(packed, ((0, 0), (0, start - rows), (0, 0))),
                              jnp.pad(upper, ((0, 0), (0, R - start - edge), (0, 0)))], axis=1)
    ring_up = [(i, (i + 1) % nf) for i in range(nf)]
    ring_down = [((i + 1) % nf, i) for i in range(nf)]
    low = lax.ppermute(packed[:, :, lanes - halo:], "fourier", ring_up)
    up = lax.ppermute(packed[:, :, :halo], "fourier", ring_down)
    hx = jnp.pad(jnp.concatenate([low, up], axis=2), ((0, 0), (0, 0), (0, 128 - 2 * halo)))
    mods = jnp.broadcast_to(moduli[None, :, :, 0, :], (nf, 21, BASIS, nodes_mine))
    mods = lax.all_to_all(mods, "fourier", split_axis=0, concat_axis=0, tiled=True)
    mods = jnp.pad(mods, ((0, 0), (0, 0), (0, 32 - BASIS), (0, 128 - nodes_mine)))

    inner, first, last, halo_last = block_tables(orders, own)
    is_first = jnp.where(me == 0, 1.0, 0.0).astype(f32)
    is_last = jnp.where(me == nf - 1, 1.0, 0.0).astype(f32)
    head, tail = 24, slice(local - 2 * ORD, local)
    row = np.arange(own + halo)
    at_order = np.where(row < own, row // 2, np.where(row < own + 2 * ORD, (row - own) // 2 - ORD,
                                                      orders + (row - own - 2 * ORD) // 2))
    nyquist = (row // 2) == (own + 2 * ORD) // 2
    turn = jnp.asarray(at_order, f32) + (me * orders).astype(f32)
    turn = turn * (1.0 - jnp.asarray(nyquist, f32) * is_last)
    scale = jnp.concatenate([jnp.ones((own + halo, W), f32), jnp.broadcast_to(turn[:, None], (own + halo, W))], axis=1)
    fix_turned = with_turned(np.where(np.arange(head)[:, None] == 1, -inner[:head, :W], 0.0).astype(np.float32))
    parts_a = [inner[:head] + is_first * first[:head], inner[head:local - 2 * ORD] * jnp.ones((1, 1), f32),
               inner[tail] + is_last * last[tail], jnp.asarray(inner[local:own]),
               inner[own:] + is_first * first[own:] + is_last * last[own:]]
    parts_f = [inner[:head] + is_first * fix_turned, parts_a[1], jnp.asarray(inner[tail]), parts_a[3],
               is_last * halo_last[own:]]
    fh, fl = split_device(jnp.concatenate(parts_f, axis=0) * scale)
    ah, al = split_device(jnp.concatenate(parts_a, axis=0) * scale)

    rows_a = basis_rows(orders)
    bh, bl = split_host(rows_a)
    a3 = np.zeros((128, rows_a.shape[1]), bf16)
    a3[0:BASIS], a3[32:32 + BASIS], a3[64:64 + BASIS] = bh, bl, bh
    aa = np.zeros((64, rows_a.shape[1]), bf16)
    aa[0:BASIS], aa[32:32 + BASIS] = bh, bl
    perm = np.zeros((nodes, nf * 128), np.float32)
    wrow = np.zeros((8, nf * 128), np.float32)
    for ea in range(count_a):
        for eb in range(EB):
            for ij in range(25):
                q = (ea * EB + eb) * 25 + ij
                spot = (q // nodes_mine) * 128 + q % nodes_mine
                perm[(ea * 25 + ij) * EB + eb, spot] = 1.0
                wrow[:, spot] = weights[ij]
    radius = jnp.transpose(inv_radius.reshape(count_a, EB, 25), (0, 2, 1)).reshape(nodes, 1)
    radius = jnp.broadcast_to(radius, (nodes, 128))

    cfg = (nf, own, R, wide, count_a, nodes, nb, start - rows, derive)
    vmem = pl.BlockSpec(memory_space=pltpu.VMEM)
    CW = rows_a.shape[1]
    force, spill, acc = pl.pallas_call(
        functools.partial(core, cfg),
        out_shape=(jax.ShapeDtypeStruct((2 * comps, R, lanes), f32),
                   jax.ShapeDtypeStruct((2 * comps, R, 128), f32),
                   jax.ShapeDtypeStruct((21, 32, nf * 128), f32)),
        in_specs=[vmem] * 12,
        out_specs=(vmem, vmem, vmem),
        scratch_shapes=[pltpu.VMEM((2 * W // 128, 4 * comps * R, 128), f32), pltpu.VMEM((12 * nodes, W), f32),
                        pltpu.VMEM((21 * nodes, CW), f32), pltpu.VMEM((21 * nodes, CW), f32),
                        pltpu.VMEM((21, 32, nodes), f32), pltpu.VMEM((lanes, 2 * own), bf16),
                        pltpu.VMEM((128, 256), bf16), pltpu.VMEM((128, 256), bf16),
                        pltpu.VMEM((2, 128, 2 * W), bf16)],
        compiler_params=pltpu.CompilerParams(vmem_limit_bytes=60 * 1024 * 1024),
    )(packed, hx, mods, radius, fh, fl, ah, al, jnp.asarray(perm.astype(bf16)), jnp.asarray(a3), jnp.asarray(aa),
      jnp.asarray(wrow * (2.0 / n)))

    to_up = lax.ppermute(spill[:, :, halo:2 * halo], "fourier", ring_up)
    to_low = lax.ppermute(spill[:, :, :halo], "fourier", ring_down)
    force = force + jnp.pad(to_up, ((0, 0), (0, 0), (0, lanes - halo)))
    force = force + jnp.pad(to_low, ((0, 0), (0, 0), (lanes - halo, 0)))
    carried = lax.ppermute(force[:, start:start + edge], "meridian", above)
    force = force[:, :rows] + jnp.pad(carried, ((0, 0), (0, rows - edge), (0, 0)))
    mass = inv_mass.reshape(rows, 2)
    is_even = lax.broadcasted_iota(jnp.int32, (rows, lanes), 1) % 2 == 0
    mass = jnp.where(is_even, mass[:, :1], mass[:, 1:])
    forward_next = 2.0 * forward_now - forward_last - mass * force[:comps]
    adjoint_next = 2.0 * adjoint_now - adjoint_last - mass * force[comps:]
    sums = acc.reshape(21, 32, nf, 128)[:, :BASIS, :, :nodes_mine]
    sums = jnp.transpose(sums, (2, 0, 1, 3))
    sums = lax.all_to_all(sums, "fourier", split_axis=0, concat_axis=0, tiled=True).sum(axis=0)
    wq = np.tile(weights, nodes_mine // 25) * (kernel_weight * 2.0 * total / n)
    return (forward_next, adjoint_next, (sums * jnp.asarray(wq, f32))[:, :, None, :])


def solution(mesh):
    field = P(None, "meridian", "fourier")
    grid = P(None, None, "meridian", "fourier")
    in_specs = (field, field, field, field, grid, P("meridian"), P("meridian"))
    return jax.shard_map(body, mesh=mesh, in_specs=in_specs, out_specs=(field, field, grid),
                         check_vma=False)
```

time: 129 us -> 127 us (0.984)
  Pallas kernels: 31.8 us -> 47.9 us
  waiting for transfers between devices: 42.7 us -> 32.9 us
  matrix products: 7.01 us -> 0 us
  other arithmetic: 18.5 us -> 12 us
  starting transfers between devices: 13.6 us -> 17.8 us
    all_to_all x2, waiting for transfers between devices: 32 us -> 8.22 us  [the longest x1 8.21 us: body(): lax.all_to_all(sums, 'fourier', split_axis=0, concat_axis=0, tiled=True)]
    pallas_call x1, Pallas kernels: 31.8 us -> 47.9 us  [body(): pl.pallas_call(functools.partial(core, cfg), out_shape=(jax.ShapeDtypeStr...]
    ppermute x1 -> x5, waiting for transfers between devices: 4.96 us -> 20.6 us  [the longest x1 9.66 us: body(): low = lax.ppermute(packed[:, :, lanes - halo:], 'fourier', ring_up)]
    convert_element_type x5 -> x2, other arithmetic: 13.4 us -> 2.18 us  [split_device(): return (hi.astype(bf16), (values - hi).astype(bf16))]
    dot_general x7 -> x0, matrix products: 7.01 us -> none  [the longest x1 2.39 us: body(): apart = jnp.einsum('crx,xy->cry', packed, order, precision=high)]
    ppermute x1 -> x5, starting transfers between devices: 4.56 us -> 8.57 us  [the longest x1 4.77 us: body(): carried = lax.ppermute(force[:, start:start + edge], 'meridian', above)]
    concatenate x2, other arithmetic: 0.09 us -> 3.88 us  [the longest x1 2.15 us: body(): jnp.concatenate([low, up], axis=2)]
    unnamed x47 -> x52, local copies, waits for them, and re-layouts: 7.61 us -> 5.25 us
  transfers between devices with their start and end apart: 4 -> 8, of which waited for: 4 -> 6; matrix products, arithmetic and copies ran while one was open for 20% -> 12% of each run, Pallas kernels for 0% -> 0%
where the time goes in v1:
time: 127 us; the launch traced here: 126 us
  Pallas kernels  47.9 us (38%)
  waiting for transfers between devices  32.9 us (26%)
  starting transfers between devices  17.8 us (14%)
  local copies, waits for them, and re-layouts  14.4 us (11%)
  other arithmetic  12 us (9%)
    pallas_call x1, Pallas kernels, body(): pl.pallas_call(functools.partial(core, cfg), out_shape=(jax.ShapeDtypeStr...  47.9 us
    ppermute x1, waiting for transfers between devices, body(): low = lax.ppermute(packed[:, :, lanes - halo:], 'fourier', ring_up)  9.66 us
    ppermute x1, waiting for transfers between devices, body(): to_up = lax.ppermute(spill[:, :, halo:2 * halo], 'fourier', ring_up)  9.34 us
    all_to_all x1, waiting for transfers between devices, body(): lax.all_to_all(sums, 'fourier', split_axis=0, concat_axis=0, tiled=True)  8.21 us
    unnamed x52, local copies, waits for them, and re-layouts  5.25 us
    ppermute x1, starting transfers between devices, body(): carried = lax.ppermute(force[:, start:start + edge], 'meridian', above)  4.77 us
    all_to_all x1, starting transfers between devices, body(): lax.all_to_all(mods, 'fourier', split_axis=0, concat_axis=0, tiled=True)  4.26 us
    ppermute x1, waiting for transfers between devices, body(): upper = lax.ppermute(packed[:, :edge], 'meridian', below)  4.05 us
  transfers between devices with their start and end apart: 8, of which 6 were waited for; matrix products, arithmetic and copies ran while one was open for 12% of the time, Pallas kernels for 0%

profile of v1, /device:TPU:0, one launch (start us, length us, event | category | flops | bytes accessed | tf_op | source)
XLA Modules:
  0.0 126.0 jit_solution(60751486976740634)
XLA Ops:
  0.7 1.3 %constant_dynamic-update-slice_fusion.1 = f32[6,132,512]{2,1,0:T(8,128)S(1)} fusion(f32[3,132,512]{2,1,0:T(8,128)} %param.26), kind=kLoop, calls=%fused_computation.38 | loop fusion | bytes 1646592
  2.1 1.2 copy-done.1
  3.4 1.4 %collective-permute-start = (f32[6,17,512]{2,1,0:T(8,128)S(1)}, f32[6,17,512]{2,1,0:T(8,128)}, u32[]{:S(2)}, u32[]{:S(2)}) collective-permute-start(f32[6,17,512]{2,1,0:T(8,128)S(1)} %slice.50), channel_id=1, source_target_pairs={{1,0},{2,1},{3,2},{4,3},{5,4},{6,5},{7,6},{9,8},{10,9},{11,10},{12... | collective-permute-start | bytes 626696 | tf_op jit(solution)/shard_map/ppermute | solution.py:385
  4.9 1.0 broadcast_in_dim.50
  5.9 4.3 %all-to-all-start = ((f32[4,21,17,100]{3,1,2,0:T(8,128)}), f32[4,21,17,100]{3,1,2,0:T(8,128)S(1)}, u32[]{:S(2)}, u32[]{:S(2)}) async-start(f32[4,21,17,100]{3,1,2,0:T(8,128)} %broadcast_in_dim.50), calls=%async_computation | async-start | bytes 1671168 | tf_op jit(solution)/shard_map/all_to_all | solution.py:394
  10.4 1.1 fusion
  11.5 4.0 %collective-permute-done = f32[6,17,512]{2,1,0:T(8,128)} collective-permute-done((f32[6,17,512]{2,1,0:T(8,128)S(1)}, f32[6,17,512]{2,1,0:T(8,128)}, u32[]{:S(2)}, u32[]{:S(2)}) %collective-permute-start) | collective-permute-done | bytes 208928 | tf_op jit(solution)/shard_map/ppermute | solution.py:385
  15.5 1.7 %select_maximum_fusion.x_ref = f32[6,160,512]{2,1,0:T(8,128)S(1)} fusion(f32[6,17,512]{2,1,0:T(8,128)} %collective-permute-done, f32[6,132,512]{2,1,0:T(8,128)} %copy-done.1), kind=kLoop, calls=%fused_computation | loop fusion | flops 2457600 | bytes 3796992 | tf_op jit(solution)/shard_map/concatenate | solution.py:386
  17.3 1.3 %fusion.13 = (f32[6,160,32]{2,1,0:T(8,128)}, f32[6,160,32]{2,1,0:T(8,128)}) fusion(f32[6,160,512]{2,1,0:T(8,128)S(1)} %select_maximum_fusion.x_ref), kind=kLoop, calls=%fused_computation.45 | loop fusion | bytes 491520 | tf_op jit(solution)/shard_map/slice | solution.py:390
  18.5 1.7 %collective-permute-start.2 = (f32[6,160,32]{2,1,0:T(8,128)}, f32[6,160,32]{2,1,0:T(8,128)}, u32[]{:S(2)}, u32[]{:S(2)}) collective-permute-start(f32[6,160,32]{2,1,0:T(8,128)} %get-tuple-element.24), channel_id=1, source_target_pairs={{8,0},{16,8},{24,16},{0,24},{9,1},{17,9},{25,17},{1,25},{10,2},{18... | collective-permute-start | bytes 368648 | tf_op jit(solution)/shard_map/ppermute | solution.py:391
  20.3 1.1 fusion.1
  21.7 9.7 %collective-permute-done.1 = f32[6,160,32]{2,1,0:T(8,128)} collective-permute-done((f32[6,160,32]{2,1,0:T(8,128)}, f32[6,160,32]{2,1,0:T(8,128)}, u32[]{:S(2)}, u32[]{:S(2)}) %collective-permute-start.1) | collective-permute-done | bytes 122912 | tf_op jit(solution)/shard_map/ppermute | solution.py:390
  31.7 2.2 %select_maximum_fusion.1.hx_ref = f32[6,160,128]{2,1,0:T(8,128)} fusion(f32[6,160,32]{2,1,0:T(8,128)} %collective-permute-done.2, f32[6,160,32]{2,1,0:T(8,128)} %collective-permute-done.1), kind=kLoop, calls=%fused_computation.24 | loop fusion | flops 491520 | bytes 737280 | tf_op jit(solution)/shard_map/concatenate | solution.py:392
  34.0 1.3 %pad.32.mod_ref = f32[4,21,32,128]{3,2,1,0:T(8,128)} pad(f32[4,21,17,100]{3,2,1,0:T(8,128)S(1)} %copy.44, f32[]{:T(128)} %constant.68.clone.1), padding=0_0x0_0x0_15x0_28 | pad | bytes 1947460 | tf_op jit(solution)/shard_map/jit(_pad)/pad | solution.py:395
  35.3 0.8 broadcast_in_dim.52.rad_ref
  36.1 47.9 %shard_map.270 = (f32[6,160,512]{2,1,0:T(8,128)}, f32[6,160,128]{2,1,0:T(8,128)}, f32[21,32,512]{2,1,0:T(8,128)}) custom-call(f32[6,160,512]{2,1,0:T(8,128)} %copy-done, f32[6,160,128]{2,1,0:T(8,128)} %select_maximum_fusion.1.hx_ref, f32[4,21,32,128]{3,2,1,0:T(8,128)} %pad.32.mod_ref, f32[400,128]{1,0:T(8,128)} %broadcast_in_dim.52.rad_ref, ...), custom_call_target="tpu_custom_call" | custom-call | tf_op jit(solution)/shard_map/pallas_call | solution.py:438
  84.0 1.4 %fusion.14 = (f32[6,160,32]{2,1,0:T(8,128)S(1)}, f32[6,160,32]{2,1,0:T(8,128)S(1)}) fusion(f32[6,160,128]{2,1,0:T(8,128)} %get-tuple-element.7), kind=kLoop, calls=%fused_computation.46 | loop fusion | bytes 491520 | tf_op jit(solution)/shard_map/slice | solution.py:454
  85.4 1.1 collective-permute-start.3
  86.6 0.9 collective-permute-start.4
  87.8 9.3 %collective-permute-done.3 = f32[6,160,32]{2,1,0:T(8,128)S(1)} collective-permute-done((f32[6,160,32]{2,1,0:T(8,128)S(1)}, f32[6,160,32]{2,1,0:T(8,128)S(1)}, u32[]{:S(2)}, u32[]{:S(2)}) %collective-permute-start.3) | collective-permute-done | bytes 122912 | tf_op jit(solution)/shard_map/ppermute | solution.py:454
  97.1 1.3 %collective-permute-done.4 = f32[6,160,32]{2,1,0:T(8,128)S(1)} collective-permute-done((f32[6,160,32]{2,1,0:T(8,128)S(1)}, f32[6,160,32]{2,1,0:T(8,128)S(1)}, u32[]{:S(2)}, u32[]{:S(2)}) %collective-permute-start.4) | collective-permute-done | bytes 122912 | tf_op jit(solution)/shard_map/ppermute | solution.py:455
  98.5 1.8 %pad_add_fusion = f32[6,160,512]{2,1,0:T(8,128)S(1)} fusion(f32[6,160,32]{2,1,0:T(8,128)S(1)} %collective-permute-done.4, f32[6,160,512]{2,1,0:T(8,128)} %get-tuple-element.6, f32[6,160,32]{2,1,0:T(8,128)S(1)} %collective-permute-done.3), kind=kLoop, calls=%fused_computation.3 | loop fusion | flops 983040 | bytes 4177920 | tf_op jit(solution)/shard_map/add | solution.py:457
  100.3 0.7 slice.54
  101.0 4.8 %collective-permute-start.5 = (f32[6,17,512]{2,1,0:T(8,128)}, f32[6,17,512]{2,1,0:T(8,128)}, u32[]{:S(2)}, u32[]{:S(2)}) collective-permute-start(f32[6,17,512]{2,1,0:T(8,128)} %slice.54), channel_id=1, source_target_pairs={{0,1},{1,2},{2,3},{3,4},{4,5},{5,6},{6,7},{8,9},{9,10},{10,11},{11... | collective-permute-start | bytes 626696 | tf_op jit(solution)/shard_map/ppermute | solution.py:458
  105.8 0.8 fusion.8
  106.6 1.7 %reshape.102 = f32[21,32,4,128]{3,2,1,0:T(4,128)S(1)} reshape(f32[21,32,512]{2,1,0:T(8,128)} %get-tuple-element.8) | data formatting | bytes 2752512 | tf_op jit(solution)/shard_map/reshape | solution.py:465
  108.4 1.0 copy.54
  109.4 3.5 %all-to-all-start.1 = ((f32[4,21,17,100]{3,1,2,0:T(8,128)}), f32[4,21,17,100]{3,1,2,0:T(8,128)S(1)}, u32[]{:S(2)}, u32[]{:S(2)}) async-start(f32[4,21,17,100]{3,1,2,0:T(8,128)} %bitcast.9), calls=%async_computation.1 | async-start | bytes 1671168 | tf_op jit(solution)/shard_map/all_to_all | solution.py:467
  113.0 1.3 %slice_add_fusion = f32[6,132,512]{2,1,0:T(8,128)S(1)} fusion(f32[6,160,512]{2,1,0:T(8,128)S(1)} %pad_add_fusion, f32[6,17,512]{2,1,0:T(8,128)} %collective-permute-done.5), kind=kLoop, calls=%fused_computation.4 | loop fusion | flops 405504 | bytes 3452928 | tf_op jit(solution)/shard_map/add | solution.py:459
  115.0 1.8 %fusion.6 = (f32[3,132,512]{2,1,0:T(8,128)}, f32[3,132,512]{2,1,0:T(8,128)}) fusion(f32[6,132,512]{2,1,0:T(8,128)S(1)} %slice_add_fusion, f32[3,132,512]{2,1,0:T(8,128)S(1)} %copy-done.7, f32[3,132,512]{2,1,0:T(8,128)S(1)} %copy-done.4, f32[132,512]{1,0:T(8,128)S(1)} %copy-done.6, f32[3,132,512]{2,1,0:T(8,128)S(1)} %copy-done.8, f32[3,132,512]{2,1,0:T(8,128)S(1)} %copy-done.2), kind=kLoop, calls=%fused_computation.20 | loop fusion | flops 1622016 | bytes 6758400 | tf_op jit(solution)/shard_map/sub | solution.py:464
  116.8 8.2 %all-to-all-done.1 = f32[4,21,17,100]{3,1,2,0:T(8,128)S(1)} async-done(((f32[4,21,17,100]{3,1,2,0:T(8,128)}), f32[4,21,17,100]{3,1,2,0:T(8,128)S(1)}, u32[]{:S(2)}, u32[]{:S(2)}) %all-to-all-start.1) | async-done | bytes 571232 | tf_op jit(solution)/shard_map/all_to_all | solution.py:467
  125.1 0.9 copy.49
  (70 shorter events, 2.4 us)
Async XLA Ops:
  0.6 1.4 %copy-start.3 = (f32[3,132,512]{2,1,0:T(8,128)S(1)}, f32[3,132,512]{2,1,0:T(8,128)}, u32[]{:S(2)}) copy-start(f32[3,132,512]{2,1,0:T(8,128)} %param.28) | copy-start | bytes 2433028
  0.6 4.2 %copy-start.10 = (f32[21,17,1,100]{3,2,1,0:T(1,128)S(1)}, f32[21,17,1,100]{3,2,1,0:T(1,128)}, u32[]{:S(2)}) copy-start(f32[21,17,1,100]{3,2,1,0:T(1,128)} %param.30) | copy-start | bytes 428404
  2.1 1.2 copy-start.1
  3.3 6.8 %copy-start.21 = (f32[288]{0:T(512)S(1)}, f32[288]{0:T(512)}, u32[]{:S(2)}) copy-start(f32[288]{0:T(512)} %constant.73.clone) | copy-start | bytes 3460
  3.3 6.8 %copy-start.22 = (f32[288]{0:T(512)S(1)}, f32[288]{0:T(512)}, u32[]{:S(2)}) copy-start(f32[288]{0:T(512)} %constant.74.clone) | copy-start | bytes 3460
  3.3 6.8 %copy-start.15 = (f32[24,768]{1,0:T(8,128)S(1)}, f32[24,768]{1,0:T(8,128)}, u32[]{:S(2)}) copy-start(f32[24,768]{1,0:T(8,128)} %constant.75.clone) | copy-start | bytes 221188
  3.3 6.8 %copy-start.16 = (f32[24,768]{1,0:T(8,128)S(1)}, f32[24,768]{1,0:T(8,128)}, u32[]{:S(2)}) copy-start(f32[24,768]{1,0:T(8,128)} %constant.76.clone) | copy-start | bytes 221188
  3.3 6.8 %copy-start.17 = (f32[24,768]{1,0:T(8,128)S(1)}, f32[24,768]{1,0:T(8,128)}, u32[]{:S(2)}) copy-start(f32[24,768]{1,0:T(8,128)} %constant.83.clone) | copy-start | bytes 221188
  3.3 6.9 %copy-start.11 = (f32[32,768]{1,0:T(8,128)S(1)}, f32[32,768]{1,0:T(8,128)}, u32[]{:S(2)}) copy-start(f32[32,768]{1,0:T(8,128)} %constant.80.clone) | copy-start | bytes 294916
  3.3 6.9 %copy-start.12 = (f32[32,768]{1,0:T(8,128)S(1)}, f32[32,768]{1,0:T(8,128)}, u32[]{:S(2)}) copy-start(f32[32,768]{1,0:T(8,128)} %constant.81.clone) | copy-start | bytes 294916
  3.4 6.9 %copy-start.13 = (f32[32,768]{1,0:T(8,128)S(1)}, f32[32,768]{1,0:T(8,128)}, u32[]{:S(2)}) copy-start(f32[32,768]{1,0:T(8,128)} %constant.82.clone) | copy-start | bytes 294916
  3.4 6.9 %copy-start.14 = (f32[32,768]{1,0:T(8,128)S(1)}, f32[32,768]{1,0:T(8,128)}, u32[]{:S(2)}) copy-start(f32[32,768]{1,0:T(8,128)} %constant.84.clone) | copy-start | bytes 294916
  3.4 12.1 %collective-permute-start = (f32[6,17,512]{2,1,0:T(8,128)S(1)}, f32[6,17,512]{2,1,0:T(8,128)}, u32[]{:S(2)}, u32[]{:S(2)}) collective-permute-start(f32[6,17,512]{2,1,0:T(8,128)S(1)} %slice.50), channel_id=1, source_target_pairs={{1,0},{2,1},{3,2},{4,3},{5,4},{6,5},{7,6},{9,8},{10,9},{11,10},{12... | collective-permute-start | bytes 626696 | tf_op jit(solution)/shard_map/ppermute | solution.py:385
  4.9 5.5 %copy-start.5 = (f32[216,768]{1,0:T(8,128)S(1)}, f32[216,768]{1,0:T(8,128)}, u32[]{:S(2)}) copy-start(f32[216,768]{1,0:T(8,128)} %constant.77.clone) | copy-start | bytes 1990660
  4.9 5.5 %copy-start.9 = (f32[16,768]{1,0:T(8,128)S(1)}, f32[16,768]{1,0:T(8,128)}, u32[]{:S(2)}) copy-start(f32[16,768]{1,0:T(8,128)} %constant.79.clone) | copy-start | bytes 147460
  5.9 28.0 %all-to-all-start = ((f32[4,21,17,100]{3,1,2,0:T(8,128)}), f32[4,21,17,100]{3,1,2,0:T(8,128)S(1)}, u32[]{:S(2)}, u32[]{:S(2)}) async-start(f32[4,21,17,100]{3,1,2,0:T(8,128)} %broadcast_in_dim.50), calls=%async_computation | async-start | bytes 1671168 | tf_op jit(solution)/shard_map/all_to_all | solution.py:394
  10.1 1.3 %copy-start.18 = (f32[16,768]{1,0:T(8,128)S(1)}, f32[16,768]{1,0:T(8,128)}, u32[]{:S(2)}) copy-start(f32[16,768]{1,0:T(8,128)} %constant.78.clone) | copy-start | bytes 147460
  17.3 4.2 %copy-start = (f32[6,160,512]{2,1,0:T(8,128)}, f32[6,160,512]{2,1,0:T(8,128)S(1)}, u32[]{:S(2)}) copy-start(f32[6,160,512]{2,1,0:T(8,128)S(1)} %select_maximum_fusion.x_ref) | copy-start | bytes 5898244
  17.3 4.2 %copy-start.19 = (f32[400]{0:T(512)S(1)}, f32[400]{0:T(512)}, u32[]{:S(2)}) copy-start(f32[400]{0:T(512)} %param.31) | copy-start | bytes 4804
  18.5 12.8 %collective-permute-start.1 = (f32[6,160,32]{2,1,0:T(8,128)}, f32[6,160,32]{2,1,0:T(8,128)}, u32[]{:S(2)}, u32[]{:S(2)}) collective-permute-start(f32[6,160,32]{2,1,0:T(8,128)} %get-tuple-element.23), channel_id=1, source_target_pairs={{0,8},{8,16},{16,24},{24,0},{1,9},{9,17},{17,25},{25,1},{2,10},{10... | collective-permute-start | bytes 368648 | tf_op jit(solution)/shard_map/ppermute | solution.py:390
  18.5 13.1 %collective-permute-start.2 = (f32[6,160,32]{2,1,0:T(8,128)}, f32[6,160,32]{2,1,0:T(8,128)}, u32[]{:S(2)}, u32[]{:S(2)}) collective-permute-start(f32[6,160,32]{2,1,0:T(8,128)} %get-tuple-element.24), channel_id=1, source_target_pairs={{8,0},{16,8},{24,16},{0,24},{9,1},{17,9},{25,17},{1,25},{10,2},{18... | collective-permute-start | bytes 368648 | tf_op jit(solution)/shard_map/ppermute | solution.py:391
  84.0 3.4 %copy-start.20 = (f32[264]{0:T(512)S(1)}, f32[264]{0:T(512)}, u32[]{:S(2)}) copy-start(f32[264]{0:T(512)} %param.32) | copy-start | bytes 3172
  85.4 11.7 %collective-permute-start.3 = (f32[6,160,32]{2,1,0:T(8,128)S(1)}, f32[6,160,32]{2,1,0:T(8,128)S(1)}, u32[]{:S(2)}, u32[]{:S(2)}) collective-permute-start(f32[6,160,32]{2,1,0:T(8,128)S(1)} %get-tuple-element.31), channel_id=1, source_target_pairs={{0,8},{8,16},{16,24},{24,0},{1,9},{9,17},{17,25},{25,1},{2,10},{10... | collective-permute-start | bytes 368648 | tf_op jit(solution)/shard_map/ppermute | solution.py:454
  86.6 11.9 %collective-permute-start.4 = (f32[6,160,32]{2,1,0:T(8,128)S(1)}, f32[6,160,32]{2,1,0:T(8,128)S(1)}, u32[]{:S(2)}, u32[]{:S(2)}) collective-permute-start(f32[6,160,32]{2,1,0:T(8,128)S(1)} %get-tuple-element.32), channel_id=1, source_target_pairs={{8,0},{16,8},{24,16},{0,24},{9,1},{17,9},{25,17},{1,25},{10,2},{18... | collective-permute-start | bytes 368648 | tf_op jit(solution)/shard_map/ppermute | solution.py:455
  101.0 11.9 %collective-permute-start.5 = (f32[6,17,512]{2,1,0:T(8,128)}, f32[6,17,512]{2,1,0:T(8,128)}, u32[]{:S(2)}, u32[]{:S(2)}) collective-permute-start(f32[6,17,512]{2,1,0:T(8,128)} %slice.54), channel_id=1, source_target_pairs={{0,1},{1,2},{2,3},{3,4},{4,5},{5,6},{6,7},{8,9},{9,10},{10,11},{11... | collective-permute-start | bytes 626696 | tf_op jit(solution)/shard_map/ppermute | solution.py:458
  109.4 15.6 %all-to-all-start.1 = ((f32[4,21,17,100]{3,1,2,0:T(8,128)}), f32[4,21,17,100]{3,1,2,0:T(8,128)S(1)}, u32[]{:S(2)}, u32[]{:S(2)}) async-start(f32[4,21,17,100]{3,1,2,0:T(8,128)} %bitcast.9), calls=%async_computation.1 | async-start | bytes 1671168 | tf_op jit(solution)/shard_map/all_to_all | solution.py:467
  112.9 1.4 %copy-start.2 = (f32[3,132,512]{2,1,0:T(8,128)S(1)}, f32[3,132,512]{2,1,0:T(8,128)}, u32[]{:S(2)}) copy-start(f32[3,132,512]{2,1,0:T(8,128)} %param.26) | copy-start | bytes 2433028
  112.9 1.5 %copy-start.4 = (f32[3,132,512]{2,1,0:T(8,128)S(1)}, f32[3,132,512]{2,1,0:T(8,128)}, u32[]{:S(2)}) copy-start(f32[3,132,512]{2,1,0:T(8,128)} %param.28) | copy-start | bytes 2433028
  112.9 1.5 %copy-start.6 = (f32[132,512]{1,0:T(8,128)S(1)}, f32[132,512]{1,0:T(8,128)}, u32[]{:S(2)}) copy-start(f32[132,512]{1,0:T(8,128)} %fusion.8) | copy-start | bytes 811012
  112.9 1.8 %copy-start.7 = (f32[3,132,512]{2,1,0:T(8,128)S(1)}, f32[3,132,512]{2,1,0:T(8,128)}, u32[]{:S(2)}) copy-start(f32[3,132,512]{2,1,0:T(8,128)} %param.29) | copy-start | bytes 2433028
  112.9 2.0 %copy-start.8 = (f32[3,132,512]{2,1,0:T(8,128)S(1)}, f32[3,132,512]{2,1,0:T(8,128)}, u32[]{:S(2)}) copy-start(f32[3,132,512]{2,1,0:T(8,128)} %param.27) | copy-start | bytes 2433028
  115.0 10.1 %copy-start.23 = (f32[100]{0:T(128)S(1)}, f32[100]{0:T(128)}, u32[]{:S(2)}) copy-start(f32[100]{0:T(128)} %constant.89.clone) | copy-start | bytes 1204

commit v2 on v1

--- a/solution.py
+++ b/solution.py
@@ -12,6 +12,8 @@
 ORD = 8
 EB = 8
 BASIS = 2 * ORD + 1
+HR = (4 * EB + 2) // 2 // 8 * 8 + 8
+MESH = pl.DeviceIdType.MESH
 kernel_weight = 0.0001
 bf16 = jnp.bfloat16
 f32 = jnp.float32
@@ -130,56 +132,185 @@
     return out
 
 
-def core(cfg, x_ref, hx_ref, mod_ref, rad_ref, fh_ref, fl_ref, ah_ref, al_ref, perm_ref, a3_ref, aa_ref, wrow_ref,
-         f_ref, hb_ref, k_ref, uz, es, cs, ps, accb, s_ref, s1_ref, s2_ref, t3_ref):
-    nf, own, R, wide, count_a, nodes, nb, hrow, derive = cfg
-    lanes = x_ref.shape[2]
+def core(cfg, fn_ref, fo_ref, an_ref, ao_ref, mod_ref, rad_ref, mass_ref, fh_ref, fl_ref, ah_ref, al_ref, perm_ref,
+         a3_ref, aa_ref, wrow_ref, krow_ref, nyq_ref, f_ref, a_ref, k_ref,
+         uz, es, cs, ps, accb, s_ref, s1_ref, s2_ref, t3_ref, xb, last, modr, modx, rh, stage, ring, force,
+         edge_f, rm, spill, rspill, kb, kr, lsem, ssem, rsem):
+    nf, nm, own, R, wide, count_a, nodes, nb, hrow, edge, derive = cfg
+    rows, lanes = fn_ref.shape[1:]
     W = 256 * nb + 128
     blocks = 2 * nb + 1
     halo = 4 * ORD
+    main = R - HR
     tables = ((fh_ref, fl_ref), (ah_ref, al_ref))
+    me, mi = lax.axis_index("fourier"), lax.axis_index("meridian")
+    up, down = lax.rem(me + 1, nf), lax.rem(me + nf - 1, nf)
+    has_prev, has_next = mi > 0, mi < nm - 1
+    is_last = jnp.where(me == nf - 1, 1.0, 0.0).astype(f32)
+
+    def remote(src, dst, at, meridian, fourier):
+        return pltpu.make_async_remote_copy(
+            src_ref=src, dst_ref=dst, send_sem=ssem.at[at], recv_sem=rsem.at[at],
+            device_id={"meridian": meridian, "fourier": fourier}, device_id_type=MESH)
+
+    first = pl.ds(0, HR)
+    body_rows, tail_rows = pl.ds(0, main), pl.ds(main, HR)
+    prev, nxt = mi - 1, mi + 1
+    to_prev = [remote(fn_ref.at[:, first], rh.at[0:3], 0, prev, me),
+               remote(an_ref.at[:, first], rh.at[3:6], 1, prev, me),
+               remote(stage.at[0, first], ring.at[0, tail_rows], 2, prev, down),
+               remote(stage.at[1, first], ring.at[1, tail_rows], 3, prev, up)]
+    to_ring = [remote(stage.at[0], ring.at[0, body_rows], 4, mi, down),
+               remote(stage.at[1], ring.at[1, body_rows], 5, mi, up)]
+    to_next = [remote(edge_f, rm, 6, nxt, me),
+               remote(spill.at[0, tail_rows], rspill.at[0, tail_rows], 7, nxt, down),
+               remote(spill.at[1, tail_rows], rspill.at[1, tail_rows], 8, nxt, up)]
+    to_spill = [remote(spill.at[0, body_rows], rspill.at[0, body_rows], 9, mi, down),
+                remote(spill.at[1, body_rows], rspill.at[1, body_rows], 10, mi, up)]
+    mod_send = [remote(mod_ref, modr.at[me], 11 + s, mi, lax.rem(me + s + 1, nf)) for s in range(nf - 1)]
+    mod_recv = [remote(mod_ref, modr.at[lax.rem(me + nf - 1 - s, nf)], 11 + s, mi, me) for s in range(nf - 1)]
+    base = 11 + nf - 1
+    k_send = [remote(kb.at[lax.rem(me + s + 1, nf)], kr.at[s], base + s, mi, lax.rem(me + s + 1, nf))
+              for s in range(nf - 1)]
+
+    barrier = pltpu.get_barrier_semaphore()
+
+    def greet(meridian, fourier):
+        pl.semaphore_signal(barrier, inc=1, device_id={"meridian": meridian, "fourier": fourier},
+                            device_id_type=MESH)
+
+    for s in range(1, nf):
+        greet(mi, lax.rem(me + s, nf))
+    for there, other in ((has_prev, prev), (has_next, nxt)):
+        @pl.when(there)
+        def _(other=other):
+            for f in (me, up, down):
+                greet(other, f)
+
+    loads = [pltpu.make_async_copy(an_ref, xb.at[3:6], lsem.at[0]), pltpu.make_async_copy(fn_ref, xb.at[0:3], lsem.at[1]),
+             pltpu.make_async_copy(fo_ref, last.at[0:3], lsem.at[2]), pltpu.make_async_copy(ao_ref, last.at[3:6], lsem.at[3]),
+             pltpu.make_async_copy(mod_ref, modr.at[me], lsem.at[4])]
+    for copy in loads:
+        copy.start()
 
     def onehot(shape, hit):
         a = lax.broadcasted_iota(jnp.int32, shape, 0)
         b = lax.broadcasted_iota(jnp.int32, shape, 1)
         return jnp.where(hit(a, b), 1.0, 0.0).astype(bf16)
 
+    loads[0].wait()
+    loads[1].wait()
+    lane_id = lax.broadcasted_iota(jnp.int32, (rows, 128), 1)
+    for way, source in enumerate((0, lanes - 128)):
+        total = jnp.zeros((rows, 128), f32)
+        for c in range(3):
+            shift = (halo * c + (halo if way else 0)) % 128
+            turned = xb[3 + c, :, source:source + 128]
+            turned = pltpu.roll(turned, shift, 1) if shift else turned
+            total = jnp.where((lane_id >= halo * c) & (lane_id < halo * (c + 1)), turned, total)
+            if way == 0:
+                turned = pltpu.roll(xb[c, :, :128], 3 * halo + 2 * c - 2, 1)
+                spot = 3 * halo + 2 * c
+                total = jnp.where((lane_id >= spot) & (lane_id < spot + 2), turned, total)
+        stage[way, :rows] = total
+        stage[way, rows:] = jnp.zeros((main - rows, 128), f32)
+
+    pl.semaphore_wait(barrier, nf - 1 + 3 * (has_prev.astype(jnp.int32) + has_next.astype(jnp.int32)))
+
+    @pl.when(has_prev)
+    def _():
+        for copy in to_prev:
+            copy.start()
+    for copy in to_ring + mod_send:
+        copy.start()
+
     s_ref[...] = onehot((lanes, 2 * own), lambda a, b: (a % 2) * own + a // 2 == b)
-    spot = lambda a: (a % 2) * 128 + (a // halo) * (2 * ORD) + (a % halo) // 2
-    s1_ref[...] = onehot((128, 256), lambda a, b: (a < 2 * halo) & ((spot(a) == b) | (spot(a) + halo == b)))
-    s2_ref[...] = onehot((128, 256), lambda a, b: (a < 2 * halo) & (spot(a) + 2 * halo == b))
+    spot = lambda a: (a % 2) * 128 + (a // 128) * (2 * ORD) + (a % 128) // 2
+    s1_ref[...] = onehot((256, 256), lambda a, b: (a % 128 < halo) & ((spot(a) == b) | (spot(a) + halo == b)))
+    s2_ref[...] = onehot((256, 256), lambda a, b: (a % 128 < halo) & (spot(a) + 2 * halo == b))
     for l, (h, lo) in enumerate(tables):
         t3_ref[l, 0:halo] = h[own:]
         t3_ref[l, halo:2 * halo] = lo[own:]
         t3_ref[l, 2 * halo:3 * halo] = h[own:]
         t3_ref[l, 3 * halo:] = jnp.zeros((128 - 3 * halo, 2 * W), bf16)
 
-    def moduli_step(r, carry):
-        m = jnp.concatenate([mod_ref[d, r] for d in range(nf)], axis=1) * wrow_ref[0:1, :]
-        h, lo = split(m)
-        rows = jnp.concatenate([h, h, lo, jnp.zeros_like(h)], axis=0)
-        mt = nt(perm_ref[...], rows).astype(bf16)
-        cs[pl.ds(pl.multiple_of(r * nodes, 8), nodes), :] = nn(mt, a3_ref[...])
-        return carry
-
-    lax.fori_loop(0, 21, moduli_step, 0)
+    def samples(x, h_ref, l_ref):
+        xh, xl = split(x)
+        dh, dl = nn(xh, s_ref[...]).astype(bf16), nn(xl, s_ref[...]).astype(bf16)
+        out = []
+        for par in range(2):
+            ph, plo = dh[:, par * own:(par + 1) * own], dl[:, par * own:(par + 1) * own]
+            out.append(nn(ph, h_ref[:own]) + nn(ph, l_ref[:own]) + nn(plo, h_ref[:own]))
+        return out
 
     for l, (h_ref, l_ref) in enumerate(tables):
         def ahead(c, carry, l=l, h_ref=h_ref, l_ref=l_ref):
             lc = 3 * l + c
-            xh, xl = split(x_ref[lc])
-            dh, dl = nn(xh, s_ref[...]).astype(bf16), nn(xl, s_ref[...]).astype(bf16)
-            hh, hl = split(hx_ref[lc])
-            he = (nn(hh, s1_ref[...]) + nn(hl, s2_ref[...])).astype(bf16)
-            for par in range(2):
-                ph, plo = dh[:, par * own:(par + 1) * own], dl[:, par * own:(par + 1) * own]
-                at = pl.ds(pl.multiple_of((2 * lc + par) * R, 8), R)
-                out = (nn(ph, h_ref[:own]) + nn(ph, l_ref[:own]) + nn(plo, h_ref[:own])
-                       + nn(he[:, par * 128:(par + 1) * 128], t3_ref[l]))
+            for par, out in enumerate(samples(xb[lc], h_ref, l_ref)):
+                at = pl.ds(pl.multiple_of((2 * lc + par) * R, 8), rows)
                 for b in range(2 * blocks):
                     uz[b, at, :] = out[:, 128 * b:128 * (b + 1)]
             return carry
         lax.fori_loop(0, 3, ahead, 0)
+
+    @pl.when(has_next)
+    def _():
+        for copy in to_prev:
+            copy.wait_recv()
+
+    @pl.when(jnp.logical_not(has_next))
+    def _():
+        rh[...] = jnp.zeros_like(rh)
+        ring[:, main:] = jnp.zeros((2, HR, 128), f32)
+    for copy in to_ring:
+        copy.wait_recv()
+    for l, (h_ref, l_ref) in enumerate(tables):
+        for par, out in enumerate(samples(rh[3 * l:3 * l + 3].reshape(3 * HR, lanes), h_ref, l_ref)):
+            for c in range(3):
+                at = (2 * (3 * l + c) + par) * R + main
+                for b in range(2 * blocks):
+                    uz[b, at:at + HR, :] = out[c * HR:(c + 1) * HR, 128 * b:128 * (b + 1)]
+    for c in range(3):
+        low, upper = ring[1], ring[0]
+        if c:
+            low, upper = pltpu.roll(low, 128 - halo * c, 1), pltpu.roll(upper, 128 - halo * c, 1)
+        hh, hl = split(jnp.concatenate([low, upper], axis=1))
+        he = (nn(hh, s1_ref[...]) + nn(hl, s2_ref[...])).astype(bf16)
+        for par in range(2):
+            at = (2 * (3 + c) + par) * R
+            out = nn(he[:, par * 128:(par + 1) * 128], t3_ref[1])
+            for b in range(2 * blocks):
+                uz[b, at:at + R, :] += out[:, 128 * b:128 * (b + 1)]
+
+    @pl.when(me == nf - 1)
+    def _():
+        for c in range(3):
+            for par in range(2):
+                spot = 3 * halo + 2 * c + par
+                column = ring[0, :, spot:spot + 1]
+                at = (2 * c + par) * R
+                for b in range(blocks):
+                    uz[b, at:at + R, :] += column * nyq_ref[0:1, 128 * b:128 * (b + 1)]
+
+    loads[4].wait()
+    for copy in mod_recv:
+        copy.wait_recv()
+    modx[...] = jnp.zeros_like(modx)
+    for r in range(21):
+        for d in range(nf):
+            modx[r, :BASIS, 128 * d:128 * (d + 1)] = modr[d, r * BASIS:(r + 1) * BASIS, :] * wrow_ref[0:1, 128 * d:128 * (d + 1)]
+
+    def moduli_step(t, carry):
+        rows_two = []
+        for k in range(2):
+            h, lo = split(modx[2 * t + k])
+            rows_two += [h, h, lo, jnp.zeros_like(h)]
+        mt = nt(perm_ref[...], jnp.concatenate(rows_two, axis=0)).astype(bf16)
+        for k in range(2):
+            cs[pl.ds(pl.multiple_of((2 * t + k) * nodes, 8), nodes), :] = nn(mt[:, 128 * k:128 * (k + 1)], a3_ref[...])
+        return carry
+
+    lax.fori_loop(0, 11, moduli_step, 0)
 
     def point(a, j):
         p = wide * a + j
@@ -196,8 +327,8 @@
                 row = []
                 for j in range(5):
                     par, r = point(4 * ea + i, j)
-                    base = (2 * (3 * l + c) + par) * R + r
-                    row.append(uz[at_blk, pl.ds(base, 8, stride=2), :])
+                    at = (2 * (3 * l + c) + par) * R + r
+                    row.append(uz[at_blk, pl.ds(at, 8, stride=2), :])
                 out.append(row)
             return out
 
@@ -241,50 +372,56 @@
         row = pl.multiple_of(t * 8, 8)
         at = lambda v: pl.ds(pl.multiple_of(v * nodes + row, 8), 8)
 
-        def one(c_lane, e_lane, prods):
-            ce, el = slice(c_lane, c_lane + 128), slice(e_lane, e_lane + 128)
-            fw = [es[at(v), el] for v in range(6)]
-            ad = [es[at(6 + v), el] for v in range(6)]
-            sf, sa = [None] * 6, [None] * 6
-
-            def add(sums, v, term):
-                sums[v] = term if sums[v] is None else sums[v] + term
-
-            out = []
+        def add(sums, v, term):
+            sums[v] = term if sums[v] is None else sums[v] + term
+
+        def one(ce, els):
+            fw = [[es[at(v), el] for v in range(6)] for el in els]
+            ad = [[es[at(6 + v), el] for v in range(6)] for el in els]
+            sf = [[None] * 6 for _ in els]
+            sa = [[None] * 6 for _ in els]
             for r, (v, w) in enumerate(PAIRS):
                 c = cs[at(r), ce]
-                add(sf, v, c * fw[w])
-                add(sa, v, c * ad[w])
-                if v != w:
-                    add(sf, w, c * fw[v])
-                    add(sa, w, c * ad[v])
-                    prod = fw[v] * ad[w] + fw[w] * ad[v]
-                else:
-                    prod = fw[v] * ad[v]
-                if prods is not None:
-                    ps[at(r), ce] = ps[at(r), ce] + prod
-                else:
-                    ps[at(r), ce] = prod
-            for v in range(6):
-                es[at(v), el] = sf[v]
-                es[at(6 + v), el] = sa[v]
-            return out
+                total = None
+                for f, a, tf, ta in zip(fw, ad, sf, sa):
+                    add(tf, v, c * f[w])
+                    add(ta, v, c * a[w])
+                    if v != w:
+                        add(tf, w, c * f[v])
+                        add(ta, w, c * a[v])
+                        prod = f[v] * a[w] + f[w] * a[v]
+                    else:
+                        prod = f[v] * a[v]
+                    total = prod if total is None else total + prod
+                ps[at(r), ce] = total
+            for el, tf, ta in zip(els, sf, sa):
+                for v in range(6):
+                    es[at(v), el] = tf[v]
+                    es[at(6 + v), el] = ta[v]
 
         for b in range(nb):
-            one(128 * b, 128 * b, None)
-            one(128 * b, 128 * (nb + b), True)
-        one(128 * nb, 256 * nb, None)
+            one(slice(128 * b, 128 * b + 128),
+                [slice(128 * b, 128 * b + 128), slice(128 * (nb + b), 128 * (nb + b) + 128)])
+        one(slice(128 * nb, 128 * nb + 128), [slice(256 * nb, 256 * nb + 128)])
         return carry
 
     lax.fori_loop(0, nodes // 8, node_step, 0)
 
     def project_step(r, carry):
         ph, plo = split(ps[pl.ds(pl.multiple_of(r * nodes, 8), nodes), :])
-        first = nt(aa_ref[...], ph)
-        accb[r] = first[:32] + first[32:] + nt(aa_ref[:32], plo)
+        both = nt(aa_ref[...], ph)
+        accb[r] = both[:32] + both[32:] + nt(aa_ref[:32], plo)
         return carry
 
     lax.fori_loop(0, 21, project_step, 0)
+    h, lo = split(accb[...].reshape(21 * 32, nodes))
+    whole = (nn(h, perm_ref[...]) + nn(lo, perm_ref[...])) * krow_ref[0:1, :]
+    for d in range(nf):
+        for r in range(21):
+            kb[d, r * BASIS:(r + 1) * BASIS, :] = whole[32 * r:32 * r + BASIS, 128 * d:128 * (d + 1)]
+        kb[d, 21 * BASIS:, :] = jnp.zeros((kb.shape[1] - 21 * BASIS, 128), f32)
+    for copy in k_send:
+        copy.start()
 
     def force_step(t, carry):
         l, blk = t // blocks, t % blocks
@@ -306,10 +443,10 @@
             uz[at_blk, pl.ds(where(0), 8, stride=2), :] = row[0] + jnp.where(top, 0.0, back)
             uz[at_blk, pl.ds(where(4) + 14, 1), :] = row[4][7:8]
 
-        last = wide * (4 * count_a + 1)
+        beyond = wide * (4 * count_a + 1)
         for c in range(3):
             held, held_z = None, None
-            spare = (2 * (3 * l + c) + last % 2) * R + last // 2 + hrow
+            spare = (2 * (3 * l + c) + beyond % 2) * R + beyond // 2 + hrow
             for b in (blk, blk_z):
                 uz[b, pl.ds(spare, 1), :] = jnp.zeros((1, 128), f32)
             for ea in range(count_a):
@@ -331,30 +468,119 @@
 
     lax.fori_loop(0, 2 * blocks, force_step, 0)
 
-    for l in range(2):
+    def interleave(values):
+        h, lo = split(values)
+        return nt(h, s_ref[...]) + nt(lo, s_ref[...])
+
+    def turn_back(parts, l, with_edge):
         h_ref, l_ref = tables[1 - l]
-
-        def back(c, carry, l=l, h_ref=h_ref, l_ref=l_ref):
-            lc = 3 * l + c
-            both, edge_h, edge_l = [], [], []
-            for par in range(2):
-                at = pl.ds(pl.multiple_of((2 * lc + par) * R, 8), R)
-                h, lo = split(jnp.concatenate([uz[b, at, :] for b in range(2 * blocks)], axis=1))
-                both.append(nt(h, h_ref[:own]) + nt(h, l_ref[:own]) + nt(lo, h_ref[:own]))
+        both, edge_h, edge_l = [], [], []
+        for part in parts:
+            h, lo = split(part)
+            both.append(nt(h, h_ref[:own]) + nt(h, l_ref[:own]) + nt(lo, h_ref[:own]))
+            if with_edge:
                 edge_h.append(nt(h, t3_ref[1 - l]))
                 edge_l.append(nt(lo, t3_ref[1 - l]))
-            h, lo = split(jnp.concatenate(both, axis=1))
-            f_ref[lc] = nt(h, s_ref[...]) + nt(lo, s_ref[...])
-            h, lo = split(jnp.concatenate(edge_h, axis=1))
-            edge = nt(h, s1_ref[...]) + nt(lo, s1_ref[...])
-            h, lo = split(jnp.concatenate(edge_l, axis=1))
-            hb_ref[lc] = edge + nt(h, s2_ref[...]) + nt(lo, s2_ref[...])
-            return carry
-        lax.fori_loop(0, 3, back, 0)
-
-    acc = accb[...].reshape(21 * 32, nodes)
-    h, lo = split(acc)
-    k_ref[...] = (nn(h, perm_ref[...]) + nn(lo, perm_ref[...])).reshape(k_ref.shape)
+        out = interleave(jnp.concatenate(both, axis=1))
+        if not with_edge:
+            return out, None
+        h, lo = split(jnp.concatenate(edge_h, axis=1))
+        side = nt(h, s1_ref[...]) + nt(lo, s1_ref[...])
+        h, lo = split(jnp.concatenate(edge_l, axis=1))
+        return out, side + nt(h, s2_ref[...]) + nt(lo, s2_ref[...])
+
+    def spread(side, c):
+        low, high = side[:, :128], side[:, 128:]
+        return (pltpu.roll(low, halo * c, 1), pltpu.roll(high, halo * c, 1)) if c else (low, high)
+
+    def read(lc, par, start, count):
+        at = (2 * lc + par) * R + start
+        return jnp.concatenate([uz[b, at:at + count, :] for b in range(2 * blocks)], axis=1)
+
+    high = jnp.zeros((R, 128), f32)
+    lane_r = lax.broadcasted_iota(jnp.int32, (R, 128), 1)
+    for c in range(3):
+        for par in range(2):
+            at = (2 * (3 + c) + par) * R
+            terms = None
+            for b in range(blocks):
+                term = uz[b, at:at + R, :] * nyq_ref[0:1, 128 * b:128 * (b + 1)]
+                terms = term if terms is None else terms + term
+            value = jnp.sum(terms, axis=1, keepdims=True) * is_last
+            high = jnp.where(lane_r == 3 * halo + 2 * c + par, value, high)
+    spill[0] = jnp.zeros((R, 128), f32)
+    spill[1] = high
+
+    for l in range(2):
+        parts = [jnp.concatenate([read(3 * l + c, par, main, HR) for c in range(3)], axis=0) for par in range(2)]
+        out, side = turn_back(parts, l, l == 0)
+        edge_f[3 * l:3 * l + 3] = out.reshape(3, HR, lanes)
+        if l == 0:
+            for c in range(3):
+                for way, value in enumerate(spread(side[c * HR:(c + 1) * HR], c)):
+                    spill[way, main:] += value
+
+    @pl.when(has_next)
+    def _():
+        for copy in to_next:
+            copy.start()
+    for c in range(3):
+        out, side = turn_back([read(c, par, 0, main) for par in range(2)], 0, True)
+        force[c] = out[:rows]
+        for way, value in enumerate(spread(side, c)):
+            spill[way, :main] += value
+    for copy in to_spill:
+        copy.start()
+    for c in range(3):
+        out, _ = turn_back([read(3 + c, par, 0, main) for par in range(2)], 1, False)
+        force[3 + c] = out[:rows]
+
+    lane_m = lax.broadcasted_iota(jnp.int32, (rows, 128), 1)
+
+    def gather(start, count):
+        for c in range(3):
+            up_turned = rspill[1, start:start + count]
+            up_turned = pltpu.roll(up_turned, 128 - halo * c, 1) if c else up_turned
+            force[c, :count, :128] += jnp.where(lane_m[:count] < halo, up_turned, 0.0)
+            low_turned = pltpu.roll(rspill[0, start:start + count], (128 - halo * (c + 1)), 1)
+            force[c, :count, lanes - 128:] += jnp.where(lane_m[:count] >= 128 - halo, low_turned, 0.0)
+            top_turned = pltpu.roll(rspill[1, start:start + count], 128 - 3 * halo - 2 * c + 2, 1)
+            force[3 + c, :count, :128] += jnp.where((lane_m[:count] >= 2) & (lane_m[:count] < 4), top_turned, 0.0)
+
+    @pl.when(has_prev)
+    def _():
+        for copy in to_next:
+            copy.wait_recv()
+        force[:, :edge] += rm[:, :edge]
+        gather(main, edge)
+    for copy in to_spill:
+        copy.wait_recv()
+    gather(0, rows)
+    loads[2].wait()
+    loads[3].wait()
+    is_even = lax.broadcasted_iota(jnp.int32, (rows, lanes), 1) % 2 == 0
+    mass = jnp.where(is_even, mass_ref[:, 0:1], mass_ref[:, 1:2])
+    for c in range(3):
+        f_ref[c] = 2.0 * xb[c] - last[c] - mass * force[c]
+        a_ref[c] = 2.0 * xb[3 + c] - last[3 + c] - mass * force[3 + c]
+    for copy in k_send:
+        copy.wait_recv()
+    total = kb[me]
+    for s in range(nf - 1):
+        total = total + kr[s]
+    k_ref[...] = total
+
+    @pl.when(has_prev)
+    def _():
+        for copy in to_prev:
+            copy.wait_send()
+
+    @pl.when(has_next)
+    def _():
+        for copy in to_next:
+            copy.wait_send()
+    for copy in to_ring + to_spill + mod_send + k_send:
+        copy.wait_send()
 
 
 def body(forward_now, forward_last, adjoint_now, adjoint_last, moduli, inv_radius, inv_mass):
@@ -374,25 +600,13 @@
     nodes = nodes_mine * nf
     edge = (wide + 1) // 2
     start = -(-rows // 8) * 8
-    R = -(-(start + edge) // 16) * 16
+    R = start + HR
     n, nb = sample_count(orders)
     W = 256 * nb + 128
     halo = 4 * ORD
 
-    packed = jnp.concatenate([forward_now, adjoint_now], axis=0)
-    below = [(i + 1, i) for i in range(nm - 1)]
-    above = [(i, i + 1) for i in range(nm - 1)]
-    upper = lax.ppermute(packed[:, :edge], "meridian", below)
-    packed = jnp.concatenate([jnp.pad(packed, ((0, 0), (0, start - rows), (0, 0))),
-                              jnp.pad(upper, ((0, 0), (0, R - start - edge), (0, 0)))], axis=1)
-    ring_up = [(i, (i + 1) % nf) for i in range(nf)]
-    ring_down = [((i + 1) % nf, i) for i in range(nf)]
-    low = lax.ppermute(packed[:, :, lanes - halo:], "fourier", ring_up)
-    up = lax.ppermute(packed[:, :, :halo], "fourier", ring_down)
-    hx = jnp.pad(jnp.concatenate([low, up], axis=2), ((0, 0), (0, 0), (0, 128 - 2 * halo)))
-    mods = jnp.broadcast_to(moduli[None, :, :, 0, :], (nf, 21, BASIS, nodes_mine))
-    mods = lax.all_to_all(mods, "fourier", split_axis=0, concat_axis=0, tiled=True)
-    mods = jnp.pad(mods, ((0, 0), (0, 0), (0, 32 - BASIS), (0, 128 - nodes_mine)))
+    flat = jnp.pad(moduli[:, :, 0, :].reshape(21 * BASIS, nodes_mine),
+                   ((0, -(21 * BASIS) % 8), (0, 128 - nodes_mine)))
 
     inner, first, last, halo_last = block_tables(orders, own)
     is_first = jnp.where(me == 0, 1.0, 0.0).astype(f32)
@@ -432,41 +646,40 @@
     radius = jnp.transpose(inv_radius.reshape(count_a, EB, 25), (0, 2, 1)).reshape(nodes, 1)
     radius = jnp.broadcast_to(radius, (nodes, 128))
 
-    cfg = (nf, own, R, wide, count_a, nodes, nb, start - rows, derive)
+    cfg = (nf, nm, own, R, wide, count_a, nodes, nb, start - rows, edge, derive)
     vmem = pl.BlockSpec(memory_space=pltpu.VMEM)
+    hbm = pl.BlockSpec(memory_space=pl.ANY)
     CW = rows_a.shape[1]
-    force, spill, acc = pl.pallas_call(
+    K_ROWS = flat.shape[0]
+    copies = 11 + 2 * (nf - 1)
+    field = jax.ShapeDtypeStruct((comps, rows, lanes), f32)
+    forward_next, adjoint_next, sums = pl.pallas_call(
         functools.partial(core, cfg),
-        out_shape=(jax.ShapeDtypeStruct((2 * comps, R, lanes), f32),
-                   jax.ShapeDtypeStruct((2 * comps, R, 128), f32),
-                   jax.ShapeDtypeStruct((21, 32, nf * 128), f32)),
-        in_specs=[vmem] * 12,
+        out_shape=(field, field, jax.ShapeDtypeStruct((K_ROWS, 128), f32)),
+        in_specs=[hbm] * 5 + [vmem] * 12,
         out_specs=(vmem, vmem, vmem),
         scratch_shapes=[pltpu.VMEM((2 * W // 128, 4 * comps * R, 128), f32), pltpu.VMEM((12 * nodes, W), f32),
-                        pltpu.VMEM((21 * nodes, CW), f32), pltpu.VMEM((21 * nodes, CW), f32),
+                        pltpu.VMEM((22 * nodes, CW), f32), pltpu.VMEM((21 * nodes, CW), f32),
                         pltpu.VMEM((21, 32, nodes), f32), pltpu.VMEM((lanes, 2 * own), bf16),
-                        pltpu.VMEM((128, 256), bf16), pltpu.VMEM((128, 256), bf16),
-                        pltpu.VMEM((2, 128, 2 * W), bf16)],
-        compiler_params=pltpu.CompilerParams(vmem_limit_bytes=60 * 1024 * 1024),
-    )(packed, hx, mods, radius, fh, fl, ah, al, jnp.asarray(perm.astype(bf16)), jnp.asarray(a3), jnp.asarray(aa),
-      jnp.asarray(wrow * (2.0 / n)))
-
-    to_up = lax.ppermute(spill[:, :, halo:2 * halo], "fourier", ring_up)
-    to_low = lax.ppermute(spill[:, :, :halo], "fourier", ring_down)
-    force = force + jnp.pad(to_up, ((0, 0), (0, 0), (0, lanes - halo)))
-    force = force + jnp.pad(to_low, ((0, 0), (0, 0), (lanes - halo, 0)))
-    carried = lax.ppermute(force[:, start:start + edge], "meridian", above)
-    force = force[:, :rows] + jnp.pad(carried, ((0, 0), (0, rows - edge), (0, 0)))
-    mass = inv_mass.reshape(rows, 2)
-    is_even = lax.broadcasted_iota(jnp.int32, (rows, lanes), 1) % 2 == 0
-    mass = jnp.where(is_even, mass[:, :1], mass[:, 1:])
-    forward_next = 2.0 * forward_now - forward_last - mass * force[:comps]
-    adjoint_next = 2.0 * adjoint_now - adjoint_last - mass * force[comps:]
-    sums = acc.reshape(21, 32, nf, 128)[:, :BASIS, :, :nodes_mine]
-    sums = jnp.transpose(sums, (2, 0, 1, 3))
-    sums = lax.all_to_all(sums, "fourier", split_axis=0, concat_axis=0, tiled=True).sum(axis=0)
-    wq = np.tile(weights, nodes_mine // 25) * (kernel_weight * 2.0 * total / n)
-    return (forward_next, adjoint_next, (sums * jnp.asarray(wq, f32))[:, :, None, :])
+                        pltpu.VMEM((256, 256), bf16), pltpu.VMEM((256, 256), bf16),
+                        pltpu.VMEM((2, 128, 2 * W), bf16),
+                        pltpu.VMEM((2 * comps, rows, lanes), f32), pltpu.VMEM((2 * comps, rows, lanes), f32),
+                        pltpu.VMEM((nf, K_ROWS, 128), f32), pltpu.VMEM((22, 32, nf * 128), f32),
+                        pltpu.VMEM((2 * comps, HR, lanes), f32), pltpu.VMEM((2, R - HR, 128), f32),
+                        pltpu.VMEM((2, R, 128), f32), pltpu.VMEM((2 * comps, rows, lanes), f32),
+                        pltpu.VMEM((2 * comps, HR, lanes), f32), pltpu.VMEM((2 * comps, HR, lanes), f32),
+                        pltpu.VMEM((2, R, 128), f32), pltpu.VMEM((2, R, 128), f32),
+                        pltpu.VMEM((nf, K_ROWS, 128), f32), pltpu.VMEM((nf - 1, K_ROWS, 128), f32),
+                        pltpu.SemaphoreType.DMA((5,)), pltpu.SemaphoreType.DMA((copies,)),
+                        pltpu.SemaphoreType.DMA((copies,))],
+        compiler_params=pltpu.CompilerParams(vmem_limit_bytes=60 * 1024 * 1024, collective_id=0,
+                                             has_side_effects=True),
+    )(forward_now, forward_last, adjoint_now, adjoint_last, flat, radius, inv_mass.reshape(rows, 2), fh, fl, ah, al,
+      jnp.asarray(perm.astype(bf16)), jnp.asarray(a3), jnp.asarray(aa), jnp.asarray(wrow * (2.0 / n)),
+      jnp.asarray(wrow * (kernel_weight * 2.0 * total / n)),
+      jnp.asarray(np.broadcast_to(0.5 * waves(orders)[0][orders + ORD], (8, W)).astype(np.float32)))
+    sums = sums[:21 * BASIS, :nodes_mine].reshape(21, BASIS, 1, nodes_mine)
+    return forward_next, adjoint_next, sums
 
 
 def solution(mesh):

time: 127 us -> 70.6 us (0.56)
  waiting for transfers between devices: 32.9 us -> 0 us
  starting transfers between devices: 17.8 us -> 0 us
  other arithmetic: 12 us -> 2.64 us
  Pallas kernels: 47.9 us -> 55.1 us
  local copies, waits for them, and re-layouts: 14.4 us -> 11 us
    ppermute x6 -> x0, waiting for transfers between devices: 24.6 us -> none  [the longest x1 9.66 us: body(): low = lax.ppermute(packed[:, :, lanes - halo:], 'fourier', ring_up)]
    ppermute x6 -> x0, starting transfers between devices: 9.99 us -> none  [the longest x1 4.77 us: body(): carried = lax.ppermute(force[:, start:start + edge], 'meridian', above)]
    all_to_all x2 -> x0, waiting for transfers between devices: 8.22 us -> none  [the longest x1 8.21 us: body(): lax.all_to_all(sums, 'fourier', split_axis=0, concat_axis=0, tiled=True)]
    all_to_all x2 -> x0, starting transfers between devices: 7.76 us -> none  [the longest x1 4.26 us: body(): lax.all_to_all(mods, 'fourier', split_axis=0, concat_axis=0, tiled=True)]
    pallas_call x1, Pallas kernels: 47.9 us -> 55.1 us  [body(): pl.pallas_call(functools.partial(core, cfg), out_shape=(field, field, jax...]
    concatenate x2 -> x0, other arithmetic: 3.88 us -> none  [the longest x1 2.15 us: body(): jnp.concatenate([low, up], axis=2)]
    slice x6 -> x0, local copies, waits for them, and re-layouts: 3.65 us -> none  [the longest x1 1.39 us: body(): to_up = lax.ppermute(spill[:, :, halo:2 * halo], 'fourier', ring_up)]
    add x2 -> x0, other arithmetic: 3.15 us -> none  [the longest x1 1.84 us: body(): force = force + jnp.pad(to_low, ((0, 0), (0, 0), (lanes - halo, 0)))]
  transfers between devices with their start and end apart: 8 -> 0, of which waited for: 6 -> 0; matrix products, arithmetic and copies ran while one was open for 12% -> 0% of each run, Pallas kernels for 0% -> 0%
where the time goes in v2:
time: 70.6 us; the launch traced here: 69.5 us
  Pallas kernels  55.1 us (78%)
  local copies, waits for them, and re-layouts  11 us (16%)
  other arithmetic  2.64 us (4%)
  between operations  0.83 us (1%)
    pallas_call x1, Pallas kernels, body(): pl.pallas_call(functools.partial(core, cfg), out_shape=(field, field, jax...  55.1 us
    unnamed x30, local copies, waits for them, and re-layouts  5.13 us
    convert_element_type x2, other arithmetic, split_device(): return (hi.astype(bf16), (values - hi).astype(bf16))  2.12 us
    reshape x1, local copies, waits for them, and re-layouts, body(): sums = sums[:21 * BASIS, :nodes_mine].reshape(21, BASIS, 1, nodes_mine)  1.77 us
    reshape x1, local copies, waits for them, and re-layouts, body(): inv_mass.reshape(rows, 2)  1.5 us

profile of v2, /device:TPU:0, one launch (start us, length us, event | category | flops | bytes accessed | tf_op | source)
XLA Modules:
  0.0 69.5 jit_solution(7740658929393070213)
XLA Ops:
  0.6 0.0 copy-start.13
  0.6 0.0 copy-start.12
  0.7 0.0 copy-start.11
  0.7 0.0 copy-start.2
  0.7 0.6 copy-done.13
  1.3 0.0 copy-done.12
  1.3 0.8 %reshape.18 = f32[2,8,25]{2,1,0:T(8,128)S(1)} reshape(f32[400]{0:T(512)} %param.32) | data formatting | bytes 3200 | tf_op jit(solution)/shard_map/reshape | solution.py:646
  2.1 0.1 copy.32
  2.2 0.1 broadcast_in_dim.6
  2.3 0.0 copy-start.8
  2.3 0.0 copy-start.9
  2.4 0.0 copy-start.7
  2.4 1.5 %reshape.19.mass_ref = f32[132,2]{1,0:T(8,128)} reshape(f32[264]{0:T(512)} %param.33) | data formatting | bytes 2112 | tf_op jit(solution)/shard_map/reshape | solution.py:677
  3.9 0.0 copy-start.4
  3.9 0.0 copy-start.5
  3.9 0.0 copy-start.6
  4.0 0.8 %copy-done.4 = f32[32,768]{1,0:T(8,128)S(1)} copy-done((f32[32,768]{1,0:T(8,128)S(1)}, f32[32,768]{1,0:T(8,128)}, u32[]{:S(2)}) %copy-start.4) | copy-done | bytes 98328
  4.8 0.0 copy-done.5
  4.8 0.0 copy-done.6
  4.9 0.8 %broadcast_in_dim.7.rad_ref = f32[400,128]{1,0:T(8,128)} broadcast(f32[400]{0:T(512)S(1)} %broadcast_in_dim.6), dimensions={0} | broadcast | bytes 206400 | tf_op jit(solution)/shard_map/broadcast_in_dim | solution.py:647
  5.7 0.1 copy-done.3
  5.8 0.5 reduce
  6.3 0.0 copy-start
  6.3 0.7 pad.5.mod_ref
  7.0 0.1 broadcast_in_dim.16
  7.1 0.3 copy-done
  7.5 1.1 %fusion.1 = (bf16[288,768]{1,0:T(8,128)(2,1)}, bf16[288,768]{1,0:T(8,128)(2,1)}) fusion(f32[288,384]{1,0:T(8,128)S(1)} %broadcast_in_dim.16, f32[32,768]{1,0:T(8,128)S(1)} %get-tuple-element.24, f32[16,768]{1,0:T(8,128)S(1)} %multiply_add_fusion.2, f32[216,768]{1,0:T(8,128)S(1)} %copy-done, f32[24,768]{1,0:T(8,128)S(1)} %get-tuple-element.22), kind=kLoop, calls=%fused_computation.9 | loop fusion | flops 1769472 | bytes 2211840 | tf_op jit(solution)/shard_map/convert_element_type | solution.py:106
  8.5 1.0 %fusion = (bf16[288,768]{1,0:T(8,128)(2,1)}, bf16[288,768]{1,0:T(8,128)(2,1)}) fusion(f32[288,384]{1,0:T(8,128)S(1)} %broadcast_in_dim.16, f32[32,768]{1,0:T(8,128)S(1)} %get-tuple-element.25, f32[16,768]{1,0:T(8,128)S(1)} %copy-done.2, f32[216,768]{1,0:T(8,128)S(1)} %copy-done, f32[24,768]{1,0:T(8,128)S(1)} %get-tuple-element.23), kind=kLoop, calls=%fused_computation.8 | loop fusion | flops 1769472 | bytes 2211840 | tf_op jit(solution)/shard_map/convert_element_type | solution.py:106
  9.6 55.1 %shard_map.279 = (f32[3,132,512]{2,1,0:T(8,128)}, f32[3,132,512]{2,1,0:T(8,128)}, f32[360,128]{1,0:T(8,128)}) custom-call(f32[3,132,512]{2,1,0:T(8,128)} %fn_ref.1, f32[3,132,512]{2,1,0:T(8,128)} %fo_ref.1, f32[3,132,512]{2,1,0:T(8,128)} %an_ref.1, f32[3,132,512]{2,1,0:T(8,128)} %ao_ref.1, f32[360,128]{1,0:T(8,128)} %pad.5.mod_ref, ...), custom_call_target="tpu_custom_call" | custom-call | tf_op jit(solution)/shard_map/pallas_call | solution.py:656
  64.7 1.8 %reshape.21 = f32[21,17,1,100]{3,2,1,0:T(1,128)} reshape(f32[357,100]{1,0:T(8,128)} %bitcast.2) | data formatting | bytes 285600 | tf_op jit(solution)/shard_map/reshape | solution.py:681
  66.5 2.2 %copy.37 = f32[3,132,512]{2,1,0:T(8,128)} copy(f32[3,132,512]{2,1,0:T(8,128)} %get-tuple-element.29) | data formatting | bytes 1622016
  68.6 0.9 %copy.38 = f32[3,132,512]{2,1,0:T(8,128)} copy(f32[3,132,512]{2,1,0:T(8,128)S(1)} %copy-done.1) | data formatting | bytes 1622016
  (15 shorter events, 0.1 us)
Async XLA Ops:
  0.6 0.7 copy-start.13
  0.6 0.7 copy-start.12
  0.7 1.6 %copy-start.11 = (f32[16,768]{1,0:T(8,128)S(1)}, f32[16,768]{1,0:T(8,128)}, u32[]{:S(2)}) copy-start(f32[16,768]{1,0:T(8,128)} %constant.62.clone) | copy-start | bytes 147460
  0.7 1.6 %copy-start.2 = (f32[16,768]{1,0:T(8,128)S(1)}, f32[16,768]{1,0:T(8,128)}, u32[]{:S(2)}) copy-start(f32[16,768]{1,0:T(8,128)} %constant.63.clone) | copy-start | bytes 147460
  2.2 1.7 %copy-start.10 = (f32[24,768]{1,0:T(8,128)S(1)}, f32[24,768]{1,0:T(8,128)}, u32[]{:S(2)}) copy-start(f32[24,768]{1,0:T(8,128)} %constant.59.clone) | copy-start | bytes 221188
  2.3 1.6 %copy-start.8 = (f32[24,768]{1,0:T(8,128)S(1)}, f32[24,768]{1,0:T(8,128)}, u32[]{:S(2)}) copy-start(f32[24,768]{1,0:T(8,128)} %constant.67.clone) | copy-start | bytes 221188
  2.3 1.5 %copy-start.9 = (f32[24,768]{1,0:T(8,128)S(1)}, f32[24,768]{1,0:T(8,128)}, u32[]{:S(2)}) copy-start(f32[24,768]{1,0:T(8,128)} %constant.60.clone) | copy-start | bytes 221188
  2.4 1.6 %copy-start.7 = (f32[32,768]{1,0:T(8,128)S(1)}, f32[32,768]{1,0:T(8,128)}, u32[]{:S(2)}) copy-start(f32[32,768]{1,0:T(8,128)} %constant.64.clone) | copy-start | bytes 294916
  3.9 0.9 %copy-start.4 = (f32[32,768]{1,0:T(8,128)S(1)}, f32[32,768]{1,0:T(8,128)}, u32[]{:S(2)}) copy-start(f32[32,768]{1,0:T(8,128)} %constant.68.clone) | copy-start | bytes 294916
  3.9 0.9 %copy-start.5 = (f32[32,768]{1,0:T(8,128)S(1)}, f32[32,768]{1,0:T(8,128)}, u32[]{:S(2)}) copy-start(f32[32,768]{1,0:T(8,128)} %constant.66.clone) | copy-start | bytes 294916
  3.9 1.0 %copy-start.6 = (f32[32,768]{1,0:T(8,128)S(1)}, f32[32,768]{1,0:T(8,128)}, u32[]{:S(2)}) copy-start(f32[32,768]{1,0:T(8,128)} %constant.65.clone) | copy-start | bytes 294916
  4.9 0.9 %copy-start.3 = (f32[21,17,1,100]{3,2,1,0:T(1,128)S(1)}, f32[21,17,1,100]{3,2,1,0:T(1,128)}, u32[]{:S(2)}) copy-start(f32[21,17,1,100]{3,2,1,0:T(1,128)} %param.31) | copy-start | bytes 428404
  6.3 1.2 %copy-start = (f32[216,768]{1,0:T(8,128)S(1)}, f32[216,768]{1,0:T(8,128)}, u32[]{:S(2)}) copy-start(f32[216,768]{1,0:T(8,128)} %constant.61.clone) | copy-start | bytes 1990660
  66.4 2.2 %copy-start.1 = (f32[3,132,512]{2,1,0:T(8,128)S(1)}, f32[3,132,512]{2,1,0:T(8,128)}, u32[]{:S(2)}) copy-start(f32[3,132,512]{2,1,0:T(8,128)} %get-tuple-element.30) | copy-start | bytes 2433028

commit v3 on v2

--- a/solution.py
+++ b/solution.py
@@ -132,17 +132,19 @@
     return out
 
 
-def core(cfg, fn_ref, fo_ref, an_ref, ao_ref, mod_ref, rad_ref, mass_ref, fh_ref, fl_ref, ah_ref, al_ref, perm_ref,
+def core(cfg, fn_ref, fo_ref, an_ref, ao_ref, mod_ref, inner_ref, fix_ref, perm_in, rrow_ref, mrow_ref,
          a3_ref, aa_ref, wrow_ref, krow_ref, nyq_ref, f_ref, a_ref, k_ref,
          uz, es, cs, ps, accb, s_ref, s1_ref, s2_ref, t3_ref, xb, last, modr, modx, rh, stage, ring, force,
-         edge_f, rm, spill, rspill, kb, kr, lsem, ssem, rsem):
-    nf, nm, own, R, wide, count_a, nodes, nb, hrow, edge, derive = cfg
+         edge_f, rm, spill, rspill, kb, kr, ks, rad_ref, mass_ref, tab_h, tab_l, inner_v, fix_v, perm_ref,
+         pack, rpack, edge_p, rmp, x3, lsem, ssem, rsem):
+    nf, nm, own, R, wide, count_a, nodes, nb, hrow, edge, own_orders, derive = cfg
     rows, lanes = fn_ref.shape[1:]
     W = 256 * nb + 128
     blocks = 2 * nb + 1
     halo = 4 * ORD
     main = R - HR
-    tables = ((fh_ref, fl_ref), (ah_ref, al_ref))
+    tables = tuple((tab_h.at[l], tab_l.at[l]) for l in range(2))
+    orders = own_orders
     me, mi = lax.axis_index("fourier"), lax.axis_index("meridian")
     up, down = lax.rem(me + 1, nf), lax.rem(me + nf - 1, nf)
     has_prev, has_next = mi > 0, mi < nm - 1
@@ -153,25 +155,39 @@
             src_ref=src, dst_ref=dst, send_sem=ssem.at[at], recv_sem=rsem.at[at],
             device_id={"meridian": meridian, "fourier": fourier}, device_id_type=MESH)
 
-    first = pl.ds(0, HR)
+    half = nf // 2
+    odd = lax.rem(me, 2)
+    partner, mine = me + 1 - 2 * odd, me // 2
+    peers = [2 * lax.rem(mine + s + 1, half) + odd for s in range(half - 1)]
+    sources = [2 * lax.rem(mine + half - 1 - s, half) + odd for s in range(half - 1)]
+    first, top = pl.ds(0, HR), pl.ds(0, edge - 1)
     body_rows, tail_rows = pl.ds(0, main), pl.ds(main, HR)
     prev, nxt = mi - 1, mi + 1
-    to_prev = [remote(fn_ref.at[:, first], rh.at[0:3], 0, prev, me),
-               remote(an_ref.at[:, first], rh.at[3:6], 1, prev, me),
-               remote(stage.at[0, first], ring.at[0, tail_rows], 2, prev, down),
-               remote(stage.at[1, first], ring.at[1, tail_rows], 3, prev, up)]
-    to_ring = [remote(stage.at[0], ring.at[0, body_rows], 4, mi, down),
-               remote(stage.at[1], ring.at[1, body_rows], 5, mi, up)]
-    to_next = [remote(edge_f, rm, 6, nxt, me),
-               remote(spill.at[0, tail_rows], rspill.at[0, tail_rows], 7, nxt, down),
-               remote(spill.at[1, tail_rows], rspill.at[1, tail_rows], 8, nxt, up)]
-    to_spill = [remote(spill.at[0, body_rows], rspill.at[0, body_rows], 9, mi, down),
-                remote(spill.at[1, body_rows], rspill.at[1, body_rows], 10, mi, up)]
-    mod_send = [remote(mod_ref, modr.at[me], 11 + s, mi, lax.rem(me + s + 1, nf)) for s in range(nf - 1)]
-    mod_recv = [remote(mod_ref, modr.at[lax.rem(me + nf - 1 - s, nf)], 11 + s, mi, me) for s in range(nf - 1)]
-    base = 11 + nf - 1
-    k_send = [remote(kb.at[lax.rem(me + s + 1, nf)], kr.at[s], base + s, mi, lax.rem(me + s + 1, nf))
-              for s in range(nf - 1)]
+    to_prev = [remote(fn_ref.at[:, top], rh.at[0:3], 0, prev, me),
+               remote(an_ref.at[:, top], rh.at[3:6], 1, prev, me),
+               remote(pack, rpack, 2, prev, me),
+               remote(stage.at[0, first], ring.at[0, tail_rows], 3, prev, down),
+               remote(stage.at[1, first], ring.at[1, tail_rows], 4, prev, up)]
+    to_ring = [remote(stage.at[0], ring.at[0, body_rows], 5, mi, down),
+               remote(stage.at[1], ring.at[1, body_rows], 6, mi, up)]
+    to_next = [remote(edge_f, rm, 7, nxt, me), remote(edge_p, rmp, 8, nxt, me),
+               remote(spill.at[0, tail_rows], rspill.at[0, tail_rows], 9, nxt, down),
+               remote(spill.at[1, tail_rows], rspill.at[1, tail_rows], 10, nxt, up)]
+    to_spill = [remote(spill.at[0, body_rows], rspill.at[0, body_rows], 11, mi, down),
+                remote(spill.at[1, body_rows], rspill.at[1, body_rows], 12, mi, up)]
+    base = 13
+    mod_far = [remote(mod_ref, modr.at[me], base + s, mi, peers[s]) for s in range(half - 1)]
+    mod_got = [remote(mod_ref, modr.at[sources[s]], base + s, mi, peers[s]) for s in range(half - 1)]
+    base += half - 1
+    mod_near = remote(mod_ref, modr.at[me], base, mi, partner)
+    near_got = remote(mod_ref, modr.at[partner], base, mi, partner)
+    mod_pass = [remote(modr.at[sources[s]], modr.at[sources[s]], base + 1 + s, mi, partner) for s in range(half - 1)]
+    pass_got = [remote(modr.at[sources[s]], modr.at[sources[s] + 1 - 2 * odd], base + 1 + s, mi, partner)
+                for s in range(half - 1)]
+    base += half
+    k_near = remote(kb.at[1 - odd], kr, base, mi, partner)
+    k_far = [remote(kb.at[odd, lax.rem(mine + s + 1, half)], ks.at[s], base + 1 + s, mi, peers[s])
+             for s in range(half - 1)]
 
     barrier = pltpu.get_barrier_semaphore()
 
@@ -189,7 +205,9 @@
 
     loads = [pltpu.make_async_copy(an_ref, xb.at[3:6], lsem.at[0]), pltpu.make_async_copy(fn_ref, xb.at[0:3], lsem.at[1]),
              pltpu.make_async_copy(fo_ref, last.at[0:3], lsem.at[2]), pltpu.make_async_copy(ao_ref, last.at[3:6], lsem.at[3]),
-             pltpu.make_async_copy(mod_ref, modr.at[me], lsem.at[4])]
+             pltpu.make_async_copy(mod_ref, modr.at[me], lsem.at[4]),
+             pltpu.make_async_copy(inner_ref, inner_v, lsem.at[5]), pltpu.make_async_copy(fix_ref, fix_v, lsem.at[6]),
+             pltpu.make_async_copy(perm_in, perm_ref, lsem.at[7])]
     for copy in loads:
         copy.start()
 
@@ -205,26 +223,86 @@
         total = jnp.zeros((rows, 128), f32)
         for c in range(3):
             shift = (halo * c + (halo if way else 0)) % 128
-            turned = xb[3 + c, :, source:source + 128]
+            turned = xb[3 + c, :rows, source:source + 128]
             turned = pltpu.roll(turned, shift, 1) if shift else turned
             total = jnp.where((lane_id >= halo * c) & (lane_id < halo * (c + 1)), turned, total)
             if way == 0:
-                turned = pltpu.roll(xb[c, :, :128], 3 * halo + 2 * c - 2, 1)
+                turned = pltpu.roll(xb[c, :rows, :128], 3 * halo + 2 * c - 2, 1)
                 spot = 3 * halo + 2 * c
                 total = jnp.where((lane_id >= spot) & (lane_id < spot + 2), turned, total)
         stage[way, :rows] = total
         stage[way, rows:] = jnp.zeros((main - rows, 128), f32)
 
+    for lc in range(6):
+        pack[lc:lc + 1, :] = xb[lc, edge - 1:edge, :]
+    pack[6:, :] = jnp.zeros((2, lanes), f32)
     pl.semaphore_wait(barrier, nf - 1 + 3 * (has_prev.astype(jnp.int32) + has_next.astype(jnp.int32)))
 
     @pl.when(has_prev)
     def _():
         for copy in to_prev:
             copy.start()
-    for copy in to_ring + mod_send:
+    for copy in to_ring + mod_far + [mod_near]:
         copy.start()
 
-    s_ref[...] = onehot((lanes, 2 * own), lambda a, b: (a % 2) * own + a // 2 == b)
+    lane8 = lax.broadcasted_iota(jnp.int32, (8, 128), 1)
+    sub8 = lax.broadcasted_iota(jnp.int32, (8, 128), 0)
+
+    def column(row_ref, lowest, highest, index):
+        total = jnp.zeros((8, 128), f32)
+        for b in range(lowest // 128, highest // 128 + 1):
+            width = min(128, row_ref.shape[1] - 128 * b)
+            values = jnp.broadcast_to(row_ref[0:1, 128 * b:128 * b + width], (8, width))
+            if width < 128:
+                values = jnp.concatenate([values, jnp.zeros((8, 128 - width), f32)], axis=1)
+            total = total + jnp.where(lane8 + 128 * b == index, values, 0.0)
+        return jnp.broadcast_to(jnp.sum(total, axis=1, keepdims=True), (8, 128))
+
+    per_row = nodes // count_a
+    for ea in range(count_a):
+        for ij in range(25):
+            at = (ea * 25 + ij) * 8
+            rad_ref[at:at + 8, :] = column(rrow_ref, ea * per_row + ij, ea * per_row + ij + 25 * (EB - 1),
+                                           25 * sub8 + (ea * per_row + ij))
+    for i in range(-(-rows // 8)):
+        high = min(16 * i + 15, mrow_ref.shape[1] - 1)
+        mass_0 = column(mrow_ref, 16 * i, high, 2 * sub8 + 16 * i)
+        mass_1 = column(mrow_ref, 16 * i, high, 2 * sub8 + (16 * i + 1))
+        mass_ref[8 * i:8 * i + 8, :] = jnp.where(lane8 % 2 == 0, mass_0, mass_1)
+    loads[5].wait()
+    loads[6].wait()
+    is_first = jnp.where(me == 0, 1.0, 0.0).astype(f32)
+    sub16 = lax.broadcasted_iota(jnp.int32, (16, W), 0)
+    start_order = (me * orders).astype(f32)
+
+    def put_rows(ls, at, value, turn):
+        h, lo = split(jnp.concatenate([value[:, :W], value[:, W:] * turn], axis=1))
+        for l in ls:
+            tab_h[l, pl.ds(at, 16)] = h
+            tab_l[l, pl.ds(at, 16)] = lo
+
+    def table_step(g, carry):
+        at = pl.multiple_of(g * 16, 16)
+        put_rows((0, 1), at, inner_v[pl.ds(at, 16), :], (8 * g + sub16 // 2).astype(f32) + start_order)
+        return carry
+
+    lax.fori_loop(0, own // 16, table_step, 0)
+    for g in range(2):
+        at, turn = 16 * g, (8 * g + sub16 // 2).astype(f32) + start_order
+        put_rows((1,), at, inner_v[at:at + 16] + is_first * fix_v[at:at + 16], turn)
+        put_rows((0,), at, inner_v[at:at + 16] + is_first * fix_v[32 + at:48 + at], turn)
+        at, low = own + 16 * g, (orders if g else -ORD)
+        turn = (low + sub16 // 2).astype(f32) + start_order
+        if g:
+            turn = jnp.where(sub16 < 2, turn * (1.0 - is_last), turn)
+        put_rows((1,), at, inner_v[at:at + 16] + is_first * fix_v[80 + 16 * g:96 + 16 * g]
+                 + is_last * fix_v[112 + 16 * g:128 + 16 * g], turn)
+        put_rows((0,), at, is_last * fix_v[144 + 16 * g:160 + 16 * g], turn)
+    at = 2 * orders - 16
+    put_rows((1,), at, inner_v[at:at + 16] + is_last * fix_v[64:80],
+             (at // 2 + sub16 // 2).astype(f32) + start_order)
+
+    s_ref[...] = onehot(s_ref.shape, lambda a, b: (a % 2) * 128 + a // 2 == b)
     spot = lambda a: (a % 2) * 128 + (a // 128) * (2 * ORD) + (a % 128) // 2
     s1_ref[...] = onehot((256, 256), lambda a, b: (a % 128 < halo) & ((spot(a) == b) | (spot(a) + halo == b)))
     s2_ref[...] = onehot((256, 256), lambda a, b: (a % 128 < halo) & (spot(a) + 2 * halo == b))
@@ -234,24 +312,33 @@
         t3_ref[l, 2 * halo:3 * halo] = h[own:]
         t3_ref[l, 3 * halo:] = jnp.zeros((128 - 3 * halo, 2 * W), bf16)
 
-    def samples(x, h_ref, l_ref):
+    lane_blocks = own // 128
+    bw = lanes // lane_blocks
+
+    def apart(x):
+        out = [nn(x[:, bw * b:bw * (b + 1)], s_ref[...]).astype(bf16) for b in range(lane_blocks)]
+        return [jnp.concatenate([o[:, 128 * par:128 * (par + 1)] for o in out], axis=1) for par in range(2)]
+
+    def samples(x, h_ref, l_ref, keep):
         xh, xl = split(x)
-        dh, dl = nn(xh, s_ref[...]).astype(bf16), nn(xl, s_ref[...]).astype(bf16)
-        out = []
-        for par in range(2):
-            ph, plo = dh[:, par * own:(par + 1) * own], dl[:, par * own:(par + 1) * own]
-            out.append(nn(ph, h_ref[:own]) + nn(ph, l_ref[:own]) + nn(plo, h_ref[:own]))
-        return out
-
-    for l, (h_ref, l_ref) in enumerate(tables):
-        def ahead(c, carry, l=l, h_ref=h_ref, l_ref=l_ref):
-            lc = 3 * l + c
-            for par, out in enumerate(samples(xb[lc], h_ref, l_ref)):
-                at = pl.ds(pl.multiple_of((2 * lc + par) * R, 8), rows)
-                for b in range(2 * blocks):
-                    uz[b, at, :] = out[:, 128 * b:128 * (b + 1)]
-            return carry
-        lax.fori_loop(0, 3, ahead, 0)
+        hi, lo = apart(xh), apart(xl)
+        for n in range(2 * W // 256):
+            ln = slice(256 * n, 256 * (n + 1))
+            for par in range(2):
+                keep(par, n, nn(hi[par], h_ref[:own, ln]) + nn(hi[par], l_ref[:own, ln]) + nn(lo[par], h_ref[:own, ln]))
+
+    def ahead(l, carry):
+        def keep(par, n, out):
+            for c in range(3):
+                at = pl.ds(pl.multiple_of((2 * (3 * l + c) + par) * R, 8), main)
+                for k in range(2):
+                    uz[2 * n + k, at, :] = out[c * main:(c + 1) * main, 128 * k:128 * (k + 1)]
+        for c in range(3):
+            x3[c * main:c * main + rows, :] = xb[3 * l + c]
+        samples(x3[...], tab_h.at[l], tab_l.at[l], keep)
+        return carry
+
+    lax.fori_loop(0, 2, ahead, 0)
 
     @pl.when(has_next)
     def _():
@@ -261,15 +348,24 @@
     @pl.when(jnp.logical_not(has_next))
     def _():
         rh[...] = jnp.zeros_like(rh)
+        rpack[...] = jnp.zeros_like(rpack)
         ring[:, main:] = jnp.zeros((2, HR, 128), f32)
     for copy in to_ring:
         copy.wait_recv()
+    for copy, forward in zip(mod_got, mod_pass):
+        copy.wait_recv()
+        forward.start()
+    count = edge - 1
     for l, (h_ref, l_ref) in enumerate(tables):
-        for par, out in enumerate(samples(rh[3 * l:3 * l + 3].reshape(3 * HR, lanes), h_ref, l_ref)):
+        def keep(par, n, out, l=l):
             for c in range(3):
                 at = (2 * (3 * l + c) + par) * R + main
-                for b in range(2 * blocks):
-                    uz[b, at:at + HR, :] = out[c * HR:(c + 1) * HR, 128 * b:128 * (b + 1)]
+                for k in range(2):
+                    ln = slice(128 * k, 128 * (k + 1))
+                    uz[2 * n + k, at:at + count, :] = out[c * count:(c + 1) * count, ln]
+                    uz[2 * n + k, at + count:at + edge, :] = out[3 * count + 3 * l + c:3 * count + 3 * l + c + 1, ln]
+        x = jnp.concatenate([rh[3 * l:3 * l + 3].reshape(3 * count, lanes), rpack[...]], axis=0)
+        samples(x, h_ref, l_ref, keep)
     for c in range(3):
         low, upper = ring[1], ring[0]
         if c:
@@ -293,24 +389,31 @@
                     uz[b, at:at + R, :] += column * nyq_ref[0:1, 128 * b:128 * (b + 1)]
 
     loads[4].wait()
-    for copy in mod_recv:
+    near_got.wait_recv()
+    for copy in pass_got:
         copy.wait_recv()
+    loads[7].wait()
     modx[...] = jnp.zeros_like(modx)
     for r in range(21):
         for d in range(nf):
-            modx[r, :BASIS, 128 * d:128 * (d + 1)] = modr[d, r * BASIS:(r + 1) * BASIS, :] * wrow_ref[0:1, 128 * d:128 * (d + 1)]
-
-    def moduli_step(t, carry):
+            ln = slice(128 * d, 128 * d + modr.shape[2])
+            modx[r, :BASIS, ln] = modr[d, r * BASIS:(r + 1) * BASIS, :] * wrow_ref[0:1, ln]
+
+    row_nodes, row_lanes = nodes // count_a, nf * 128 // count_a
+    pairs_each = -(-11 // (2 * blocks))
+
+    def moduli_pair(t):
         rows_two = []
         for k in range(2):
             h, lo = split(modx[2 * t + k])
             rows_two += [h, h, lo, jnp.zeros_like(h)]
-        mt = nt(perm_ref[...], jnp.concatenate(rows_two, axis=0)).astype(bf16)
-        for k in range(2):
-            cs[pl.ds(pl.multiple_of((2 * t + k) * nodes, 8), nodes), :] = nn(mt[:, 128 * k:128 * (k + 1)], a3_ref[...])
-        return carry
-
-    lax.fori_loop(0, 11, moduli_step, 0)
+        two = jnp.concatenate(rows_two, axis=0)
+        for ea in range(count_a):
+            ln = slice(ea * row_lanes, (ea + 1) * row_lanes)
+            mt = nt(perm_ref[ea * row_nodes:(ea + 1) * row_nodes, ln], two[:, ln]).astype(bf16)
+            for k in range(2):
+                at = pl.multiple_of((2 * t + k) * nodes + ea * row_nodes, 8)
+                cs[pl.ds(at, row_nodes), :] = nn(mt[:, 128 * k:128 * (k + 1)], a3_ref[...])
 
     def point(a, j):
         p = wide * a + j
@@ -364,6 +467,8 @@
             for i in range(5):
                 for j in range(5):
                     put(2, ea, i, j, rad(i, j) * z[i][j])
+        for k in range(pairs_each):
+            moduli_pair(t * pairs_each + k)
         return carry
 
     lax.fori_loop(0, 2 * blocks, strain_step, 0)
@@ -407,21 +512,12 @@
 
     lax.fori_loop(0, nodes // 8, node_step, 0)
 
-    def project_step(r, carry):
+    each = -(-21 // (2 * blocks))
+
+    def project(r):
         ph, plo = split(ps[pl.ds(pl.multiple_of(r * nodes, 8), nodes), :])
         both = nt(aa_ref[...], ph)
         accb[r] = both[:32] + both[32:] + nt(aa_ref[:32], plo)
-        return carry
-
-    lax.fori_loop(0, 21, project_step, 0)
-    h, lo = split(accb[...].reshape(21 * 32, nodes))
-    whole = (nn(h, perm_ref[...]) + nn(lo, perm_ref[...])) * krow_ref[0:1, :]
-    for d in range(nf):
-        for r in range(21):
-            kb[d, r * BASIS:(r + 1) * BASIS, :] = whole[32 * r:32 * r + BASIS, 128 * d:128 * (d + 1)]
-        kb[d, 21 * BASIS:, :] = jnp.zeros((kb.shape[1] - 21 * BASIS, 128), f32)
-    for copy in k_send:
-        copy.start()
 
     def force_step(t, carry):
         l, blk = t // blocks, t % blocks
@@ -464,13 +560,29 @@
                     else:
                         store(c, 4 * ea + i, row, blk)
                         store(c, 4 * ea + i, row_z, blk_z)
+        for k in range(each):
+            project(t * each + k)
         return carry
 
     lax.fori_loop(0, 2 * blocks, force_step, 0)
-
-    def interleave(values):
-        h, lo = split(values)
-        return nt(h, s_ref[...]) + nt(lo, s_ref[...])
+    h, lo = split(accb[:21].reshape(21 * 32, nodes))
+    for ea in range(count_a):
+        q, ln = slice(ea * row_nodes, (ea + 1) * row_nodes), slice(ea * row_lanes, (ea + 1) * row_lanes)
+        part = (nn(h[:, q], perm_ref[q, ln]) + nn(lo[:, q], perm_ref[q, ln])) * krow_ref[0:1, ln]
+        for k in range(nf // count_a):
+            for r in range(21):
+                d = ea * (nf // count_a) + k
+                kb[d % 2, d // 2, r * BASIS:(r + 1) * BASIS, :] = \
+                    part[32 * r:32 * r + BASIS, 128 * k:128 * k + kb.shape[3]]
+    k_near.start()
+
+    def interleave(both):
+        out = []
+        for b in range(lane_blocks):
+            ln = slice(128 * b, 128 * (b + 1))
+            h, lo = split(jnp.concatenate([both[0][:, ln], both[1][:, ln]], axis=1))
+            out.append(nt(h, s_ref[...]) + nt(lo, s_ref[...]))
+        return jnp.concatenate(out, axis=1)
 
     def turn_back(parts, l, with_edge):
         h_ref, l_ref = tables[1 - l]
@@ -481,7 +593,7 @@
             if with_edge:
                 edge_h.append(nt(h, t3_ref[1 - l]))
                 edge_l.append(nt(lo, t3_ref[1 - l]))
-        out = interleave(jnp.concatenate(both, axis=1))
+        out = interleave(both)
         if not with_edge:
             return out, None
         h, lo = split(jnp.concatenate(edge_h, axis=1))
@@ -514,16 +626,25 @@
     for l in range(2):
         parts = [jnp.concatenate([read(3 * l + c, par, main, HR) for c in range(3)], axis=0) for par in range(2)]
         out, side = turn_back(parts, l, l == 0)
-        edge_f[3 * l:3 * l + 3] = out.reshape(3, HR, lanes)
+        for c in range(3):
+            edge_f[3 * l + c] = out[c * HR:c * HR + count]
+            edge_p[3 * l + c:3 * l + c + 1, :] = out[c * HR + count:c * HR + edge]
         if l == 0:
             for c in range(3):
                 for way, value in enumerate(spread(side[c * HR:(c + 1) * HR], c)):
                     spill[way, main:] += value
 
+    edge_p[6:, :] = jnp.zeros((2, lanes), f32)
+
     @pl.when(has_next)
     def _():
         for copy in to_next:
             copy.start()
+    k_near.wait_recv()
+    k_near.wait_send()
+    kb[odd] += kr[...]
+    for copy in k_far:
+        copy.start()
     for c in range(3):
         out, side = turn_back([read(c, par, 0, main) for par in range(2)], 0, True)
         force[c] = out[:rows]
@@ -531,9 +652,15 @@
             spill[way, :main] += value
     for copy in to_spill:
         copy.start()
-    for c in range(3):
-        out, _ = turn_back([read(3 + c, par, 0, main) for par in range(2)], 1, False)
+
+    def adjoint_back(c, carry):
+        at = [pl.ds(pl.multiple_of((2 * (3 + c) + par) * R, 8), main) for par in range(2)]
+        parts = [jnp.concatenate([uz[b, a, :] for b in range(2 * blocks)], axis=1) for a in at]
+        out, _ = turn_back(parts, 1, False)
         force[3 + c] = out[:rows]
+        return carry
+
+    lax.fori_loop(0, 3, adjoint_back, 0)
 
     lane_m = lax.broadcasted_iota(jnp.int32, (rows, 128), 1)
 
@@ -551,24 +678,26 @@
     def _():
         for copy in to_next:
             copy.wait_recv()
-        force[:, :edge] += rm[:, :edge]
+        force[:, :edge - 1] += rm[...]
+        for lc in range(6):
+            force[lc, edge - 1:edge, :] += rmp[lc:lc + 1, :]
         gather(main, edge)
     for copy in to_spill:
         copy.wait_recv()
     gather(0, rows)
     loads[2].wait()
     loads[3].wait()
-    is_even = lax.broadcasted_iota(jnp.int32, (rows, lanes), 1) % 2 == 0
-    mass = jnp.where(is_even, mass_ref[:, 0:1], mass_ref[:, 1:2])
+    mass = jnp.concatenate([mass_ref[:rows]] * (lanes // 128), axis=1)
     for c in range(3):
-        f_ref[c] = 2.0 * xb[c] - last[c] - mass * force[c]
-        a_ref[c] = 2.0 * xb[3 + c] - last[3 + c] - mass * force[3 + c]
-    for copy in k_send:
+        f_ref[c] = 2.0 * xb[c, :rows] - last[c] - mass * force[c]
+        a_ref[c] = 2.0 * xb[3 + c, :rows] - last[3 + c] - mass * force[3 + c]
+    for copy in k_far:
         copy.wait_recv()
-    total = kb[me]
-    for s in range(nf - 1):
-        total = total + kr[s]
-    k_ref[...] = total
+    total = kb[odd, mine]
+    for s in range(half - 1):
+        total = total + ks[s]
+    for r in range(21):
+        k_ref[r, :, 0, :] = total[r * BASIS:(r + 1) * BASIS]
 
     @pl.when(has_prev)
     def _():
@@ -579,7 +708,7 @@
     def _():
         for copy in to_next:
             copy.wait_send()
-    for copy in to_ring + to_spill + mod_send + k_send:
+    for copy in to_ring + to_spill + mod_far + [mod_near] + mod_pass + k_far:
         copy.wait_send()
 
 
@@ -605,28 +734,12 @@
     W = 256 * nb + 128
     halo = 4 * ORD
 
-    flat = jnp.pad(moduli[:, :, 0, :].reshape(21 * BASIS, nodes_mine),
-                   ((0, -(21 * BASIS) % 8), (0, 128 - nodes_mine)))
+    flat = moduli.reshape(21 * BASIS, nodes_mine)
 
     inner, first, last, halo_last = block_tables(orders, own)
-    is_first = jnp.where(me == 0, 1.0, 0.0).astype(f32)
-    is_last = jnp.where(me == nf - 1, 1.0, 0.0).astype(f32)
-    head, tail = 24, slice(local - 2 * ORD, local)
-    row = np.arange(own + halo)
-    at_order = np.where(row < own, row // 2, np.where(row < own + 2 * ORD, (row - own) // 2 - ORD,
-                                                      orders + (row - own - 2 * ORD) // 2))
-    nyquist = (row // 2) == (own + 2 * ORD) // 2
-    turn = jnp.asarray(at_order, f32) + (me * orders).astype(f32)
-    turn = turn * (1.0 - jnp.asarray(nyquist, f32) * is_last)
-    scale = jnp.concatenate([jnp.ones((own + halo, W), f32), jnp.broadcast_to(turn[:, None], (own + halo, W))], axis=1)
-    fix_turned = with_turned(np.where(np.arange(head)[:, None] == 1, -inner[:head, :W], 0.0).astype(np.float32))
-    parts_a = [inner[:head] + is_first * first[:head], inner[head:local - 2 * ORD] * jnp.ones((1, 1), f32),
-               inner[tail] + is_last * last[tail], jnp.asarray(inner[local:own]),
-               inner[own:] + is_first * first[own:] + is_last * last[own:]]
-    parts_f = [inner[:head] + is_first * fix_turned, parts_a[1], jnp.asarray(inner[tail]), parts_a[3],
-               is_last * halo_last[own:]]
-    fh, fl = split_device(jnp.concatenate(parts_f, axis=0) * scale)
-    ah, al = split_device(jnp.concatenate(parts_a, axis=0) * scale)
+    drop = np.zeros_like(first[:32])
+    drop[:] = with_turned(np.where(np.arange(32)[:, None] == 1, -inner[:32, :W], 0.0))
+    fixes = np.concatenate([first[:32], drop, last[local - 16:local], first[own:], last[own:], halo_last[own:]], axis=0)
 
     rows_a = basis_rows(orders)
     bh, bl = split_host(rows_a)
@@ -643,42 +756,45 @@
                 spot = (q // nodes_mine) * 128 + q % nodes_mine
                 perm[(ea * 25 + ij) * EB + eb, spot] = 1.0
                 wrow[:, spot] = weights[ij]
-    radius = jnp.transpose(inv_radius.reshape(count_a, EB, 25), (0, 2, 1)).reshape(nodes, 1)
-    radius = jnp.broadcast_to(radius, (nodes, 128))
-
-    cfg = (nf, nm, own, R, wide, count_a, nodes, nb, start - rows, edge, derive)
+    cfg = (nf, nm, own, R, wide, count_a, nodes, nb, start - rows, edge, orders, derive)
     vmem = pl.BlockSpec(memory_space=pltpu.VMEM)
     hbm = pl.BlockSpec(memory_space=pl.ANY)
     CW = rows_a.shape[1]
-    K_ROWS = flat.shape[0]
-    copies = 11 + 2 * (nf - 1)
+    steps = 2 * (2 * nb + 1)
+    pairs, terms = -(-11 // steps) * steps, -(-21 // steps) * steps
+    copies = 13 + 2 * nf
     field = jax.ShapeDtypeStruct((comps, rows, lanes), f32)
     forward_next, adjoint_next, sums = pl.pallas_call(
         functools.partial(core, cfg),
-        out_shape=(field, field, jax.ShapeDtypeStruct((K_ROWS, 128), f32)),
-        in_specs=[hbm] * 5 + [vmem] * 12,
+        out_shape=(field, field, jax.ShapeDtypeStruct(moduli.shape, f32)),
+        in_specs=[hbm] * 8 + [vmem] * 7,
         out_specs=(vmem, vmem, vmem),
         scratch_shapes=[pltpu.VMEM((2 * W // 128, 4 * comps * R, 128), f32), pltpu.VMEM((12 * nodes, W), f32),
-                        pltpu.VMEM((22 * nodes, CW), f32), pltpu.VMEM((21 * nodes, CW), f32),
-                        pltpu.VMEM((21, 32, nodes), f32), pltpu.VMEM((lanes, 2 * own), bf16),
+                        pltpu.VMEM((2 * pairs * nodes, CW), f32), pltpu.VMEM((terms * nodes, CW), f32),
+                        pltpu.VMEM((terms, 32, nodes), f32), pltpu.VMEM((lanes * 128 // own, 256), bf16),
                         pltpu.VMEM((256, 256), bf16), pltpu.VMEM((256, 256), bf16),
                         pltpu.VMEM((2, 128, 2 * W), bf16),
                         pltpu.VMEM((2 * comps, rows, lanes), f32), pltpu.VMEM((2 * comps, rows, lanes), f32),
-                        pltpu.VMEM((nf, K_ROWS, 128), f32), pltpu.VMEM((22, 32, nf * 128), f32),
-                        pltpu.VMEM((2 * comps, HR, lanes), f32), pltpu.VMEM((2, R - HR, 128), f32),
+                        pltpu.VMEM((nf,) + flat.shape, f32), pltpu.VMEM((2 * pairs, 32, nf * 128), f32),
+                        pltpu.VMEM((2 * comps, edge - 1, lanes), f32), pltpu.VMEM((2, R - HR, 128), f32),
                         pltpu.VMEM((2, R, 128), f32), pltpu.VMEM((2 * comps, rows, lanes), f32),
-                        pltpu.VMEM((2 * comps, HR, lanes), f32), pltpu.VMEM((2 * comps, HR, lanes), f32),
+                        pltpu.VMEM((2 * comps, edge - 1, lanes), f32), pltpu.VMEM((2 * comps, edge - 1, lanes), f32),
                         pltpu.VMEM((2, R, 128), f32), pltpu.VMEM((2, R, 128), f32),
-                        pltpu.VMEM((nf, K_ROWS, 128), f32), pltpu.VMEM((nf - 1, K_ROWS, 128), f32),
-                        pltpu.SemaphoreType.DMA((5,)), pltpu.SemaphoreType.DMA((copies,)),
+                        pltpu.VMEM((2, nf // 2) + flat.shape, f32), pltpu.VMEM((nf // 2,) + flat.shape, f32),
+                        pltpu.VMEM((max(nf // 2 - 1, 1),) + flat.shape, f32),
+                        pltpu.VMEM((nodes, 128), f32), pltpu.VMEM((-(-rows // 8) * 8, 128), f32),
+                        pltpu.VMEM((2, own + halo, 2 * W), bf16), pltpu.VMEM((2, own + halo, 2 * W), bf16),
+                        pltpu.VMEM(inner.shape, f32), pltpu.VMEM(fixes.shape, f32), pltpu.VMEM(perm.shape, bf16),
+                        pltpu.VMEM((8, lanes), f32), pltpu.VMEM((8, lanes), f32),
+                        pltpu.VMEM((8, lanes), f32), pltpu.VMEM((8, lanes), f32), pltpu.VMEM((comps * start, lanes), f32),
+                        pltpu.SemaphoreType.DMA((8,)), pltpu.SemaphoreType.DMA((copies,)),
                         pltpu.SemaphoreType.DMA((copies,))],
         compiler_params=pltpu.CompilerParams(vmem_limit_bytes=60 * 1024 * 1024, collective_id=0,
                                              has_side_effects=True),
-    )(forward_now, forward_last, adjoint_now, adjoint_last, flat, radius, inv_mass.reshape(rows, 2), fh, fl, ah, al,
-      jnp.asarray(perm.astype(bf16)), jnp.asarray(a3), jnp.asarray(aa), jnp.asarray(wrow * (2.0 / n)),
+    )(forward_now, forward_last, adjoint_now, adjoint_last, flat, jnp.asarray(inner), jnp.asarray(fixes),
+      jnp.asarray(perm.astype(bf16)), inv_radius.reshape(1, nodes), inv_mass.reshape(1, 2 * rows), jnp.asarray(a3), jnp.asarray(aa), jnp.asarray(wrow * (2.0 / n)),
       jnp.asarray(wrow * (kernel_weight * 2.0 * total / n)),
       jnp.asarray(np.broadcast_to(0.5 * waves(orders)[0][orders + ORD], (8, W)).astype(np.float32)))
-    sums = sums[:21 * BASIS, :nodes_mine].reshape(21, BASIS, 1, nodes_mine)
     return forward_next, adjoint_next, sums
 
 

time: 70.6 us -> 56.3 us (0.80); the launches traced: 69.5 us -> 56 us
  Pallas kernels: 55.1 us -> 48.1 us
  local copies, waits for them, and re-layouts: 11 us -> 5.87 us
  other arithmetic: 2.64 us -> 1.38 us
    pallas_call x1, Pallas kernels: 55.1 us -> 48.1 us  [body(): pl.pallas_call(functools.partial(core, cfg), out_shape=(field, field, jax...]
    convert_element_type x2 -> x0, other arithmetic: 2.12 us -> none  [split_device(): return (hi.astype(bf16), (values - hi).astype(bf16))]
    reshape x3 -> x2, local copies, waits for them, and re-layouts: 4.03 us -> 1.94 us  [the longest x1 1.25 us: body(): inv_mass.reshape(1, 2 * rows)]
    unnamed x30 -> x7, local copies, waits for them, and re-layouts: 5.13 us -> 3.94 us
    broadcast_in_dim x3 -> x0, local copies, waits for them, and re-layouts: 1 us -> none  [the longest x2 0.9 us: body(): radius = jnp.broadcast_to(radius, (nodes, 128))]
    unnamed x1, other arithmetic: 0.46 us -> 1.38 us
where the time goes in v3:
time: 56.3 us; the launch traced here: 56 us
  Pallas kernels  48.1 us (85%)
  local copies, waits for them, and re-layouts  5.87 us (10%)
  other arithmetic  1.38 us (2%)
  between operations  0.65 us (1%)
    pallas_call x1, Pallas kernels, body(): pl.pallas_call(functools.partial(core, cfg), out_shape=(field, field, jax...  48.1 us
    unnamed x7, local copies, waits for them, and re-layouts  3.94 us
    unnamed x1, other arithmetic  1.38 us
    reshape x1, local copies, waits for them, and re-layouts, body(): inv_mass.reshape(1, 2 * rows)  1.25 us

profile of v3, /device:TPU:0, one launch (start us, length us, event | category | flops | bytes accessed | tf_op | source)
XLA Modules:
  0.0 56.0 jit_solution(15762858070430591640)
XLA Ops:
  0.6 1.2 %reshape.17.mrow_ref = f32[1,264]{1,0:T(1,128)} reshape(f32[264]{0:T(512)} %param.21) | data formatting | bytes 2112 | tf_op jit(solution)/shard_map/reshape | solution.py:795
  1.9 1.4 %reduce = f32[21,17,100]{2,1,0:T(8,128)S(1)} reduce(f32[21,17,1,100]{3,2,1,0:T(1,128)} %param.19, f32[]{:T(128)} %constant.29), dimensions={2}, to_apply=%param.19.reduce_sub_computation | reduce | bytes 285604 | tf_op args[4]
  3.3 0.7 %reshape.15.mod_ref = f32[357,100]{1,0:T(8,128)} reshape(f32[21,17,100]{2,1,0:T(8,128)S(1)} %reduce) | data formatting | bytes 285600 | tf_op jit(solution)/shard_map/reshape | solution.py:737
  4.0 48.1 %shard_map.166 = (f32[3,132,512]{2,1,0:T(8,128)}, f32[3,132,512]{2,1,0:T(8,128)}, f32[21,17,1,100]{3,2,1,0:T(1,128)}) custom-call(f32[3,132,512]{2,1,0:T(8,128)} %fn_ref.1, f32[3,132,512]{2,1,0:T(8,128)} %fo_ref.1, f32[3,132,512]{2,1,0:T(8,128)} %an_ref.1, f32[3,132,512]{2,1,0:T(8,128)} %ao_ref.1, f32[357,100]{1,0:T(8,128)} %reshape.15.mod_ref, ...), custom_call_target="tpu_custom_call" | custom-call | tf_op jit(solution)/shard_map/pallas_call | solution.py:767
  52.1 0.0 copy-start
  52.1 2.2 %copy.22 = f32[3,132,512]{2,1,0:T(8,128)} copy(f32[3,132,512]{2,1,0:T(8,128)} %get-tuple-element.6) | data formatting | bytes 1622016
  54.3 0.0 copy-done
  54.3 0.0 copy-start.1
  54.3 0.9 %copy.23 = f32[3,132,512]{2,1,0:T(8,128)} copy(f32[3,132,512]{2,1,0:T(8,128)S(1)} %copy-done) | data formatting | bytes 1622016
  55.2 0.2 copy-done.1
  55.3 0.7 %copy.24 = f32[21,17,1,100]{3,2,1,0:T(1,128)} copy(f32[21,17,1,100]{3,2,1,0:T(1,128)S(1)} %copy-done.1) | data formatting | bytes 285600
Async XLA Ops:
  52.1 2.2 %copy-start = (f32[3,132,512]{2,1,0:T(8,128)S(1)}, f32[3,132,512]{2,1,0:T(8,128)}, u32[]{:S(2)}) copy-start(f32[3,132,512]{2,1,0:T(8,128)} %get-tuple-element.7) | copy-start | bytes 2433028
  54.3 1.1 %copy-start.1 = (f32[21,17,1,100]{3,2,1,0:T(1,128)S(1)}, f32[21,17,1,100]{3,2,1,0:T(1,128)}, u32[]{:S(2)}) copy-start(f32[21,17,1,100]{3,2,1,0:T(1,128)} %get-tuple-element.8) | copy-start | bytes 428404

commit v4 on v3

--- a/solution.py
+++ b/solution.py
@@ -132,9 +132,9 @@
     return out
 
 
-def core(cfg, fn_ref, fo_ref, an_ref, ao_ref, mod_ref, inner_ref, fix_ref, perm_in, rrow_ref, mrow_ref,
+def core(cfg, fn_ref, an_ref, mod_ref, inner_ref, fix_ref, perm_in, rrow_ref, mrow_ref,
          a3_ref, aa_ref, wrow_ref, krow_ref, nyq_ref, f_ref, a_ref, k_ref,
-         uz, es, cs, ps, accb, s_ref, s1_ref, s2_ref, t3_ref, xb, last, modr, modx, rh, stage, ring, force,
+         uz, es, cs, ps, accb, s_ref, s1_ref, s2_ref, t3_ref, xb, modr, modx, rh, stage, ring, force,
          edge_f, rm, spill, rspill, kb, kr, ks, rad_ref, mass_ref, tab_h, tab_l, inner_v, fix_v, perm_ref,
          pack, rpack, edge_p, rmp, x3, lsem, ssem, rsem):
     nf, nm, own, R, wide, count_a, nodes, nb, hrow, edge, own_orders, derive = cfg
@@ -204,10 +204,9 @@
                 greet(other, f)
 
     loads = [pltpu.make_async_copy(an_ref, xb.at[3:6], lsem.at[0]), pltpu.make_async_copy(fn_ref, xb.at[0:3], lsem.at[1]),
-             pltpu.make_async_copy(fo_ref, last.at[0:3], lsem.at[2]), pltpu.make_async_copy(ao_ref, last.at[3:6], lsem.at[3]),
-             pltpu.make_async_copy(mod_ref, modr.at[me], lsem.at[4]),
-             pltpu.make_async_copy(inner_ref, inner_v, lsem.at[5]), pltpu.make_async_copy(fix_ref, fix_v, lsem.at[6]),
-             pltpu.make_async_copy(perm_in, perm_ref, lsem.at[7])]
+             pltpu.make_async_copy(mod_ref, modr.at[me], lsem.at[2]),
+             pltpu.make_async_copy(inner_ref, inner_v, lsem.at[3]), pltpu.make_async_copy(fix_ref, fix_v, lsem.at[4]),
+             pltpu.make_async_copy(perm_in, perm_ref, lsem.at[5])]
     for copy in loads:
         copy.start()
 
@@ -269,8 +268,8 @@
         mass_0 = column(mrow_ref, 16 * i, high, 2 * sub8 + 16 * i)
         mass_1 = column(mrow_ref, 16 * i, high, 2 * sub8 + (16 * i + 1))
         mass_ref[8 * i:8 * i + 8, :] = jnp.where(lane8 % 2 == 0, mass_0, mass_1)
-    loads[5].wait()
-    loads[6].wait()
+    loads[3].wait()
+    loads[4].wait()
     is_first = jnp.where(me == 0, 1.0, 0.0).astype(f32)
     sub16 = lax.broadcasted_iota(jnp.int32, (16, W), 0)
     start_order = (me * orders).astype(f32)
@@ -366,17 +365,19 @@
                     uz[2 * n + k, at + count:at + edge, :] = out[3 * count + 3 * l + c:3 * count + 3 * l + c + 1, ln]
         x = jnp.concatenate([rh[3 * l:3 * l + 3].reshape(3 * count, lanes), rpack[...]], axis=0)
         samples(x, h_ref, l_ref, keep)
+    near = []
     for c in range(3):
         low, upper = ring[1], ring[0]
         if c:
             low, upper = pltpu.roll(low, 128 - halo * c, 1), pltpu.roll(upper, 128 - halo * c, 1)
         hh, hl = split(jnp.concatenate([low, upper], axis=1))
         he = (nn(hh, s1_ref[...]) + nn(hl, s2_ref[...])).astype(bf16)
-        for par in range(2):
-            at = (2 * (3 + c) + par) * R
-            out = nn(he[:, par * 128:(par + 1) * 128], t3_ref[1])
-            for b in range(2 * blocks):
-                uz[b, at:at + R, :] += out[:, 128 * b:128 * (b + 1)]
+        near += [he[:, :128], he[:, 128:]]
+    near = jnp.concatenate(near, axis=0)
+    for n in range(2 * W // 256):
+        out = nn(near, t3_ref[1, :, 256 * n:256 * (n + 1)])
+        for k in range(2):
+            uz[2 * n + k, 6 * R:12 * R, :] += out[:, 128 * k:128 * (k + 1)]
 
     @pl.when(me == nf - 1)
     def _():
@@ -388,32 +389,38 @@
                 for b in range(blocks):
                     uz[b, at:at + R, :] += column * nyq_ref[0:1, 128 * b:128 * (b + 1)]
 
-    loads[4].wait()
+    loads[2].wait()
     near_got.wait_recv()
     for copy in pass_got:
         copy.wait_recv()
-    loads[7].wait()
+    loads[5].wait()
     modx[...] = jnp.zeros_like(modx)
     for r in range(21):
         for d in range(nf):
-            ln = slice(128 * d, 128 * d + modr.shape[2])
-            modx[r, :BASIS, ln] = modr[d, r * BASIS:(r + 1) * BASIS, :] * wrow_ref[0:1, ln]
+            ln = slice(128 * d, 128 * d + modr.shape[4])
+            modx[r, :BASIS, ln] = modr[d, r, :, 0, :] * wrow_ref[0:1, ln]
 
     row_nodes, row_lanes = nodes // count_a, nf * 128 // count_a
     pairs_each = -(-11 // (2 * blocks))
 
-    def moduli_pair(t):
-        rows_two = []
-        for k in range(2):
-            h, lo = split(modx[2 * t + k])
-            rows_two += [h, h, lo, jnp.zeros_like(h)]
-        two = jnp.concatenate(rows_two, axis=0)
+    def moduli_pairs(ts):
+        spread_out = []
+        for t in ts:
+            rows_two = []
+            for k in range(2):
+                h, lo = split(modx[2 * t + k])
+                rows_two += [h, h, lo, jnp.zeros_like(h)]
+            spread_out.append(jnp.concatenate(rows_two, axis=0))
+        turned = []
         for ea in range(count_a):
             ln = slice(ea * row_lanes, (ea + 1) * row_lanes)
-            mt = nt(perm_ref[ea * row_nodes:(ea + 1) * row_nodes, ln], two[:, ln]).astype(bf16)
-            for k in range(2):
-                at = pl.multiple_of((2 * t + k) * nodes + ea * row_nodes, 8)
-                cs[pl.ds(at, row_nodes), :] = nn(mt[:, 128 * k:128 * (k + 1)], a3_ref[...])
+            for t, two in zip(ts, spread_out):
+                mt = nt(perm_ref[ea * row_nodes:(ea + 1) * row_nodes, ln], two[:, ln]).astype(bf16)
+                turned += [(t, k, ea, mt[:, 128 * k:128 * (k + 1)]) for k in range(2)]
+        out = nn(jnp.concatenate([mt for _, _, _, mt in turned], axis=0), a3_ref[...])
+        for i, (t, k, ea, _) in enumerate(turned):
+            at = pl.multiple_of((2 * t + k) * nodes + ea * row_nodes, 8)
+            cs[pl.ds(at, row_nodes), :] = out[i * row_nodes:(i + 1) * row_nodes]
 
     def point(a, j):
         p = wide * a + j
@@ -421,7 +428,6 @@
 
     def strain_step(t, carry):
         l, blk = t // blocks, t % blocks
-        lane = pl.multiple_of(blk * 128, 128)
         blk_z = blocks + blk
 
         def grid(c, ea, at_blk):
@@ -436,8 +442,8 @@
             return out
 
         def put(v, ea, i, j, value):
-            row = pl.multiple_of((6 * l + v) * nodes + ((ea * 5 + i) * 5 + j) * 8, 8)
-            es[pl.ds(row, 8), pl.ds(lane, 128)] = value
+            row = v * nodes + ((ea * 5 + i) * 5 + j) * 8
+            es[l, blk, row:row + 8, :] = value
 
         for ea in range(count_a):
             rad = lambda i, j: rad_ref[((ea * 5 + i) * 5 + j) * 8:((ea * 5 + i) * 5 + j) * 8 + 8, :]
@@ -467,8 +473,7 @@
             for i in range(5):
                 for j in range(5):
                     put(2, ea, i, j, rad(i, j) * z[i][j])
-        for k in range(pairs_each):
-            moduli_pair(t * pairs_each + k)
+        moduli_pairs([t * pairs_each + k for k in range(pairs_each)])
         return carry
 
     lax.fori_loop(0, 2 * blocks, strain_step, 0)
@@ -481,8 +486,8 @@
             sums[v] = term if sums[v] is None else sums[v] + term
 
         def one(ce, els):
-            fw = [[es[at(v), el] for v in range(6)] for el in els]
-            ad = [[es[at(6 + v), el] for v in range(6)] for el in els]
+            fw = [[es[0, el, at(v), :] for v in range(6)] for el in els]
+            ad = [[es[1, el, at(v), :] for v in range(6)] for el in els]
             sf = [[None] * 6 for _ in els]
             sa = [[None] * 6 for _ in els]
             for r, (v, w) in enumerate(PAIRS):
@@ -501,16 +506,16 @@
                 ps[at(r), ce] = total
             for el, tf, ta in zip(els, sf, sa):
                 for v in range(6):
-                    es[at(v), el] = tf[v]
-                    es[at(6 + v), el] = ta[v]
+                    es[0, el, at(v), :] = tf[v]
+                    es[1, el, at(v), :] = ta[v]
 
         for b in range(nb):
             one(slice(128 * b, 128 * b + 128),
-                [slice(128 * b, 128 * b + 128), slice(128 * (nb + b), 128 * (nb + b) + 128)])
-        one(slice(128 * nb, 128 * nb + 128), [slice(256 * nb, 256 * nb + 128)])
+                [b, nb + b])
+        one(slice(128 * nb, 128 * nb + 128), [2 * nb])
         return carry
 
-    lax.fori_loop(0, nodes // 8, node_step, 0)
+    lax.fori_loop(0, nodes // 8, node_step, 0, unroll=2)
 
     each = -(-21 // (2 * blocks))
 
@@ -521,13 +526,12 @@
 
     def force_step(t, carry):
         l, blk = t // blocks, t % blocks
-        lane = pl.multiple_of(blk * 128, 128)
         blk_z = blocks + blk
         top = lax.broadcasted_iota(jnp.int32, (8, 128), 0) == 0
 
         def get(v, ea, i, j):
-            row = pl.multiple_of((6 * l + v) * nodes + ((ea * 5 + i) * 5 + j) * 8, 8)
-            return es[pl.ds(row, 8), pl.ds(lane, 128)]
+            row = v * nodes + ((ea * 5 + i) * 5 + j) * 8
+            return es[l, blk, row:row + 8, :]
 
         def store(c, a, row, at_blk):
             def where(j):
@@ -685,12 +689,10 @@
     for copy in to_spill:
         copy.wait_recv()
     gather(0, rows)
-    loads[2].wait()
-    loads[3].wait()
     mass = jnp.concatenate([mass_ref[:rows]] * (lanes // 128), axis=1)
     for c in range(3):
-        f_ref[c] = 2.0 * xb[c, :rows] - last[c] - mass * force[c]
-        a_ref[c] = 2.0 * xb[3 + c, :rows] - last[3 + c] - mass * force[3 + c]
+        f_ref[c] = mass * force[c]
+        a_ref[c] = mass * force[3 + c]
     for copy in k_far:
         copy.wait_recv()
     total = kb[odd, mine]
@@ -734,7 +736,7 @@
     W = 256 * nb + 128
     halo = 4 * ORD
 
-    flat = moduli.reshape(21 * BASIS, nodes_mine)
+    flat = jax.ShapeDtypeStruct((21 * BASIS, nodes_mine), f32)
 
     inner, first, last, halo_last = block_tables(orders, own)
     drop = np.zeros_like(first[:32])
@@ -764,18 +766,18 @@
     pairs, terms = -(-11 // steps) * steps, -(-21 // steps) * steps
     copies = 13 + 2 * nf
     field = jax.ShapeDtypeStruct((comps, rows, lanes), f32)
-    forward_next, adjoint_next, sums = pl.pallas_call(
+    force_f, force_a, sums = pl.pallas_call(
         functools.partial(core, cfg),
         out_shape=(field, field, jax.ShapeDtypeStruct(moduli.shape, f32)),
-        in_specs=[hbm] * 8 + [vmem] * 7,
+        in_specs=[hbm] * 6 + [vmem] * 7,
         out_specs=(vmem, vmem, vmem),
-        scratch_shapes=[pltpu.VMEM((2 * W // 128, 4 * comps * R, 128), f32), pltpu.VMEM((12 * nodes, W), f32),
+        scratch_shapes=[pltpu.VMEM((2 * W // 128, 4 * comps * R, 128), f32), pltpu.VMEM((2, W // 128, 6 * nodes, 128), f32),
                         pltpu.VMEM((2 * pairs * nodes, CW), f32), pltpu.VMEM((terms * nodes, CW), f32),
                         pltpu.VMEM((terms, 32, nodes), f32), pltpu.VMEM((lanes * 128 // own, 256), bf16),
                         pltpu.VMEM((256, 256), bf16), pltpu.VMEM((256, 256), bf16),
                         pltpu.VMEM((2, 128, 2 * W), bf16),
-                        pltpu.VMEM((2 * comps, rows, lanes), f32), pltpu.VMEM((2 * comps, rows, lanes), f32),
-                        pltpu.VMEM((nf,) + flat.shape, f32), pltpu.VMEM((2 * pairs, 32, nf * 128), f32),
+                        pltpu.VMEM((2 * comps, rows, lanes), f32),
+                        pltpu.VMEM((nf,) + moduli.shape, f32), pltpu.VMEM((2 * pairs, 32, nf * 128), f32),
                         pltpu.VMEM((2 * comps, edge - 1, lanes), f32), pltpu.VMEM((2, R - HR, 128), f32),
                         pltpu.VMEM((2, R, 128), f32), pltpu.VMEM((2 * comps, rows, lanes), f32),
                         pltpu.VMEM((2 * comps, edge - 1, lanes), f32), pltpu.VMEM((2 * comps, edge - 1, lanes), f32),
@@ -787,15 +789,15 @@
                         pltpu.VMEM(inner.shape, f32), pltpu.VMEM(fixes.shape, f32), pltpu.VMEM(perm.shape, bf16),
                         pltpu.VMEM((8, lanes), f32), pltpu.VMEM((8, lanes), f32),
                         pltpu.VMEM((8, lanes), f32), pltpu.VMEM((8, lanes), f32), pltpu.VMEM((comps * start, lanes), f32),
-                        pltpu.SemaphoreType.DMA((8,)), pltpu.SemaphoreType.DMA((copies,)),
+                        pltpu.SemaphoreType.DMA((6,)), pltpu.SemaphoreType.DMA((copies,)),
                         pltpu.SemaphoreType.DMA((copies,))],
         compiler_params=pltpu.CompilerParams(vmem_limit_bytes=60 * 1024 * 1024, collective_id=0,
                                              has_side_effects=True),
-    )(forward_now, forward_last, adjoint_now, adjoint_last, flat, jnp.asarray(inner), jnp.asarray(fixes),
+    )(forward_now, adjoint_now, moduli, jnp.asarray(inner), jnp.asarray(fixes),
       jnp.asarray(perm.astype(bf16)), inv_radius.reshape(1, nodes), inv_mass.reshape(1, 2 * rows), jnp.asarray(a3), jnp.asarray(aa), jnp.asarray(wrow * (2.0 / n)),
       jnp.asarray(wrow * (kernel_weight * 2.0 * total / n)),
       jnp.asarray(np.broadcast_to(0.5 * waves(orders)[0][orders + ORD], (8, W)).astype(np.float32)))
-    return forward_next, adjoint_next, sums
+    return 2.0 * forward_now - forward_last - force_f, 2.0 * adjoint_now - adjoint_last - force_a, sums
 
 
 def solution(mesh):

time: 56.3 us -> 47.9 us (0.85)
  Pallas kernels: 48.1 us -> 41.9 us
  local copies, waits for them, and re-layouts: 5.87 us -> 1.94 us
  other arithmetic: 1.38 us -> 3.21 us
    pallas_call x1, Pallas kernels: 48.1 us -> 41.9 us  [body(): pl.pallas_call(functools.partial(core, cfg), out_shape=(field, field, jax...]
    unnamed x7 -> x11, local copies, waits for them, and re-layouts: 3.94 us -> 0.69 us
    sub x0 -> x1, other arithmetic: none -> 3.21 us  [body(): 2.0 * adjoint_now - adjoint_last - force_a]
    unnamed x1 -> x0, other arithmetic: 1.38 us -> none
    reshape x1 -> x0, local copies, waits for them, and re-layouts: 0.69 us -> none  [body(): flat = moduli.reshape(21 * BASIS, nodes_mine)]
where the time goes in v4:
time: 47.9 us; the launch traced here: 47.7 us
  Pallas kernels  41.9 us (87%)
  other arithmetic  3.21 us (7%)
  local copies, waits for them, and re-layouts  1.94 us (4%)
  between operations  0.68 us (1%)
    pallas_call x1, Pallas kernels, body(): pl.pallas_call(functools.partial(core, cfg), out_shape=(field, field, jax...  41.9 us
    sub x1, other arithmetic, body(): 2.0 * adjoint_now - adjoint_last - force_a  3.21 us
    reshape x1, local copies, waits for them, and re-layouts, body(): inv_mass.reshape(1, 2 * rows)  1.25 us

profile of v4, /device:TPU:0, one launch (start us, length us, event | category | flops | bytes accessed | tf_op | source)
XLA Modules:
  0.0 47.7 jit_solution(12310438649415344398)
XLA Ops:
  0.6 1.2 %reshape.13.mrow_ref = f32[1,264]{1,0:T(1,128)} reshape(f32[264]{0:T(512)} %param.21) | data formatting | bytes 2112 | tf_op jit(solution)/shard_map/reshape | solution.py:797
  1.9 0.0 copy-start
  1.9 0.0 copy-start.1
  1.9 0.0 copy-start.2
  1.9 0.0 copy-start.3
  1.9 41.9 %shard_map.166 = (f32[3,132,512]{2,1,0:T(8,128)}, f32[3,132,512]{2,1,0:T(8,128)}, f32[21,17,1,100]{3,2,1,0:T(1,128)}) custom-call(f32[3,132,512]{2,1,0:T(8,128)} %fn_ref.1, f32[3,132,512]{2,1,0:T(8,128)} %an_ref.1, f32[21,17,1,100]{3,2,1,0:T(1,128)} %mod_ref.1, f32[288,768]{1,0:T(8,128)} %constant.18.clone.inner_ref, f32[176,768]{1,0:T(8,128)} %constant.19.clone.fix_ref, ...), custom_call_target="tpu_custom_call" | custom-call | tf_op jit(solution)/shard_map/pallas_call | solution.py:769
  43.8 0.0 copy-done
  43.8 0.0 copy-done.1
  43.8 0.0 copy-done.2
  43.8 0.0 copy-done.3
  43.8 0.0 copy-start.4
  43.9 3.2 %subtract_subtract_fusion = (f32[3,132,512]{2,1,0:T(8,128)}, f32[3,132,512]{2,1,0:T(8,128)}) fusion(f32[3,132,512]{2,1,0:T(8,128)} %get-tuple-element.7, f32[3,132,512]{2,1,0:T(8,128)S(1)} %copy-done.2, f32[3,132,512]{2,1,0:T(8,128)S(1)} %copy-done.1, f32[3,132,512]{2,1,0:T(8,128)} %get-tuple-element.6, f32[3,132,512]{2,1,0:T(8,128)S(1)} %copy-done.3, ...), kind=kLoop, calls=%fused_computation | loop fusion | flops 1216512 | bytes 6488064 | tf_op jit(solution)/shard_map/sub | solution.py:800
  47.1 0.0 copy-done.4
  47.1 0.7 %copy.19 = f32[21,17,1,100]{3,2,1,0:T(1,128)} copy(f32[21,17,1,100]{3,2,1,0:T(1,128)S(1)} %copy-done.4) | data formatting | bytes 285600
Async XLA Ops:
  1.9 41.9 %copy-start = (f32[3,132,512]{2,1,0:T(8,128)S(1)}, f32[3,132,512]{2,1,0:T(8,128)}, u32[]{:S(2)}) copy-start(f32[3,132,512]{2,1,0:T(8,128)} %fn_ref.1) | copy-start | bytes 2433028
  1.9 41.9 %copy-start.1 = (f32[3,132,512]{2,1,0:T(8,128)S(1)}, f32[3,132,512]{2,1,0:T(8,128)}, u32[]{:S(2)}) copy-start(f32[3,132,512]{2,1,0:T(8,128)} %an_ref.1) | copy-start | bytes 2433028
  1.9 41.9 %copy-start.2 = (f32[3,132,512]{2,1,0:T(8,128)S(1)}, f32[3,132,512]{2,1,0:T(8,128)}, u32[]{:S(2)}) copy-start(f32[3,132,512]{2,1,0:T(8,128)} %param.18) | copy-start | bytes 2433028
  1.9 42.0 %copy-start.3 = (f32[3,132,512]{2,1,0:T(8,128)S(1)}, f32[3,132,512]{2,1,0:T(8,128)}, u32[]{:S(2)}) copy-start(f32[3,132,512]{2,1,0:T(8,128)} %param.16) | copy-start | bytes 2433028
  43.8 3.2 %copy-start.4 = (f32[21,17,1,100]{3,2,1,0:T(1,128)S(1)}, f32[21,17,1,100]{3,2,1,0:T(1,128)}, u32[]{:S(2)}) copy-start(f32[21,17,1,100]{3,2,1,0:T(1,128)} %get-tuple-element.16) | copy-start | bytes 428404

commit v5 on v4

--- a/solution.py
+++ b/solution.py
@@ -237,11 +237,14 @@
     pack[6:, :] = jnp.zeros((2, lanes), f32)
     pl.semaphore_wait(barrier, nf - 1 + 3 * (has_prev.astype(jnp.int32) + has_next.astype(jnp.int32)))
 
+    for copy in to_ring:
+        copy.start()
+
     @pl.when(has_prev)
     def _():
-        for copy in to_prev:
+        for copy in to_prev[::-1]:
             copy.start()
-    for copy in to_ring + mod_far + [mod_near]:
+    for copy in mod_far + [mod_near]:
         copy.start()
 
     lane8 = lax.broadcasted_iota(jnp.int32, (8, 128), 1)
@@ -341,7 +344,7 @@
 
     @pl.when(has_next)
     def _():
-        for copy in to_prev:
+        for copy in to_prev[3:]:
             copy.wait_recv()
 
     @pl.when(jnp.logical_not(has_next))
@@ -351,20 +354,6 @@
         ring[:, main:] = jnp.zeros((2, HR, 128), f32)
     for copy in to_ring:
         copy.wait_recv()
-    for copy, forward in zip(mod_got, mod_pass):
-        copy.wait_recv()
-        forward.start()
-    count = edge - 1
-    for l, (h_ref, l_ref) in enumerate(tables):
-        def keep(par, n, out, l=l):
-            for c in range(3):
-                at = (2 * (3 * l + c) + par) * R + main
-                for k in range(2):
-                    ln = slice(128 * k, 128 * (k + 1))
-                    uz[2 * n + k, at:at + count, :] = out[c * count:(c + 1) * count, ln]
-                    uz[2 * n + k, at + count:at + edge, :] = out[3 * count + 3 * l + c:3 * count + 3 * l + c + 1, ln]
-        x = jnp.concatenate([rh[3 * l:3 * l + 3].reshape(3 * count, lanes), rpack[...]], axis=0)
-        samples(x, h_ref, l_ref, keep)
     near = []
     for c in range(3):
         low, upper = ring[1], ring[0]
@@ -377,8 +366,33 @@
     for n in range(2 * W // 256):
         out = nn(near, t3_ref[1, :, 256 * n:256 * (n + 1)])
         for k in range(2):
-            uz[2 * n + k, 6 * R:12 * R, :] += out[:, 128 * k:128 * (k + 1)]
-
+            ln = slice(128 * k, 128 * (k + 1))
+            for i in range(6):
+                uz[2 * n + k, (6 + i) * R:(6 + i) * R + main, :] += out[i * R:i * R + main, ln]
+                uz[2 * n + k, (6 + i) * R + main:(7 + i) * R, :] = out[i * R + main:(i + 1) * R, ln]
+
+    for copy, forward in zip(mod_got, mod_pass):
+        copy.wait_recv()
+        forward.start()
+
+    @pl.when(has_next)
+    def _():
+        for copy in to_prev[:3]:
+            copy.wait_recv()
+    count = edge - 1
+    for l, (h_ref, l_ref) in enumerate(tables):
+        def keep(par, n, out, l=l):
+            for c in range(3):
+                at = (2 * (3 * l + c) + par) * R + main
+                for k in range(2):
+                    ln = slice(128 * k, 128 * (k + 1))
+                    some, one = out[c * count:(c + 1) * count, ln], out[3 * count + 3 * l + c:3 * count + 3 * l + c + 1, ln]
+                    if l:
+                        some, one = some + uz[2 * n + k, at:at + count, :], one + uz[2 * n + k, at + count:at + edge, :]
+                    uz[2 * n + k, at:at + count, :] = some
+                    uz[2 * n + k, at + count:at + edge, :] = one
+        x = jnp.concatenate([rh[3 * l:3 * l + 3].reshape(3 * count, lanes), rpack[...]], axis=0)
+        samples(x, h_ref, l_ref, keep)
     @pl.when(me == nf - 1)
     def _():
         for c in range(3):
@@ -590,16 +604,17 @@
 
     def turn_back(parts, l, with_edge):
         h_ref, l_ref = tables[1 - l]
-        both, edge_h, edge_l = [], [], []
-        for part in parts:
-            h, lo = split(part)
-            both.append(nt(h, h_ref[:own]) + nt(h, l_ref[:own]) + nt(lo, h_ref[:own]))
-            if with_edge:
-                edge_h.append(nt(h, t3_ref[1 - l]))
-                edge_l.append(nt(lo, t3_ref[1 - l]))
-        out = interleave(both)
         if not with_edge:
-            return out, None
+            both = []
+            for part in parts:
+                h, lo = split(part)
+                both.append(nt(h, h_ref[:own]) + nt(h, l_ref[:own]) + nt(lo, h_ref[:own]))
+            return interleave(both), None
+        count = parts[0].shape[0]
+        h, lo = split(jnp.concatenate(parts, axis=0))
+        cut = lambda v: [v[:count], v[count:]]
+        out = interleave(cut(nt(h, h_ref[:own]) + nt(h, l_ref[:own]) + nt(lo, h_ref[:own])))
+        edge_h, edge_l = cut(nt(h, t3_ref[1 - l])), cut(nt(lo, t3_ref[1 - l]))
         h, lo = split(jnp.concatenate(edge_h, axis=1))
         side = nt(h, s1_ref[...]) + nt(lo, s1_ref[...])
         h, lo = split(jnp.concatenate(edge_l, axis=1))

time: 47.9 us -> 47.9 us (level)
  no operation moved by 1% of the time
where the time goes in v5:
time: 47.9 us; the launch traced here: 47.7 us
  Pallas kernels  41.9 us (87%)
  other arithmetic  3.21 us (7%)
  local copies, waits for them, and re-layouts  1.94 us (4%)
  between operations  0.68 us (1%)
    pallas_call x1, Pallas kernels, body(): pl.pallas_call(functools.partial(core, cfg), out_shape=(field, field, jax...  41.9 us
    sub x1, other arithmetic, body(): 2.0 * adjoint_now - adjoint_last - force_a  3.21 us
    reshape x1, local copies, waits for them, and re-layouts, body(): inv_mass.reshape(1, 2 * rows)  1.25 us

profile of v5, /device:TPU:0, one launch (start us, length us, event | category | flops | bytes accessed | tf_op | source)
XLA Modules:
  0.0 47.7 jit_solution(10687723208079248087)
XLA Ops:
  0.6 1.2 %reshape.13.mrow_ref = f32[1,264]{1,0:T(1,128)} reshape(f32[264]{0:T(512)} %param.21) | data formatting | bytes 2112 | tf_op jit(solution)/shard_map/reshape | solution.py:812
  1.9 0.0 copy-start
  1.9 0.0 copy-start.1
  1.9 0.0 copy-start.2
  1.9 0.0 copy-start.3
  1.9 41.9 %shard_map.166 = (f32[3,132,512]{2,1,0:T(8,128)}, f32[3,132,512]{2,1,0:T(8,128)}, f32[21,17,1,100]{3,2,1,0:T(1,128)}) custom-call(f32[3,132,512]{2,1,0:T(8,128)} %fn_ref.1, f32[3,132,512]{2,1,0:T(8,128)} %an_ref.1, f32[21,17,1,100]{3,2,1,0:T(1,128)} %mod_ref.1, f32[288,768]{1,0:T(8,128)} %constant.18.clone.inner_ref, f32[176,768]{1,0:T(8,128)} %constant.19.clone.fix_ref, ...), custom_call_target="tpu_custom_call" | custom-call | tf_op jit(solution)/shard_map/pallas_call | solution.py:784
  43.8 0.0 copy-done
  43.8 0.0 copy-done.1
  43.8 0.0 copy-done.2
  43.8 0.0 copy-done.3
  43.8 0.0 copy-start.4
  43.9 3.2 %subtract_subtract_fusion = (f32[3,132,512]{2,1,0:T(8,128)}, f32[3,132,512]{2,1,0:T(8,128)}) fusion(f32[3,132,512]{2,1,0:T(8,128)} %get-tuple-element.7, f32[3,132,512]{2,1,0:T(8,128)S(1)} %copy-done.2, f32[3,132,512]{2,1,0:T(8,128)S(1)} %copy-done.1, f32[3,132,512]{2,1,0:T(8,128)} %get-tuple-element.6, f32[3,132,512]{2,1,0:T(8,128)S(1)} %copy-done.3, ...), kind=kLoop, calls=%fused_computation | loop fusion | flops 1216512 | bytes 6488064 | tf_op jit(solution)/shard_map/sub | solution.py:815
  47.1 0.0 copy-done.4
  47.1 0.7 %copy.19 = f32[21,17,1,100]{3,2,1,0:T(1,128)} copy(f32[21,17,1,100]{3,2,1,0:T(1,128)S(1)} %copy-done.4) | data formatting | bytes 285600
Async XLA Ops:
  1.9 41.9 %copy-start = (f32[3,132,512]{2,1,0:T(8,128)S(1)}, f32[3,132,512]{2,1,0:T(8,128)}, u32[]{:S(2)}) copy-start(f32[3,132,512]{2,1,0:T(8,128)} %fn_ref.1) | copy-start | bytes 2433028
  1.9 41.9 %copy-start.1 = (f32[3,132,512]{2,1,0:T(8,128)S(1)}, f32[3,132,512]{2,1,0:T(8,128)}, u32[]{:S(2)}) copy-start(f32[3,132,512]{2,1,0:T(8,128)} %an_ref.1) | copy-start | bytes 2433028
  1.9 41.9 %copy-start.2 = (f32[3,132,512]{2,1,0:T(8,128)S(1)}, f32[3,132,512]{2,1,0:T(8,128)}, u32[]{:S(2)}) copy-start(f32[3,132,512]{2,1,0:T(8,128)} %param.18) | copy-start | bytes 2433028
  1.9 42.0 %copy-start.3 = (f32[3,132,512]{2,1,0:T(8,128)S(1)}, f32[3,132,512]{2,1,0:T(8,128)}, u32[]{:S(2)}) copy-start(f32[3,132,512]{2,1,0:T(8,128)} %param.16) | copy-start | bytes 2433028
  43.8 3.2 %copy-start.4 = (f32[21,17,1,100]{3,2,1,0:T(1,128)S(1)}, f32[21,17,1,100]{3,2,1,0:T(1,128)}, u32[]{:S(2)}) copy-start(f32[21,17,1,100]{3,2,1,0:T(1,128)} %get-tuple-element.16) | copy-start | bytes 428404
